TPU v7x, 512 devices: a whole 4x8x8 slice. The times are simulated.
512 devices in a mesh: tm: 128 (over y, x, z_hi, core), coord: 4 (over z_lo).
Axes of the slice: x: 4, y: 8, z: 8 (z_hi: 2, z_lo: 4; z = z_hi * 4 + z_lo), core: 2. Of those that a mesh axis runs over, the one named last changes fastest.
Arguments:
- state: float32 [256, 16384], P('tm', 'coord'), may hold values from -6 to 6
- multiplier: float32 [256, 2048], P('tm', 'coord'), may hold values from -6 to 6
- force: float32 [256, 16384], P('tm', 'coord'), may hold values from -6 to 6
- initial: float32 [16384], P('coord'), may hold values from -6 to 6
- mass: float32 [16384], P('coord'), may hold values from 0.25 to 4
- stiff_diag: float32 [16384], P('coord'), may hold values from 0.9 to 1.8
- stab: float32 [2048], P('coord'), may hold values from 2.5 to 10
- bank: float32 [16, 128, 128], replicated, may hold values from -0.20412415 to 0.20412415
- k_offsets: int32 [128, 3], P('coord'), may hold values from 0 to 4, as said below
- k_tiles: int32 [128, 3], P('coord'), may hold values from 0 to 15
- g_cols: int32 [16, 4], P('coord'), may hold values from 0 to 31, as said below
- g_tiles: int32 [16, 4], P('coord'), may hold values from 0 to 15
Outputs:
- new_state: float32 [256, 16384], P('tm', 'coord')
- new_multiplier: float32 [256, 2048], P('tm', 'coord')
Inputs may be any that keep to these rules, and one draw needn't show every extreme that they name: `k_offsets`: each row holds 3 different values. `g_cols`: each row holds 4 different values.
All inputs are finite; a program needn't handle non-finite values.
Results may differ from a plain program's by a relative error of at most 0.0055.
Values sent between devices are 32-bit elements; how exact they have to be, the bound alone decides.
No kernel may reach another device: no remote copies, remote signals or barrier semaphores. Data moves between devices by JAX's collectives and lax.ppermute only.
A program may use at most 64 MiB of HBM per device.

v0:
```python
import math

import jax
import jax.numpy as jnp
import numpy as np
from jax import lax
from jax.experimental import pallas as pl
from jax.experimental.pallas import tpu as pltpu
from jax.sharding import Mesh, PartitionSpec as P

BLK = 128
REACH = 2
SWEEPS = 8
ALPHA = 0.001
HIGHEST = lax.Precision.HIGHEST
F32 = jnp.float32
BF16 = jnp.bfloat16


def tables(steps, low):
    ids = np.arange(steps)
    frequency = np.where(ids == 1, steps // 2, ids // 2)
    angles = 2.0 * np.pi / steps * ((frequency[:, None] * ids[None, :]) % steps)
    is_sine = (ids % 2 == 1) & (ids > 1)
    wave = np.where(is_sine[:, None], -np.sin(angles), np.cos(angles))
    scale = np.exp(math.log(ALPHA) * ids / steps)
    forward = wave * scale[None, :]
    weights = np.where(ids < 2, 1.0, 2.0) / steps
    inverse = (wave * weights[:, None]).T / scale[:, None]
    inverse = inverse.reshape(steps // (2 * low), low, 2, steps // 2, 2)
    inverse = inverse.transpose(1, 2, 0, 4, 3).reshape(low, steps // low, steps)
    beta = math.exp(math.log(ALPHA) / steps)
    pair = np.arange(steps // 2)
    theta = 2.0 * np.pi * pair / steps
    zero = pair == 0
    a_even = np.where(zero, 1.0 - beta, 1.0 - beta * np.cos(theta))
    a_odd = np.where(zero, 1.0 + beta, 1.0 - beta * np.cos(theta))
    b_even = np.where(zero, 0.0, -beta * np.sin(theta))
    factors = np.stack([a_even, a_odd, b_even, zero.astype(np.float64)], axis=1)
    return forward.astype(np.float32), inverse.astype(np.float32), factors.astype(np.float32)


def split3(value):
    high = value.astype(BF16)
    rest = value - high.astype(F32)
    mid = rest.astype(BF16)
    return high, mid, (rest - mid.astype(F32)).astype(BF16)


def bank_kernel(bank_ref, w1, w2, w3, v1, v2, v3):
    for tile in range(bank_ref.shape[0]):
        pair, side = tile // 2, slice(tile % 2 * BLK, tile % 2 * BLK + BLK)
        value = bank_ref[tile]
        for mat, (o1, o2, o3) in ((value, (w1, w2, w3)), (value.T, (v1, v2, v3))):
            high, mid, low = split3(mat)
            o1[pair, :BLK, side] = high
            o1[pair, BLK:, side] = high
            o2[pair, :BLK, side] = mid
            o2[pair, BLK:, side] = mid
            o3[pair, :BLK, side] = low
            o3[pair, BLK:, side] = high


def swapped(value):
    rows = value.shape[0]
    even = lax.broadcasted_iota(jnp.int32, value.shape, 0) % 2 == 0
    return jnp.where(even, pltpu.roll(value, rows - 1, 0), pltpu.roll(value, 1, 0))


def doubled(value, odd):
    rows = value.shape[0]
    even = lax.broadcasted_iota(jnp.int32, value.shape, 0) % 2 == 0
    if odd:
        return jnp.where(even, pltpu.roll(value, rows - 1, 0), value)
    return jnp.where(even, value, pltpu.roll(value, 1, 0))


def make_solve(nb, ncb, co, tiles, knb, gnb, lay):
    nrow = 2 * nb * co
    crow = 2 * ncb * co
    prow = tiles * nrow

    def kernel(
        fac_ref, own_ref, r_ref, w1, w2, w3, v1, v2, v3, out_ref,
        p_ref, q_ref, acc, xs, rhs, e_ref, c_ref, gy, sc, istab, idxv, idxs, sem,
    ):
        a_even, a_odd, b_even, is_zero = fac_ref[0], fac_ref[1], fac_ref[2], fac_ref[3]

        def part(name, rows):
            return r_ref[lay[name] * 2 * co : lay[name] * 2 * co + rows]

        idxv[...] = part("idx", 2 * co).astype(jnp.int32)
        copy = pltpu.make_async_copy(idxv, idxs, sem)
        copy.start()
        p_ref[prow : prow + 8] = jnp.zeros((8, BLK), F32)

        def products(value, mats, dst):
            rows = value.shape[0]
            high, mid, low = split3(value)
            two = jnp.concatenate([high, mid], axis=1)
            ends = jnp.concatenate([high, low], axis=1)
            m1, m2, m3 = mats
            for pair in range(tiles // 2):
                res = jnp.dot(two, m1[pair], preferred_element_type=F32)
                res += jnp.dot(two, m2[pair], preferred_element_type=F32)
                res += jnp.dot(ends, m3[pair], preferred_element_type=F32)
                for side in range(2):
                    start = (2 * pair + side) * rows
                    dst[start : start + rows] = res[:, side * BLK : side * BLK + BLK]

        def couple():
            for b in range(nb):
                for o in range(co):
                    row = (b * co + o) * 2
                    total = p_ref[pl.ds(idxs[2 * o, b * knb], 2), :]
                    for k in range(1, knb):
                        total = total + p_ref[pl.ds(idxs[2 * o, b * knb + k], 2), :]
                    acc[row : row + 2] = total

        def constrain():
            for c in range(ncb):
                for o in range(co):
                    row = (c * co + o) * 2
                    at = nb * knb + c * gnb
                    total = p_ref[pl.ds(idxs[2 * o, at], 2), :]
                    for j in range(1, gnb):
                        total = total + p_ref[pl.ds(idxs[2 * o, at + j], 2), :]
                    gy[row : row + 2] = total

        def scatter():
            for c in range(ncb):
                for o in range(co):
                    row = (c * co + o) * 2
                    for j in range(gnb):
                        at = idxs[2 * o, nb * knb + c * gnb + j]
                        tile = at // nrow
                        dst = pl.ds(at - tile * nrow, 2)
                        acc[dst, :] += q_ref[pl.ds(tile * crow + row, 2), :]

        even = lax.broadcasted_iota(jnp.int32, (nrow, BLK), 0) % 2 == 0
        state = part("state", nrow)
        mult = part("mult", crow)
        products(state, (w1, w2, w3), p_ref)
        products(mult, (v1, v2, v3), q_ref)
        cm = part("wrap", nrow)
        mass = doubled(cm, True)
        half = part("stiff", nrow // 2)
        stiff = jnp.concatenate([doubled(half, False), doubled(half, True)], axis=0)
        shalf = part("stab", crow // 2)
        stab = jnp.concatenate([doubled(shalf, False), doubled(shalf, True)], axis=0)
        wrap = jnp.where(even, cm, is_zero * pltpu.roll(cm, 1, 0))
        a_self = jnp.where(even, a_even, a_odd)
        a_other = jnp.where(even, a_odd, a_even)
        b_self = jnp.where(even, b_even, -b_even)
        d_self = a_self * mass + stiff
        d_other = a_other * mass + stiff
        cross = b_self * mass
        inv = 1.0 / (d_self * d_other + cross * cross)
        e_ref[...] = d_other * inv
        c_ref[...] = cross * inv
        istab[...] = 1.0 / stab
        copy.wait()
        couple()
        constrain()
        scatter()
        spec = part("force", nrow) + wrap - (d_self * state + cross * swapped(state)) - acc[...]
        rhs[...] = spec
        sc[...] = stab * mult - gy[...]
        xs[...] = e_ref[...] * spec - c_ref[...] * swapped(spec)

        def sweep(_, carry):
            products(xs[...], (w1, w2, w3), p_ref)
            constrain()
            products((gy[...] - sc[...]) * istab[...], (v1, v2, v3), q_ref)
            couple()
            scatter()
            res = rhs[...] - acc[...]
            xs[...] = e_ref[...] * res - c_ref[...] * swapped(res)
            return carry

        lax.fori_loop(0, SWEEPS - 1, sweep, 0)
        products(xs[...], (w1, w2, w3), p_ref)
        constrain()
        gy[...] = (gy[...] - sc[...]) * istab[...]
        own = own_ref[0]
        parts = out_ref.shape[0] // (4 * lay["chunks"])
        for b in range(nb + ncb):
            src, blk = (xs, b) if b < nb else (gy, b - nb)
            value = src[pl.ds((blk * co + own) * 2, 2), :]
            for z in range(parts):
                row = ((b // 2) * parts + z) * 4 + b % 2 * 2
                out_ref[row : row + 2] = value
        used = -(-(nb + ncb) // 2) * parts * 4
        out_ref[used:] = jnp.zeros((out_ref.shape[0] - used, BLK), F32)

    return kernel, [
        pltpu.VMEM((prow + 8, BLK), F32),
        pltpu.VMEM((tiles * crow, BLK), F32),
        pltpu.VMEM((nrow, BLK), F32),
        pltpu.VMEM((nrow, BLK), F32),
        pltpu.VMEM((nrow, BLK), F32),
        pltpu.VMEM((nrow, BLK), F32),
        pltpu.VMEM((nrow, BLK), F32),
        pltpu.VMEM((crow, BLK), F32),
        pltpu.VMEM((crow, BLK), F32),
        pltpu.VMEM((crow, BLK), F32),
        pltpu.VMEM((2 * co, BLK), jnp.int32),
        pltpu.SMEM((2 * co, BLK), jnp.int32),
        pltpu.SemaphoreType.DMA(()),
    ]


def inverse_kernel(table_ref, x_ref, out_ref):
    slots = table_ref.shape[1]
    rows = table_ref.shape[0]
    for h in range(2):
        value = jnp.concatenate(
            [x_ref[pl.ds(2 * h + s, slots // 2, stride=4), :] for s in range(2)], axis=0
        )
        res = jnp.dot(table_ref[...], value, precision=HIGHEST, preferred_element_type=F32)
        for l in range(2):
            half = rows // 2
            out_ref[pl.ds(2 * h + l, half, stride=4), :] = res[l * half : (l + 1) * half]


VM = pl.BlockSpec(memory_space=pltpu.VMEM)
SM = pl.BlockSpec(memory_space=pltpu.SMEM)


def layout(nb, ncb):
    state, force, mult = 0, nb, 2 * nb
    wrap = mult + ncb
    stiff = wrap + nb
    stab = stiff + nb // 2
    idx = stab + ncb // 2
    return {"state": state, "force": force, "mult": mult, "wrap": wrap, "stiff": stiff, "stab": stab, "idx": idx}


def solve_call(fac, own, recv, mats, nb, ncb, co, tiles, knb, gnb, lay, parts):
    kernel, scratch = make_solve(nb, ncb, co, tiles, knb, gnb, lay)
    return pl.pallas_call(
        kernel,
        out_shape=jax.ShapeDtypeStruct((lay["chunks"] * parts * 4, BLK), F32),
        in_specs=[SM, SM] + [VM] * 7,
        out_specs=VM,
        scratch_shapes=scratch,
        name="solve",
    )(fac, own, recv, *mats)


def bank_call(bank):
    shape = jax.ShapeDtypeStruct((bank.shape[0] // 2, 2 * BLK, 2 * BLK), BF16)
    return pl.pallas_call(
        bank_kernel, out_shape=[shape] * 6, in_specs=[VM], out_specs=[VM] * 6, name="bank"
    )(bank)


def inverse_call(table, value, high):
    return pl.pallas_call(
        inverse_kernel,
        out_shape=jax.ShapeDtypeStruct((high * 4, BLK), F32),
        in_specs=[VM, VM],
        out_specs=VM,
        name="inverse",
    )(table, value)


def index_row(k_offsets, k_tiles, g_cols, g_tiles, o, nb, co, tiles):
    block = o * nb + jnp.arange(nb, dtype=jnp.int32)[:, None] + k_offsets - REACH
    inside = (block >= 0) & (block < nb * co)
    stored = ((block % nb) * co + block // nb) * 2
    rows = nb * co * 2
    k_rows = jnp.where(inside, k_tiles * rows + stored, tiles * rows)
    g_rows = g_tiles * rows + (g_cols * co + o) * 2
    both = jnp.concatenate([k_rows.reshape(-1), g_rows.reshape(-1)])
    return jnp.pad(both, (0, 2 * BLK - both.shape[0])).astype(F32).reshape(1, 2, BLK)


def make_local(forward, inverse, factors, low):
    steps = forward.shape[0]
    group = ("high", "low")

    def blocks(value):
        return value.reshape(value.shape[0], -1, BLK).transpose(1, 0, 2)

    def local(
        state, multiplier, force, initial, mass, stiff_diag, stab,
        bank, k_offsets, k_tiles, g_cols, g_tiles,
    ):
        nb = state.shape[1] // BLK
        ncb = multiplier.shape[1] // BLK
        tiles = bank.shape[0]
        tm = lax.axis_size(group)
        co = lax.axis_size("coord")
        high = tm // low
        t = lax.axis_index(group)
        o = lax.axis_index("coord")
        lay = layout(nb, ncb)
        lay["chunks"] = high
        first = jnp.where(t == 0, mass * initial, 0.0)
        force = force + jnp.stack([first, jnp.zeros_like(first)])
        st = blocks(state)
        sent = jnp.concatenate([st, blocks(force), blocks(multiplier), st], axis=0)
        sent = jnp.pad(sent, ((0, tm - sent.shape[0]), (0, 0), (0, 0)))
        columns = lax.all_to_all(sent, group, split_axis=0, concat_axis=0, tiled=True)
        columns = columns.reshape(steps, BLK)

        mb = mass.reshape(nb, BLK)
        extra = jnp.concatenate(
            [
                jnp.stack([jnp.zeros_like(mb), mb], axis=1),
                stiff_diag.reshape(2, nb // 2, BLK).transpose(1, 0, 2),
                stab.reshape(2, ncb // 2, BLK).transpose(1, 0, 2),
                index_row(k_offsets, k_tiles, g_cols, g_tiles, o, nb, co, tiles),
            ],
            axis=0,
        )
        at = t - lay["wrap"]
        extra = lax.dynamic_index_in_dim(
            extra, jnp.clip(at, 0, extra.shape[0] - 1), 0, keepdims=False
        )
        last = columns[-1] * extra[1] * -ALPHA
        is_wrap = (at >= 0) & (at < nb)
        extra = extra + jnp.stack([jnp.where(is_wrap, last, 0.0), jnp.zeros_like(last)])
        spectrum = jnp.dot(forward, columns, precision=HIGHEST).reshape(tm, 2, BLK)
        spectrum = jnp.where(at < 0, spectrum, extra[None])
        spread = jnp.broadcast_to(spectrum[:, None], (tm, co, 2, BLK)).reshape(tm * co, 2, BLK)
        recv = lax.all_to_all(
            spread, group + ("coord",), split_axis=0, concat_axis=0, tiled=True
        ).reshape(tm * co * 2, BLK)

        mats = bank_call(bank)
        fac = lax.dynamic_index_in_dim(jnp.asarray(factors), t, 0, keepdims=False)
        solved = solve_call(
            fac, o.reshape(1).astype(jnp.int32), recv, mats,
            nb, ncb, co, tiles, k_tiles.shape[1], g_tiles.shape[1], lay, low,
        )
        slots = lax.all_to_all(
            solved.reshape(tm, 4, BLK), group, split_axis=0, concat_axis=0, tiled=True
        ).reshape(tm * 4, BLK)
        table = lax.dynamic_index_in_dim(
            jnp.asarray(inverse), lax.axis_index("low"), 0, keepdims=False
        )
        rows = inverse_call(table, slots, high).reshape(high, 4, BLK)
        rows = lax.all_to_all(rows, "high", split_axis=0, concat_axis=0, tiled=True)
        rows = rows.reshape(high * 2, 2, BLK)
        update = rows[: nb + ncb].transpose(1, 0, 2).reshape(2, (nb + ncb) * BLK)
        return state + update[:, : nb * BLK], multiplier + update[:, nb * BLK :]

    return local


def solution(mesh):
    tm, co = mesh.shape["tm"], mesh.shape["coord"]
    low = 4
    split = Mesh(mesh.devices.reshape(tm // low, low, co), ("high", "low", "coord"))
    forward, inverse, factors = tables(2 * tm, low)
    time = ("high", "low")
    return jax.shard_map(
        make_local(forward, inverse, factors, low),
        mesh=split,
        in_specs=(
            P(time, "coord"),
            P(time, "coord"),
            P(time, "coord"),
            P("coord"),
            P("coord"),
            P("coord"),
            P("coord"),
            P(),
            P("coord", None),
            P("coord", None),
            P("coord", None),
            P("coord", None),
        ),
        out_specs=(P(time, "coord"), P(time, "coord")),
        check_vma=False,
    )
```

profile of v0, /device:TPU:1, one launch (start us, length us, event | category | flops | bytes accessed | tf_op | source)
XLA Modules:
  0.0 136.4 jit_solution(10318801272966490393)
XLA Ops:
  0.7 0.7 copy-done.4
  1.3 0.7 multiply_select_fusion
  2.1 0.7 copy-done.3
  2.8 0.7 select_maximum_fusion
  3.5 21.0 %all-to-all-start = ((f32[128,2,128]{2,1,0:T(2,128)}), f32[128,2,128]{2,1,0:T(2,128)S(1)}, u32[]{:S(2)}, u32[]{:S(2)}) async-start(f32[128,2,128]{2,1,0:T(2,128)} %select_maximum_fusion), calls=%async_computation | async-start | bytes 262144 | tf_op jit(solution)/shard_map/all_to_all | solution.py:305
  24.6 0.6 copy-done.9
  25.5 0.5 copy-done.10
  26.1 0.7 copy-done.12
  26.8 13.1 %all-to-all-done = f32[128,2,128]{2,1,0:T(2,128)S(1)} async-done(((f32[128,2,128]{2,1,0:T(2,128)}), f32[128,2,128]{2,1,0:T(2,128)S(1)}, u32[]{:S(2)}, u32[]{:S(2)}) %all-to-all-start) | async-done | bytes 131104 | tf_op jit(solution)/shard_map/all_to_all | solution.py:305
  40.3 0.9 broadcast_in_dim.32
  41.3 9.4 %all-to-all-start.1 = ((f32[512,2,128]{2,1,0:T(2,128)}), f32[512,2,128]{2,1,0:T(2,128)S(1)}, u32[]{:S(2)}, u32[]{:S(2)}) async-start(f32[512,2,128]{2,1,0:T(2,128)} %bitcast.20), calls=%async_computation.1 | async-start | bytes 1048576 | tf_op jit(solution)/shard_map/all_to_all | solution.py:328
  50.7 4.6 %bank.1 = (bf16[8,256,256]{2,1,0:T(8,128)(2,1)}, bf16[8,256,256]{2,1,0:T(8,128)(2,1)}, bf16[8,256,256]{2,1,0:T(8,128)(2,1)}, bf16[8,256,256]{2,1,0:T(8,128)(2,1)...) custom-call(f32[16,128,128]{2,1,0:T(8,128)} %bank_ref.1), custom_call_target="tpu_custom_call" | custom-call | tf_op jit(solution)/shard_map/bank/pallas_call | solution.py:253
  55.3 1.2 fusion.10.fac_ref
  56.5 16.1 %all-to-all-done.1 = f32[512,2,128]{2,1,0:T(2,128)S(1)} async-done(((f32[512,2,128]{2,1,0:T(2,128)}), f32[512,2,128]{2,1,0:T(2,128)S(1)}, u32[]{:S(2)}, u32[]{:S(2)}) %all-to-all-start.1) | async-done | bytes 524320 | tf_op jit(solution)/shard_map/all_to_all | solution.py:328
  72.5 0.8 copy-done
  73.3 21.9 %solve.1 = f32[512,128]{1,0:T(8,128)} custom-call(f32[4]{0:T(128)} %fusion.10.fac_ref, s32[1]{0:T(128)} %bitcast.2.own_ref, f32[1024,128]{1,0:T(8,128)} %bitcast.46, bf16[8,256,256]{2,1,0:T(8,128)(2,1)} %get-tuple-element.8.w1, bf16[8,256,256]{2,1,0:T(8,128)(2,1)} %get-tuple-element.9.w2, bf16[8,256,256]{2,1,0:T(8,128)(2,1)} %get-tuple-element.10.w3, ...), custom_call_target="tpu_custom_call" | custom-call | tf_op jit(solution)/shard_map/solve/pallas_call | solution.py:241
  95.2 7.1 %all-to-all-start.2 = ((f32[128,4,128]{2,1,0:T(4,128)}), f32[128,4,128]{2,1,0:T(4,128)S(1)}, u32[]{:S(2)}, u32[]{:S(2)}) async-start(f32[128,4,128]{2,1,0:T(4,128)} %bitcast.48), calls=%async_computation.2 | async-start | bytes 524288 | tf_op jit(solution)/shard_map/all_to_all | solution.py:338
  102.3 1.5 %dynamic-slice_bitcast_fusion.table_ref = f32[64,256]{1,0:T(8,128)} fusion(f32[4,64,256]{2,1,0:T(8,128)} %constant.93.clone, s32[]{:T(128)S(6)} %select_n.55), kind=kLoop, calls=%fused_computation.4 | loop fusion | bytes 131076 | tf_op jit(solution)/shard_map/jit(dynamic_index_in_dim)/squeeze | solution.py:341
  103.8 16.0 %all-to-all-done.2 = f32[128,4,128]{2,1,0:T(4,128)S(1)} async-done(((f32[128,4,128]{2,1,0:T(4,128)}), f32[128,4,128]{2,1,0:T(4,128)S(1)}, u32[]{:S(2)}, u32[]{:S(2)}) %all-to-all-start.2) | async-done | bytes 262176 | tf_op jit(solution)/shard_map/all_to_all | solution.py:338
  119.7 0.7 copy-done.1
  120.4 1.9 %inverse.1 = f32[128,128]{1,0:T(8,128)} custom-call(f32[64,256]{1,0:T(8,128)} %dynamic-slice_bitcast_fusion.table_ref, f32[512,128]{1,0:T(8,128)} %bitcast.47), custom_call_target="tpu_custom_call" | custom-call | tf_op jit(solution)/shard_map/inverse/pallas_call | solution.py:259
  122.3 12.8 %all_to_all.20 = f32[32,4,128]{2,1,0:T(4,128)S(1)} all-to-all(f32[32,4,128]{2,1,0:T(4,128)} %bitcast.53), channel_id=1, replica_groups=mesh['high'=32,'low'=4,'coord'=4] {'high'}, dimensions={0} | all-to-all | bytes 131072 | tf_op jit(solution)/shard_map/all_to_all | solution.py:345
  135.2 0.6 slice_add_fusion
  135.8 0.6 slice_add_fusion.1
  (37 shorter events, 0.9 us)
Async XLA Ops:
  0.6 0.7 copy-start.4
  0.6 1.4 %copy-start.5 = (f32[2,4096]{1,0:T(2,128)S(1)}, f32[2,4096]{1,0:T(2,128)}, u32[]{:S(2)}) copy-start(f32[2,4096]{1,0:T(2,128)} %param.17) | copy-start | bytes 98308
  2.1 0.8 copy-start.3
  2.1 0.8 copy-start.6
  3.5 36.4 %copy-start.2 = (f32[256,256]{1,0:T(8,128)S(1)}, f32[256,256]{1,0:T(8,128)}, u32[]{:S(2)}) copy-start(f32[256,256]{1,0:T(8,128)} %constant.91.clone) | copy-start | bytes 786436
  3.5 36.4 %all-to-all-start = ((f32[128,2,128]{2,1,0:T(2,128)}), f32[128,2,128]{2,1,0:T(2,128)S(1)}, u32[]{:S(2)}, u32[]{:S(2)}) async-start(f32[128,2,128]{2,1,0:T(2,128)} %select_maximum_fusion), calls=%async_computation | async-start | bytes 262144 | tf_op jit(solution)/shard_map/all_to_all | solution.py:305
  24.5 0.7 copy-start.9
  24.5 0.7 copy-start.8
  25.2 0.7 copy-start.10
  25.3 0.7 copy-start.11
  25.4 0.8 copy-start.7
  26.1 0.7 copy-start.12
  41.3 31.3 %all-to-all-start.1 = ((f32[512,2,128]{2,1,0:T(2,128)}), f32[512,2,128]{2,1,0:T(2,128)S(1)}, u32[]{:S(2)}, u32[]{:S(2)}) async-start(f32[512,2,128]{2,1,0:T(2,128)} %bitcast.20), calls=%async_computation.1 | async-start | bytes 1048576 | tf_op jit(solution)/shard_map/all_to_all | solution.py:328
  72.5 0.8 copy-start
  95.2 24.5 %all-to-all-start.2 = ((f32[128,4,128]{2,1,0:T(4,128)}), f32[128,4,128]{2,1,0:T(4,128)S(1)}, u32[]{:S(2)}, u32[]{:S(2)}) async-start(f32[128,4,128]{2,1,0:T(4,128)} %bitcast.48), calls=%async_computation.2 | async-start | bytes 524288 | tf_op jit(solution)/shard_map/all_to_all | solution.py:338
  119.7 0.7 copy-start.1
where the time goes:
time: 138 us; the launch traced here: 136 us
  waiting for transfers between devices  45.1 us (33%)
  starting transfers between devices  37.4 us (27%)
  Pallas kernels  28.4 us (21%)
  blocking collectives  12.8 us (9%)
  local copies, waits for them, and re-layouts  8.63 us (6%)
  other arithmetic  2.82 us (2%)
    pallas_call x1, Pallas kernels, solve_call(): pl.pallas_call(kernel, out_shape=jax.ShapeDtypeStruct((lay['chunks'] * pa...  21.9 us
    all_to_all x1, starting transfers between devices, local(): lax.all_to_all(sent, group, split_axis=0, concat_axis=0, tiled=True)  21 us
    all_to_all x1, waiting for transfers between devices, local(): lax.all_to_all(spread, group + ('coord',), split_axis=0, concat_axis=0, t...  16.1 us
    all_to_all x1, waiting for transfers between devices, local(): lax.all_to_all(solved.reshape(tm, 4, BLK), group, split_axis=0, concat_ax...  16 us
    all_to_all x1, waiting for transfers between devices, local(): lax.all_to_all(sent, group, split_axis=0, concat_axis=0, tiled=True)  13.1 us
    all_to_all x1, blocking collectives, local(): rows = lax.all_to_all(rows, 'high', split_axis=0, concat_axis=0, tiled=True)  12.8 us
    all_to_all x1, starting transfers between devices, local(): lax.all_to_all(spread, group + ('coord',), split_axis=0, concat_axis=0, t...  9.38 us
    all_to_all x1, starting transfers between devices, local(): lax.all_to_all(solved.reshape(tm, 4, BLK), group, split_axis=0, concat_ax...  7.08 us
  transfers between devices with their start and end apart: 3, of which 3 were waited for; matrix products, arithmetic and copies ran while one was open for 2% of the time, Pallas kernels for 3%

commit v1 on v0

--- a/solution.py
+++ b/solution.py
@@ -27,8 +27,9 @@
     forward = wave * scale[None, :]
     weights = np.where(ids < 2, 1.0, 2.0) / steps
     inverse = (wave * weights[:, None]).T / scale[:, None]
-    inverse = inverse.reshape(steps // (2 * low), low, 2, steps // 2, 2)
-    inverse = inverse.transpose(1, 2, 0, 4, 3).reshape(low, steps // low, steps)
+    inverse = inverse.reshape(steps // (2 * low), low, 1, 2, steps // 2, 1, 2).swapaxes(0, 1)
+    inverse = inverse * np.eye(2).reshape(1, 1, 2, 1, 1, 2, 1)
+    inverse = inverse.reshape(2 * steps, 2 * steps)
     beta = math.exp(math.log(ALPHA) / steps)
     pair = np.arange(steps // 2)
     theta = 2.0 * np.pi * pair / steps
@@ -51,14 +52,9 @@
     for tile in range(bank_ref.shape[0]):
         pair, side = tile // 2, slice(tile % 2 * BLK, tile % 2 * BLK + BLK)
         value = bank_ref[tile]
-        for mat, (o1, o2, o3) in ((value, (w1, w2, w3)), (value.T, (v1, v2, v3))):
-            high, mid, low = split3(mat)
-            o1[pair, :BLK, side] = high
-            o1[pair, BLK:, side] = high
-            o2[pair, :BLK, side] = mid
-            o2[pair, BLK:, side] = mid
-            o3[pair, :BLK, side] = low
-            o3[pair, BLK:, side] = high
+        for mat, outs in ((value, (w1, w2, w3)), (value.T, (v1, v2, v3))):
+            for out, piece in zip(outs, split3(mat)):
+                out[pair, :, side] = piece
 
 
 def swapped(value):
@@ -82,17 +78,33 @@
 
     def kernel(
         fac_ref, own_ref, r_ref, w1, w2, w3, v1, v2, v3, out_ref,
-        p_ref, q_ref, acc, xs, rhs, e_ref, c_ref, gy, sc, istab, idxv, idxs, sem,
+        p_ref, q_ref, acc, gts, xs, rhs, e_ref, c_ref, gy, sc, istab, idxv, idxs, sem,
     ):
         a_even, a_odd, b_even, is_zero = fac_ref[0], fac_ref[1], fac_ref[2], fac_ref[3]
 
         def part(name, rows):
             return r_ref[lay[name] * 2 * co : lay[name] * 2 * co + rows]
 
-        idxv[...] = part("idx", 2 * co).astype(jnp.int32)
+        raw = part("idx", 2 * co).astype(jnp.int32)
+        lane = lax.broadcasted_iota(jnp.int32, raw.shape, 1)
+        line = lax.broadcasted_iota(jnp.int32, raw.shape, 0)
+        coord = line // 2
+        column = jnp.where(line % 2 == 0, raw, pltpu.roll(raw, 1, 0))
+        tile = jnp.where(line % 2 == 0, pltpu.roll(raw, 2 * co - 1, 0), raw)
+        block = coord * nb + lane // knb + column - REACH
+        inside = (block >= 0) & (block < nb * co)
+        k_row = ((block % nb) * co + block // nb) * 2
+        k_row = jnp.where(inside, tile * nrow + k_row, prow)
+        g_row = (column * co + coord) * 2
+        is_k = lane < nb * knb
+        q_row = tile * crow + (((lane - nb * knb) // gnb) * co + coord) * 2
+        idxv[: 2 * co] = jnp.where(is_k, k_row, tile * nrow + g_row)
+        idxv[2 * co : 4 * co] = q_row
+        idxv[4 * co :] = g_row
         copy = pltpu.make_async_copy(idxv, idxs, sem)
         copy.start()
         p_ref[prow : prow + 8] = jnp.zeros((8, BLK), F32)
+        gts[...] = jnp.zeros(gts.shape, F32)
 
         def products(value, mats, dst):
             rows = value.shape[0]
@@ -101,9 +113,10 @@
             ends = jnp.concatenate([high, low], axis=1)
             m1, m2, m3 = mats
             for pair in range(tiles // 2):
-                res = jnp.dot(two, m1[pair], preferred_element_type=F32)
-                res += jnp.dot(two, m2[pair], preferred_element_type=F32)
-                res += jnp.dot(ends, m3[pair], preferred_element_type=F32)
+                b1, b2, b3 = m1[pair], m2[pair], m3[pair]
+                res = jnp.dot(two, jnp.concatenate([b1, b1]), preferred_element_type=F32)
+                res += jnp.dot(two, jnp.concatenate([b2, b2]), preferred_element_type=F32)
+                res += jnp.dot(ends, jnp.concatenate([b3, b1]), preferred_element_type=F32)
                 for side in range(2):
                     start = (2 * pair + side) * rows
                     dst[start : start + rows] = res[:, side * BLK : side * BLK + BLK]
@@ -130,12 +143,16 @@
         def scatter():
             for c in range(ncb):
                 for o in range(co):
-                    row = (c * co + o) * 2
                     for j in range(gnb):
-                        at = idxs[2 * o, nb * knb + c * gnb + j]
-                        tile = at // nrow
-                        dst = pl.ds(at - tile * nrow, 2)
-                        acc[dst, :] += q_ref[pl.ds(tile * crow + row, 2), :]
+                        src = idxs[2 * (co + o), nb * knb + c * gnb + j]
+                        dst = idxs[2 * (2 * co + o), nb * knb + c * gnb + j]
+                        gts[c, pl.ds(dst, 2), :] = q_ref[pl.ds(src, 2), :]
+
+        def coupled():
+            total = acc[...]
+            for c in range(ncb):
+                total = total + gts[c]
+            return total
 
         even = lax.broadcasted_iota(jnp.int32, (nrow, BLK), 0) % 2 == 0
         state = part("state", nrow)
@@ -163,7 +180,7 @@
         couple()
         constrain()
         scatter()
-        spec = part("force", nrow) + wrap - (d_self * state + cross * swapped(state)) - acc[...]
+        spec = part("force", nrow) + wrap - (d_self * state + cross * swapped(state)) - coupled()
         rhs[...] = spec
         sc[...] = stab * mult - gy[...]
         xs[...] = e_ref[...] * spec - c_ref[...] * swapped(spec)
@@ -174,7 +191,7 @@
             products((gy[...] - sc[...]) * istab[...], (v1, v2, v3), q_ref)
             couple()
             scatter()
-            res = rhs[...] - acc[...]
+            res = rhs[...] - coupled()
             xs[...] = e_ref[...] * res - c_ref[...] * swapped(res)
             return carry
 
@@ -197,6 +214,7 @@
         pltpu.VMEM((prow + 8, BLK), F32),
         pltpu.VMEM((tiles * crow, BLK), F32),
         pltpu.VMEM((nrow, BLK), F32),
+        pltpu.VMEM((ncb, nrow, BLK), F32),
         pltpu.VMEM((nrow, BLK), F32),
         pltpu.VMEM((nrow, BLK), F32),
         pltpu.VMEM((nrow, BLK), F32),
@@ -204,23 +222,10 @@
         pltpu.VMEM((crow, BLK), F32),
         pltpu.VMEM((crow, BLK), F32),
         pltpu.VMEM((crow, BLK), F32),
-        pltpu.VMEM((2 * co, BLK), jnp.int32),
-        pltpu.SMEM((2 * co, BLK), jnp.int32),
+        pltpu.VMEM((6 * co, BLK), jnp.int32),
+        pltpu.SMEM((6 * co, BLK), jnp.int32),
         pltpu.SemaphoreType.DMA(()),
     ]
-
-
-def inverse_kernel(table_ref, x_ref, out_ref):
-    slots = table_ref.shape[1]
-    rows = table_ref.shape[0]
-    for h in range(2):
-        value = jnp.concatenate(
-            [x_ref[pl.ds(2 * h + s, slots // 2, stride=4), :] for s in range(2)], axis=0
-        )
-        res = jnp.dot(table_ref[...], value, precision=HIGHEST, preferred_element_type=F32)
-        for l in range(2):
-            half = rows // 2
-            out_ref[pl.ds(2 * h + l, half, stride=4), :] = res[l * half : (l + 1) * half]
 
 
 VM = pl.BlockSpec(memory_space=pltpu.VMEM)
@@ -249,31 +254,17 @@
 
 
 def bank_call(bank):
-    shape = jax.ShapeDtypeStruct((bank.shape[0] // 2, 2 * BLK, 2 * BLK), BF16)
+    shape = jax.ShapeDtypeStruct((bank.shape[0] // 2, BLK, 2 * BLK), BF16)
     return pl.pallas_call(
         bank_kernel, out_shape=[shape] * 6, in_specs=[VM], out_specs=[VM] * 6, name="bank"
     )(bank)
 
 
-def inverse_call(table, value, high):
-    return pl.pallas_call(
-        inverse_kernel,
-        out_shape=jax.ShapeDtypeStruct((high * 4, BLK), F32),
-        in_specs=[VM, VM],
-        out_specs=VM,
-        name="inverse",
-    )(table, value)
-
-
-def index_row(k_offsets, k_tiles, g_cols, g_tiles, o, nb, co, tiles):
-    block = o * nb + jnp.arange(nb, dtype=jnp.int32)[:, None] + k_offsets - REACH
-    inside = (block >= 0) & (block < nb * co)
-    stored = ((block % nb) * co + block // nb) * 2
-    rows = nb * co * 2
-    k_rows = jnp.where(inside, k_tiles * rows + stored, tiles * rows)
-    g_rows = g_tiles * rows + (g_cols * co + o) * 2
-    both = jnp.concatenate([k_rows.reshape(-1), g_rows.reshape(-1)])
-    return jnp.pad(both, (0, 2 * BLK - both.shape[0])).astype(F32).reshape(1, 2, BLK)
+def index_rows(k_offsets, k_tiles, g_cols, g_tiles):
+    first = jnp.concatenate([k_offsets.reshape(-1), g_cols.reshape(-1)])
+    second = jnp.concatenate([k_tiles.reshape(-1), g_tiles.reshape(-1)])
+    both = jnp.pad(jnp.stack([first, second]), ((0, 0), (0, BLK - first.shape[0])))
+    return both.astype(F32)[None]
 
 
 def make_local(forward, inverse, factors, low):
@@ -297,8 +288,6 @@
         o = lax.axis_index("coord")
         lay = layout(nb, ncb)
         lay["chunks"] = high
-        first = jnp.where(t == 0, mass * initial, 0.0)
-        force = force + jnp.stack([first, jnp.zeros_like(first)])
         st = blocks(state)
         sent = jnp.concatenate([st, blocks(force), blocks(multiplier), st], axis=0)
         sent = jnp.pad(sent, ((0, tm - sent.shape[0]), (0, 0), (0, 0)))
@@ -308,10 +297,10 @@
         mb = mass.reshape(nb, BLK)
         extra = jnp.concatenate(
             [
-                jnp.stack([jnp.zeros_like(mb), mb], axis=1),
+                jnp.stack([initial.reshape(nb, BLK), mb], axis=1),
                 stiff_diag.reshape(2, nb // 2, BLK).transpose(1, 0, 2),
                 stab.reshape(2, ncb // 2, BLK).transpose(1, 0, 2),
-                index_row(k_offsets, k_tiles, g_cols, g_tiles, o, nb, co, tiles),
+                index_rows(k_offsets, k_tiles, g_cols, g_tiles),
             ],
             axis=0,
         )
@@ -319,9 +308,9 @@
         extra = lax.dynamic_index_in_dim(
             extra, jnp.clip(at, 0, extra.shape[0] - 1), 0, keepdims=False
         )
-        last = columns[-1] * extra[1] * -ALPHA
         is_wrap = (at >= 0) & (at < nb)
-        extra = extra + jnp.stack([jnp.where(is_wrap, last, 0.0), jnp.zeros_like(last)])
+        wrap = jnp.where(is_wrap, extra[1] * (extra[0] - ALPHA * columns[-1]), extra[0])
+        extra = jnp.stack([wrap, extra[1]])
         spectrum = jnp.dot(forward, columns, precision=HIGHEST).reshape(tm, 2, BLK)
         spectrum = jnp.where(at < 0, spectrum, extra[None])
         spread = jnp.broadcast_to(spectrum[:, None], (tm, co, 2, BLK)).reshape(tm * co, 2, BLK)
@@ -330,6 +319,7 @@
         ).reshape(tm * co * 2, BLK)
 
         mats = bank_call(bank)
+        recv = pltpu.with_memory_space_constraint(recv, pltpu.VMEM)
         fac = lax.dynamic_index_in_dim(jnp.asarray(factors), t, 0, keepdims=False)
         solved = solve_call(
             fac, o.reshape(1).astype(jnp.int32), recv, mats,
@@ -338,10 +328,12 @@
         slots = lax.all_to_all(
             solved.reshape(tm, 4, BLK), group, split_axis=0, concat_axis=0, tiled=True
         ).reshape(tm * 4, BLK)
-        table = lax.dynamic_index_in_dim(
-            jnp.asarray(inverse), lax.axis_index("low"), 0, keepdims=False
+        table = lax.dynamic_slice_in_dim(
+            jnp.asarray(inverse), lax.axis_index("low") * (4 * high), 4 * high, axis=0
         )
-        rows = inverse_call(table, slots, high).reshape(high, 4, BLK)
+        table = lax.optimization_barrier(table)
+        rows = lax.optimization_barrier(jnp.dot(table, slots, precision=HIGHEST))
+        rows = rows.reshape(high, 4, BLK)
         rows = lax.all_to_all(rows, "high", split_axis=0, concat_axis=0, tiled=True)
         rows = rows.reshape(high * 2, 2, BLK)
         update = rows[: nb + ncb].transpose(1, 0, 2).reshape(2, (nb + ncb) * BLK)

time: 138 us -> 131 us (0.949)
  Pallas kernels: 28.4 us -> 22.2 us
    pallas_call x1, Pallas kernels: 21.9 us -> 18.9 us  [solve_call(): pl.pallas_call(kernel, out_shape=jax.ShapeDtypeStruct((lay['chunks'] * pa...]
    pallas_call x1 -> x0, Pallas kernels: 1.88 us -> none  [inverse_call(): pl.pallas_call(inverse_kernel, out_shape=jax.ShapeDtypeStruct((high * 4,...]
    all_to_all x1, waiting for transfers between devices: 13.1 us -> 11.5 us  [local(): lax.all_to_all(sent, group, split_axis=0, concat_axis=0, tiled=True)]
    squeeze x1, local copies, waits for them, and re-layouts: 1.47 us -> 0.01 us  [local(): extra[1] * (extra[0] - ALPHA * columns[-1])]
    unnamed x27 -> x25, local copies, waits for them, and re-layouts: 4.74 us -> 4.68 us
where the time goes in v1:
time: 131 us; the launch traced here: 130 us
  waiting for transfers between devices  45.3 us (35%)
  starting transfers between devices  37.5 us (29%)
  Pallas kernels  22.2 us (17%)
  blocking collectives  12.6 us (10%)
  local copies, waits for them, and re-layouts  8.17 us (6%)
  other arithmetic  2.92 us (2%)
    all_to_all x1, starting transfers between devices, local(): lax.all_to_all(sent, group, split_axis=0, concat_axis=0, tiled=True)  21 us
    pallas_call x1, Pallas kernels, solve_call(): pl.pallas_call(kernel, out_shape=jax.ShapeDtypeStruct((lay['chunks'] * pa...  18.9 us
    all_to_all x1, waiting for transfers between devices, local(): lax.all_to_all(spread, group + ('coord',), split_axis=0, concat_axis=0, t...  17.2 us
    all_to_all x1, waiting for transfers between devices, local(): lax.all_to_all(solved.reshape(tm, 4, BLK), group, split_axis=0, concat_ax...  16.5 us
    all_to_all x1, blocking collectives, local(): rows = lax.all_to_all(rows, 'high', split_axis=0, concat_axis=0, tiled=True)  12.6 us
    all_to_all x1, waiting for transfers between devices, local(): lax.all_to_all(sent, group, split_axis=0, concat_axis=0, tiled=True)  11.5 us
    all_to_all x1, starting transfers between devices, local(): lax.all_to_all(spread, group + ('coord',), split_axis=0, concat_axis=0, t...  9.38 us
    all_to_all x1, starting transfers between devices, local(): lax.all_to_all(solved.reshape(tm, 4, BLK), group, split_axis=0, concat_ax...  7.14 us
  transfers between devices with their start and end apart: 3, of which 3 were waited for; matrix products, arithmetic and copies ran while one was open for 2% of the time, Pallas kernels for 3%

profile of v1, /device:TPU:1, one launch (start us, length us, event | category | flops | bytes accessed | tf_op | source)
XLA Modules:
  0.0 130.2 jit_solution(313257271375723386)
XLA Ops:
  0.6 0.7 copy-done.2
  1.3 1.6 %select_maximum_fusion = f32[128,2,128]{2,1,0:T(2,128)} fusion(f32[32,2,128]{2,1,0:T(2,128)} %bitcast.61, f32[4,2,128]{2,1,0:T(2,128)S(1)} %bitcast.64, f32[32,2,128]{2,1,0:T(2,128)} %bitcast.62), kind=kLoop, calls=%fused_computation | loop fusion | flops 262144 | bytes 200704 | tf_op jit(solution)/shard_map/concatenate | solution.py:292
  2.9 21.0 %all-to-all-start = ((f32[128,2,128]{2,1,0:T(2,128)}), f32[128,2,128]{2,1,0:T(2,128)S(1)}, u32[]{:S(2)}, u32[]{:S(2)}) async-start(f32[128,2,128]{2,1,0:T(2,128)} %select_maximum_fusion), calls=%async_computation | async-start | bytes 262144 | tf_op jit(solution)/shard_map/all_to_all | solution.py:294
  23.9 0.7 copy-done.6
  24.7 0.6 copy-done.7
  25.5 0.5 copy-done.8
  26.1 0.6 copy-done.9
  26.9 0.6 copy-done.10
  27.7 11.5 %all-to-all-done = f32[128,2,128]{2,1,0:T(2,128)S(1)} async-done(((f32[128,2,128]{2,1,0:T(2,128)}), f32[128,2,128]{2,1,0:T(2,128)S(1)}, u32[]{:S(2)}, u32[]{:S(2)}) %all-to-all-start) | async-done | bytes 131104 | tf_op jit(solution)/shard_map/all_to_all | solution.py:294
  39.2 0.4 fusion.7
  39.7 0.9 broadcast_in_dim.20
  40.6 9.4 %all-to-all-start.1 = ((f32[512,2,128]{2,1,0:T(2,128)}), f32[512,2,128]{2,1,0:T(2,128)S(1)}, u32[]{:S(2)}, u32[]{:S(2)}) async-start(f32[512,2,128]{2,1,0:T(2,128)} %bitcast.21), calls=%async_computation.1 | async-start | bytes 1048576 | tf_op jit(solution)/shard_map/all_to_all | solution.py:317
  50.0 3.4 %bank.1 = (bf16[8,128,256]{2,1,0:T(8,128)(2,1)}, bf16[8,128,256]{2,1,0:T(8,128)(2,1)}, bf16[8,128,256]{2,1,0:T(8,128)(2,1)}, bf16[8,128,256]{2,1,0:T(8,128)(2,1)...) custom-call(f32[16,128,128]{2,1,0:T(8,128)} %bank_ref.1), custom_call_target="tpu_custom_call" | custom-call | tf_op jit(solution)/shard_map/bank/pallas_call | solution.py:258
  53.4 1.2 fusion.4.fac_ref
  54.6 17.2 %all-to-all-done.1 = f32[512,2,128]{2,1,0:T(2,128)S(1)} async-done(((f32[512,2,128]{2,1,0:T(2,128)}), f32[512,2,128]{2,1,0:T(2,128)S(1)}, u32[]{:S(2)}, u32[]{:S(2)}) %all-to-all-start.1) | async-done | bytes 524320 | tf_op jit(solution)/shard_map/all_to_all | solution.py:317
  71.8 18.9 %solve.1 = f32[512,128]{1,0:T(8,128)} custom-call(f32[4]{0:T(128)} %fusion.4.fac_ref, s32[1]{0:T(128)} %bitcast.1.own_ref, f32[1024,128]{1,0:T(8,128)S(1)} %bitcast.51, bf16[8,128,256]{2,1,0:T(8,128)(2,1)} %get-tuple-element.8.w1, bf16[8,128,256]{2,1,0:T(8,128)(2,1)} %get-tuple-element.9.w2, bf16[8,128,256]{2,1,0:T(8,128)(2,1)} %get-tuple-element.10.w3, ...), custom_call_target="tpu_custom_call" | custom-call | tf_op jit(solution)/shard_map/solve/pallas_call | solution.py:246
  90.7 7.1 %all-to-all-start.2 = ((f32[128,4,128]{2,1,0:T(4,128)}), f32[128,4,128]{2,1,0:T(4,128)S(1)}, u32[]{:S(2)}, u32[]{:S(2)}) async-start(f32[128,4,128]{2,1,0:T(4,128)} %bitcast.52), calls=%async_computation.2 | async-start | bytes 524288 | tf_op jit(solution)/shard_map/all_to_all | solution.py:328
  97.8 1.0 constant_dynamic-slice_fusion.1
  98.8 16.5 %all-to-all-done.2 = f32[128,4,128]{2,1,0:T(4,128)S(1)} async-done(((f32[128,4,128]{2,1,0:T(4,128)}), f32[128,4,128]{2,1,0:T(4,128)S(1)}, u32[]{:S(2)}, u32[]{:S(2)}) %all-to-all-start.2) | async-done | bytes 262176 | tf_op jit(solution)/shard_map/all_to_all | solution.py:328
  115.3 0.4 fusion.8
  115.7 12.6 %all_to_all.20 = f32[32,4,128]{2,1,0:T(4,128)S(1)} all-to-all(f32[32,4,128]{2,1,0:T(4,128)S(1)} %bitcast.58), channel_id=1, replica_groups=mesh['high'=32,'low'=4,'coord'=4] {'high'}, dimensions={0} | all-to-all | bytes 131072 | tf_op jit(solution)/shard_map/all_to_all | solution.py:337
  128.2 0.8 copy-done.1
  129.0 0.6 slice_add_fusion
  129.6 0.6 slice_add_fusion.1
  (33 shorter events, 0.8 us)
Async XLA Ops:
  0.6 0.7 copy-start.2
  2.9 36.4 %copy-start = (f32[256,256]{1,0:T(8,128)S(1)}, f32[256,256]{1,0:T(8,128)}, u32[]{:S(2)}) copy-start(f32[256,256]{1,0:T(8,128)} %constant.47.clone) | copy-start | bytes 786436
  2.9 36.4 %all-to-all-start = ((f32[128,2,128]{2,1,0:T(2,128)}), f32[128,2,128]{2,1,0:T(2,128)S(1)}, u32[]{:S(2)}, u32[]{:S(2)}) async-start(f32[128,2,128]{2,1,0:T(2,128)} %select_maximum_fusion), calls=%async_computation | async-start | bytes 262144 | tf_op jit(solution)/shard_map/all_to_all | solution.py:294
  23.9 0.7 copy-start.6
  24.6 0.7 copy-start.7
  25.3 0.7 copy-start.8
  25.4 1.5 %copy-start.3 = (f32[4096]{0:T(1024)S(1)}, f32[4096]{0:T(1024)}, u32[]{:S(2)}) copy-start(f32[4096]{0:T(1024)} %param.20) | copy-start | bytes 49156
  26.0 0.7 copy-start.9
  26.9 0.7 copy-start.10
  26.9 0.7 copy-start.5
  26.9 0.7 copy-start.4
  40.6 31.2 %all-to-all-start.1 = ((f32[512,2,128]{2,1,0:T(2,128)}), f32[512,2,128]{2,1,0:T(2,128)S(1)}, u32[]{:S(2)}, u32[]{:S(2)}) async-start(f32[512,2,128]{2,1,0:T(2,128)} %bitcast.21), calls=%async_computation.1 | async-start | bytes 1048576 | tf_op jit(solution)/shard_map/all_to_all | solution.py:317
  90.7 24.6 %all-to-all-start.2 = ((f32[128,4,128]{2,1,0:T(4,128)}), f32[128,4,128]{2,1,0:T(4,128)S(1)}, u32[]{:S(2)}, u32[]{:S(2)}) async-start(f32[128,4,128]{2,1,0:T(4,128)} %bitcast.52), calls=%async_computation.2 | async-start | bytes 524288 | tf_op jit(solution)/shard_map/all_to_all | solution.py:328
  128.2 0.8 copy-start.1

commit v2 on v1

--- a/solution.py
+++ b/solution.py
@@ -27,9 +27,7 @@
     forward = wave * scale[None, :]
     weights = np.where(ids < 2, 1.0, 2.0) / steps
     inverse = (wave * weights[:, None]).T / scale[:, None]
-    inverse = inverse.reshape(steps // (2 * low), low, 1, 2, steps // 2, 1, 2).swapaxes(0, 1)
-    inverse = inverse * np.eye(2).reshape(1, 1, 2, 1, 1, 2, 1)
-    inverse = inverse.reshape(2 * steps, 2 * steps)
+    inverse = inverse.reshape(steps // (2 * low), low, 2, steps).swapaxes(0, 1).reshape(steps, steps)
     beta = math.exp(math.log(ALPHA) / steps)
     pair = np.arange(steps // 2)
     theta = 2.0 * np.pi * pair / steps
@@ -48,13 +46,47 @@
     return high, mid, (rest - mid.astype(F32)).astype(BF16)
 
 
-def bank_kernel(bank_ref, w1, w2, w3, v1, v2, v3):
+def bank_kernel(bank_ref, w1, w2, v1, v2):
     for tile in range(bank_ref.shape[0]):
-        pair, side = tile // 2, slice(tile % 2 * BLK, tile % 2 * BLK + BLK)
         value = bank_ref[tile]
-        for mat, outs in ((value, (w1, w2, w3)), (value.T, (v1, v2, v3))):
+        for mat, outs in ((value, (w1, w2)), (value.T, (v1, v2))):
             for out, piece in zip(outs, split3(mat)):
-                out[pair, :, side] = piece
+                out[tile] = piece
+
+
+def gather_kernel(state, force, mult, out, sems):
+    copies = []
+    start = 0
+    while start < out.shape[0]:
+        for src in (state, force, mult) if start == 0 else (state, force):
+            count = min(src.shape[0], out.shape[0] - start)
+            if count > 0:
+                copies.append((src.at[pl.ds(0, count)], out.at[pl.ds(start, count)]))
+                start += count
+    copies = [pltpu.make_async_copy(a, b, sems.at[i]) for i, (a, b) in enumerate(copies)]
+    for copy in copies:
+        copy.start()
+    for copy in copies:
+        copy.wait()
+
+
+def finish_kernel(cols_ref, tiles_ref, state, mult, stab, update, w1, w2, new_state, new_mult):
+    ncb, gnb = cols_ref.shape
+    new_state[...] = state[...] + update[...]
+    owner = lax.broadcasted_iota(jnp.int32, mult.shape, 0) // 2
+    total = jnp.zeros(mult.shape, F32)
+    for j in range(gnb):
+        value = jnp.concatenate(
+            [new_state[pl.ds(cols_ref[c, j] * 2, 2), :] for c in range(ncb)], axis=0
+        )
+        high, mid, _ = split3(value)
+        two = jnp.concatenate([high, mid], axis=1)
+        for c in range(ncb):
+            b1, b2 = w1[tiles_ref[c, j]], w2[tiles_ref[c, j]]
+            res = jnp.dot(two, jnp.concatenate([b1, b1]), preferred_element_type=F32)
+            res += jnp.dot(two, jnp.concatenate([b2, b2]), preferred_element_type=F32)
+            total += jnp.where(owner == c, res, 0.0)
+    new_mult[...] = mult[...] + (total - stab[...] * mult[...]) / stab[...]
 
 
 def swapped(value):
@@ -77,13 +109,14 @@
     prow = tiles * nrow
 
     def kernel(
-        fac_ref, own_ref, r_ref, w1, w2, w3, v1, v2, v3, out_ref,
+        fac_ref, own_ref, r_ref, w1, w2, v1, v2, out_ref,
         p_ref, q_ref, acc, gts, xs, rhs, e_ref, c_ref, gy, sc, istab, idxv, idxs, sem,
     ):
         a_even, a_odd, b_even, is_zero = fac_ref[0], fac_ref[1], fac_ref[2], fac_ref[3]
 
-        def part(name, rows):
-            return r_ref[lay[name] * 2 * co : lay[name] * 2 * co + rows]
+        def part(name, rows, start=0):
+            start += lay[name] * 2 * co
+            return r_ref[start : start + rows]
 
         raw = part("idx", 2 * co).astype(jnp.int32)
         lane = lax.broadcasted_iota(jnp.int32, raw.shape, 1)
@@ -106,23 +139,25 @@
         p_ref[prow : prow + 8] = jnp.zeros((8, BLK), F32)
         gts[...] = jnp.zeros(gts.shape, F32)
 
-        def products(value, mats, dst):
+        def products(value, mats, dst, beside):
             rows = value.shape[0]
             high, mid, low = split3(value)
             two = jnp.concatenate([high, mid], axis=1)
-            ends = jnp.concatenate([high, low], axis=1)
-            m1, m2, m3 = mats
+            m1, m2 = mats
             for pair in range(tiles // 2):
-                b1, b2, b3 = m1[pair], m2[pair], m3[pair]
+                b1 = jnp.concatenate([m1[2 * pair], m1[2 * pair + 1]], axis=1)
+                b2 = jnp.concatenate([m2[2 * pair], m2[2 * pair + 1]], axis=1)
                 res = jnp.dot(two, jnp.concatenate([b1, b1]), preferred_element_type=F32)
                 res += jnp.dot(two, jnp.concatenate([b2, b2]), preferred_element_type=F32)
-                res += jnp.dot(ends, jnp.concatenate([b3, b1]), preferred_element_type=F32)
+                res += jnp.dot(low, b1, preferred_element_type=F32)
                 for side in range(2):
                     start = (2 * pair + side) * rows
                     dst[start : start + rows] = res[:, side * BLK : side * BLK + BLK]
-
-        def couple():
-            for b in range(nb):
+                beside(pair)
+
+        def couple(i):
+            count = nb // (tiles // 2)
+            for b in range(i * count, (i + 1) * count):
                 for o in range(co):
                     row = (b * co + o) * 2
                     total = p_ref[pl.ds(idxs[2 * o, b * knb], 2), :]
@@ -154,61 +189,58 @@
                 total = total + gts[c]
             return total
 
-        even = lax.broadcasted_iota(jnp.int32, (nrow, BLK), 0) % 2 == 0
-        state = part("state", nrow)
+        chunk = nrow // (tiles // 2)
+        even = lax.broadcasted_iota(jnp.int32, (chunk, BLK), 0) % 2 == 0
+
+        def prepare(i):
+            start = i * chunk
+            rows = slice(start, start + chunk)
+            state = part("state", chunk, start)
+            cm = part("wrap", chunk, start)
+            mass = doubled(cm, True)
+            stiff = doubled(part("stiff", chunk, start % (nrow // 2)), start >= nrow // 2)
+            wrap = jnp.where(even, cm, is_zero * pltpu.roll(cm, 1, 0))
+            d_self = jnp.where(even, a_even, a_odd) * mass + stiff
+            d_other = jnp.where(even, a_odd, a_even) * mass + stiff
+            cross = jnp.where(even, b_even, -b_even) * mass
+            inv = 1.0 / (d_self * d_other + cross * cross)
+            e_ref[rows] = d_other * inv
+            c_ref[rows] = cross * inv
+            rhs[rows] = part("force", chunk, start) + wrap - (d_self * state + cross * swapped(state))
+
+        def precondition(res):
+            xs[...] = e_ref[...] * res - c_ref[...] * swapped(res)
+
         mult = part("mult", crow)
-        products(state, (w1, w2, w3), p_ref)
-        products(mult, (v1, v2, v3), q_ref)
-        cm = part("wrap", nrow)
-        mass = doubled(cm, True)
-        half = part("stiff", nrow // 2)
-        stiff = jnp.concatenate([doubled(half, False), doubled(half, True)], axis=0)
         shalf = part("stab", crow // 2)
         stab = jnp.concatenate([doubled(shalf, False), doubled(shalf, True)], axis=0)
-        wrap = jnp.where(even, cm, is_zero * pltpu.roll(cm, 1, 0))
-        a_self = jnp.where(even, a_even, a_odd)
-        a_other = jnp.where(even, a_odd, a_even)
-        b_self = jnp.where(even, b_even, -b_even)
-        d_self = a_self * mass + stiff
-        d_other = a_other * mass + stiff
-        cross = b_self * mass
-        inv = 1.0 / (d_self * d_other + cross * cross)
-        e_ref[...] = d_other * inv
-        c_ref[...] = cross * inv
         istab[...] = 1.0 / stab
+        products(part("state", nrow), (w1, w2), p_ref, prepare)
         copy.wait()
-        couple()
+        products(mult, (v1, v2), q_ref, couple)
         constrain()
         scatter()
-        spec = part("force", nrow) + wrap - (d_self * state + cross * swapped(state)) - coupled()
+        spec = rhs[...] - coupled()
         rhs[...] = spec
         sc[...] = stab * mult - gy[...]
-        xs[...] = e_ref[...] * spec - c_ref[...] * swapped(spec)
+        precondition(spec)
 
         def sweep(_, carry):
-            products(xs[...], (w1, w2, w3), p_ref)
+            products(xs[...], (w1, w2), p_ref, lambda i: None)
             constrain()
-            products((gy[...] - sc[...]) * istab[...], (v1, v2, v3), q_ref)
-            couple()
+            products((gy[...] - sc[...]) * istab[...], (v1, v2), q_ref, couple)
             scatter()
-            res = rhs[...] - coupled()
-            xs[...] = e_ref[...] * res - c_ref[...] * swapped(res)
+            precondition(rhs[...] - coupled())
             return carry
 
         lax.fori_loop(0, SWEEPS - 1, sweep, 0)
-        products(xs[...], (w1, w2, w3), p_ref)
-        constrain()
-        gy[...] = (gy[...] - sc[...]) * istab[...]
         own = own_ref[0]
-        parts = out_ref.shape[0] // (4 * lay["chunks"])
-        for b in range(nb + ncb):
-            src, blk = (xs, b) if b < nb else (gy, b - nb)
-            value = src[pl.ds((blk * co + own) * 2, 2), :]
+        parts = out_ref.shape[0] // (2 * nb)
+        for b in range(nb):
+            value = xs[pl.ds((b * co + own) * 2, 2), :]
             for z in range(parts):
-                row = ((b // 2) * parts + z) * 4 + b % 2 * 2
+                row = (b * parts + z) * 2
                 out_ref[row : row + 2] = value
-        used = -(-(nb + ncb) // 2) * parts * 4
-        out_ref[used:] = jnp.zeros((out_ref.shape[0] - used, BLK), F32)
 
     return kernel, [
         pltpu.VMEM((prow + 8, BLK), F32),
@@ -245,8 +277,8 @@
     kernel, scratch = make_solve(nb, ncb, co, tiles, knb, gnb, lay)
     return pl.pallas_call(
         kernel,
-        out_shape=jax.ShapeDtypeStruct((lay["chunks"] * parts * 4, BLK), F32),
-        in_specs=[SM, SM] + [VM] * 7,
+        out_shape=jax.ShapeDtypeStruct((2 * nb * parts, BLK), F32),
+        in_specs=[SM, SM] + [VM] * 5,
         out_specs=VM,
         scratch_shapes=scratch,
         name="solve",
@@ -254,10 +286,34 @@
 
 
 def bank_call(bank):
-    shape = jax.ShapeDtypeStruct((bank.shape[0] // 2, BLK, 2 * BLK), BF16)
+    shape = jax.ShapeDtypeStruct(bank.shape, BF16)
     return pl.pallas_call(
-        bank_kernel, out_shape=[shape] * 6, in_specs=[VM], out_specs=[VM] * 6, name="bank"
+        bank_kernel, out_shape=[shape] * 4, in_specs=[VM], out_specs=[VM] * 4, name="bank"
     )(bank)
+
+
+def gather_call(state, force, mult, count):
+    return pl.pallas_call(
+        gather_kernel,
+        out_shape=jax.ShapeDtypeStruct((count, 2, BLK), F32),
+        in_specs=[pl.BlockSpec(memory_space=pl.ANY)] * 3,
+        out_specs=pl.BlockSpec(memory_space=pl.ANY),
+        scratch_shapes=[pltpu.SemaphoreType.DMA((8,))],
+        name="gather",
+    )(state, force, mult)
+
+
+def finish_call(cols, tiles, state, mult, stab, update, w1, w2):
+    return pl.pallas_call(
+        finish_kernel,
+        out_shape=[
+            jax.ShapeDtypeStruct(state.shape, F32),
+            jax.ShapeDtypeStruct(mult.shape, F32),
+        ],
+        in_specs=[SM, SM] + [VM] * 6,
+        out_specs=[VM, VM],
+        name="finish",
+    )(cols, tiles, state, mult, stab, update, w1, w2)
 
 
 def index_rows(k_offsets, k_tiles, g_cols, g_tiles):
@@ -287,10 +343,7 @@
         t = lax.axis_index(group)
         o = lax.axis_index("coord")
         lay = layout(nb, ncb)
-        lay["chunks"] = high
-        st = blocks(state)
-        sent = jnp.concatenate([st, blocks(force), blocks(multiplier), st], axis=0)
-        sent = jnp.pad(sent, ((0, tm - sent.shape[0]), (0, 0), (0, 0)))
+        sent = gather_call(blocks(state), blocks(force), blocks(multiplier), tm)
         columns = lax.all_to_all(sent, group, split_axis=0, concat_axis=0, tiled=True)
         columns = columns.reshape(steps, BLK)
 
@@ -326,18 +379,30 @@
             nb, ncb, co, tiles, k_tiles.shape[1], g_tiles.shape[1], lay, low,
         )
         slots = lax.all_to_all(
-            solved.reshape(tm, 4, BLK), group, split_axis=0, concat_axis=0, tiled=True
-        ).reshape(tm * 4, BLK)
+            solved.reshape(tm, 2, BLK), group, split_axis=0, concat_axis=0, tiled=True
+        ).reshape(steps, BLK)
         table = lax.dynamic_slice_in_dim(
-            jnp.asarray(inverse), lax.axis_index("low") * (4 * high), 4 * high, axis=0
+            jnp.asarray(inverse), lax.axis_index("low") * (2 * high), 2 * high, axis=0
         )
         table = lax.optimization_barrier(table)
         rows = lax.optimization_barrier(jnp.dot(table, slots, precision=HIGHEST))
-        rows = rows.reshape(high, 4, BLK)
-        rows = lax.all_to_all(rows, "high", split_axis=0, concat_axis=0, tiled=True)
-        rows = rows.reshape(high * 2, 2, BLK)
-        update = rows[: nb + ncb].transpose(1, 0, 2).reshape(2, (nb + ncb) * BLK)
-        return state + update[:, : nb * BLK], multiplier + update[:, nb * BLK :]
+        rows = lax.all_to_all(
+            rows.reshape(high, 2, BLK), "high", split_axis=0, concat_axis=0, tiled=True
+        ).reshape(2 * nb, BLK)
+        new_state, new_mult = finish_call(
+            g_cols,
+            g_tiles,
+            blocks(state).reshape(2 * nb, BLK),
+            blocks(multiplier).reshape(2 * ncb, BLK),
+            jnp.repeat(stab.reshape(ncb, BLK), 2, axis=0),
+            pltpu.with_memory_space_constraint(rows, pltpu.VMEM),
+            *[pltpu.with_memory_space_constraint(m, pltpu.VMEM) for m in mats[:2]],
+        )
+
+        def lines(value):
+            return value.reshape(-1, 2, BLK).transpose(1, 0, 2).reshape(2, -1)
+
+        return lines(new_state), lines(new_mult)
 
     return local
 

time: 131 us -> 130 us (level)
  Pallas kernels: 22.2 us -> 26.7 us
  other arithmetic: 2.92 us -> 0.14 us
  waiting for transfers between devices: 45.3 us -> 43.9 us
    pallas_call x2 -> x4, Pallas kernels: 22.2 us -> 26.7 us  [the longest x1 16.9 us: solve_call(): pl.pallas_call(kernel, out_shape=jax.ShapeDtypeStruct((2 * nb * parts, BL...]
    all_to_all x1, waiting for transfers between devices: 16.5 us -> 14.5 us  [local(): lax.all_to_all(solved.reshape(tm, 2, BLK), group, split_axis=0, concat_ax...]
    concatenate x1 -> x0, other arithmetic: 1.55 us -> none  [local(): sent = jnp.concatenate([st, blocks(force), blocks(multiplier), st], axis=0)]
    unnamed x25, local copies, waits for them, and re-layouts: 4.68 us -> 3.25 us
  transfers between devices with their start and end apart: 3 -> 3, of which waited for: 3 -> 3; matrix products, arithmetic and copies ran while one was open for 2% -> 2% of each run, Pallas kernels for 3% -> 2%
where the time goes in v2:
time: 130 us; the launch traced here: 129 us
  waiting for transfers between devices  43.9 us (34%)
  starting transfers between devices  37.7 us (29%)
  Pallas kernels  26.7 us (21%)
  blocking collectives  11.9 us (9%)
  local copies, waits for them, and re-layouts  7.21 us (6%)
    all_to_all x1, starting transfers between devices, local(): lax.all_to_all(sent, group, split_axis=0, concat_axis=0, tiled=True)  21 us
    all_to_all x1, waiting for transfers between devices, local(): lax.all_to_all(spread, group + ('coord',), split_axis=0, concat_axis=0, t...  17.8 us
    pallas_call x1, Pallas kernels, solve_call(): pl.pallas_call(kernel, out_shape=jax.ShapeDtypeStruct((2 * nb * parts, BL...  16.9 us
    all_to_all x1, waiting for transfers between devices, local(): lax.all_to_all(solved.reshape(tm, 2, BLK), group, split_axis=0, concat_ax...  14.5 us
    all_to_all x1, blocking collectives, local(): lax.all_to_all(rows.reshape(high, 2, BLK), 'high', split_axis=0, concat_a...  11.9 us
    all_to_all x1, waiting for transfers between devices, local(): lax.all_to_all(sent, group, split_axis=0, concat_axis=0, tiled=True)  11.5 us
    all_to_all x1, starting transfers between devices, local(): lax.all_to_all(spread, group + ('coord',), split_axis=0, concat_axis=0, t...  9.4 us
    all_to_all x1, starting transfers between devices, local(): lax.all_to_all(solved.reshape(tm, 2, BLK), group, split_axis=0, concat_ax...  7.28 us
  transfers between devices with their start and end apart: 3, of which 3 were waited for; matrix products, arithmetic and copies ran while one was open for 2% of the time, Pallas kernels for 2%

profile of v2, /device:TPU:1, one launch (start us, length us, event | category | flops | bytes accessed | tf_op | source)
XLA Modules:
  0.0 128.9 jit_solution(10788433307644721157)
XLA Ops:
  0.6 5.1 %gather.1 = f32[128,2,128]{2,1,0:T(2,128)} custom-call(f32[32,2,128]{2,1,0:T(2,128)} %bitcast.71, f32[32,2,128]{2,1,0:T(2,128)} %bitcast.74, f32[4,2,128]{2,1,0:T(2,128)} %bitcast.75), custom_call_target="tpu_custom_call" | custom-call | tf_op jit(solution)/shard_map/gather/pallas_call | solution.py:296
  5.8 21.0 %all-to-all-start = ((f32[128,2,128]{2,1,0:T(2,128)}), f32[128,2,128]{2,1,0:T(2,128)S(1)}, u32[]{:S(2)}, u32[]{:S(2)}) async-start(f32[128,2,128]{2,1,0:T(2,128)} %gather.1), calls=%async_computation | async-start | bytes 262144 | tf_op jit(solution)/shard_map/all_to_all | solution.py:347
  26.8 0.7 copy-done.9
  27.6 0.1 reshape.108
  27.7 0.6 copy-done.10
  28.3 0.1 reshape.110
  28.4 0.5 copy-done.6
  29.0 0.6 copy-done.7
  29.9 0.6 copy-done.8
  30.6 11.5 %all-to-all-done = f32[128,2,128]{2,1,0:T(2,128)S(1)} async-done(((f32[128,2,128]{2,1,0:T(2,128)}), f32[128,2,128]{2,1,0:T(2,128)S(1)}, u32[]{:S(2)}, u32[]{:S(2)}) %all-to-all-start) | async-done | bytes 131104 | tf_op jit(solution)/shard_map/all_to_all | solution.py:347
  42.2 0.4 fusion.7
  42.6 0.9 broadcast_in_dim.24
  43.5 9.4 %all-to-all-start.1 = ((f32[512,2,128]{2,1,0:T(2,128)}), f32[512,2,128]{2,1,0:T(2,128)S(1)}, u32[]{:S(2)}, u32[]{:S(2)}) async-start(f32[512,2,128]{2,1,0:T(2,128)} %bitcast.27), calls=%async_computation.1 | async-start | bytes 1048576 | tf_op jit(solution)/shard_map/all_to_all | solution.py:370
  52.9 2.8 %bank.1 = (bf16[16,128,128]{2,1,0:T(8,128)(2,1)}, bf16[16,128,128]{2,1,0:T(8,128)(2,1)}, bf16[16,128,128]{2,1,0:T(8,128)(2,1)}, bf16[16,128,128]{2,1,0:T(8,128)(2,1)}) custom-call(f32[16,128,128]{2,1,0:T(8,128)} %bank_ref.1), custom_call_target="tpu_custom_call" | custom-call | tf_op jit(solution)/shard_map/bank/pallas_call | solution.py:290
  55.7 1.2 fusion.4.fac_ref
  56.9 17.8 %all-to-all-done.1 = f32[512,2,128]{2,1,0:T(2,128)S(1)} async-done(((f32[512,2,128]{2,1,0:T(2,128)}), f32[512,2,128]{2,1,0:T(2,128)S(1)}, u32[]{:S(2)}, u32[]{:S(2)}) %all-to-all-start.1) | async-done | bytes 524320 | tf_op jit(solution)/shard_map/all_to_all | solution.py:370
  74.7 16.9 %solve.1 = f32[256,128]{1,0:T(8,128)} custom-call(f32[4]{0:T(128)} %fusion.4.fac_ref, s32[1]{0:T(128)} %bitcast.9.own_ref, f32[1024,128]{1,0:T(8,128)S(1)} %bitcast.63, bf16[16,128,128]{2,1,0:T(8,128)(2,1)} %get-tuple-element.8.w1, bf16[16,128,128]{2,1,0:T(8,128)(2,1)} %get-tuple-element.9.w2, bf16[16,128,128]{2,1,0:T(8,128)(2,1)} %get-tuple-element.10.v1, ...), custom_call_target="tpu_custom_call" | custom-call | tf_op jit(solution)/shard_map/solve/pallas_call | solution.py:278
  91.7 7.3 %all-to-all-start.2 = ((f32[128,2,128]{2,1,0:T(2,128)}), f32[128,2,128]{2,1,0:T(2,128)S(1)}, u32[]{:S(2)}, u32[]{:S(2)}) async-start(f32[128,2,128]{2,1,0:T(2,128)} %bitcast.67), calls=%async_computation.2 | async-start | bytes 262144 | tf_op jit(solution)/shard_map/all_to_all | solution.py:381
  99.0 0.9 constant_dynamic-slice_fusion.1
  99.8 14.5 %all-to-all-done.2 = f32[128,2,128]{2,1,0:T(2,128)S(1)} async-done(((f32[128,2,128]{2,1,0:T(2,128)}), f32[128,2,128]{2,1,0:T(2,128)S(1)}, u32[]{:S(2)}, u32[]{:S(2)}) %all-to-all-start.2) | async-done | bytes 131104 | tf_op jit(solution)/shard_map/all_to_all | solution.py:381
  114.3 0.2 fusion.8
  114.6 11.9 %all_to_all.20 = f32[32,2,128]{2,1,0:T(2,128)S(1)} all-to-all(f32[32,2,128]{2,1,0:T(2,128)S(1)} %bitcast.73), channel_id=1, replica_groups=mesh['high'=32,'low'=4,'coord'=4] {'high'}, dimensions={0} | all-to-all | bytes 65536 | tf_op jit(solution)/shard_map/all_to_all | solution.py:389
  126.5 0.6 broadcast_in_dim.21
  127.1 1.9 %finish.1 = (f32[64,128]{1,0:T(8,128)}, f32[8,128]{1,0:T(8,128)}) custom-call(s32[4,4]{1,0:T(4,128)} %cols_ref.1, s32[4,4]{1,0:T(4,128)} %tiles_ref.1, f32[64,128]{1,0:T(8,128)} %bitcast.72, f32[8,128]{1,0:T(8,128)} %bitcast.76, f32[8,128]{1,0:T(8,128)} %bitcast.78, f32[64,128]{1,0:T(8,128)S(1)} %bitcast.64, bf16[16,128,128]{2,1,0:T(8,128)(2,1)S(1)} %copy-done, ...), custom_call_target="tpu_custom_call" | custom-call | tf_op jit(solution)/shard_map/finish/pallas_call | solution.py:307
  (32 shorter events, 0.6 us)
Async XLA Ops:
  5.8 36.4 %copy-start.2 = (f32[256,256]{1,0:T(8,128)S(1)}, f32[256,256]{1,0:T(8,128)}, u32[]{:S(2)}) copy-start(f32[256,256]{1,0:T(8,128)} %constant.46.clone) | copy-start | bytes 786436
  5.8 36.4 %all-to-all-start = ((f32[128,2,128]{2,1,0:T(2,128)}), f32[128,2,128]{2,1,0:T(2,128)S(1)}, u32[]{:S(2)}, u32[]{:S(2)}) async-start(f32[128,2,128]{2,1,0:T(2,128)} %gather.1), calls=%async_computation | async-start | bytes 262144 | tf_op jit(solution)/shard_map/all_to_all | solution.py:347
  26.8 0.7 copy-start.9
  27.6 0.7 copy-start.10
  28.3 0.7 copy-start.6
  28.3 1.5 %copy-start.3 = (f32[4096]{0:T(1024)S(1)}, f32[4096]{0:T(1024)}, u32[]{:S(2)}) copy-start(f32[4096]{0:T(1024)} %param.20) | copy-start | bytes 49156
  28.9 0.7 copy-start.7
  29.8 0.7 copy-start.8
  29.8 0.7 copy-start.5
  29.9 0.7 copy-start.4
  43.5 31.2 %all-to-all-start.1 = ((f32[512,2,128]{2,1,0:T(2,128)}), f32[512,2,128]{2,1,0:T(2,128)S(1)}, u32[]{:S(2)}, u32[]{:S(2)}) async-start(f32[512,2,128]{2,1,0:T(2,128)} %bitcast.27), calls=%async_computation.1 | async-start | bytes 1048576 | tf_op jit(solution)/shard_map/all_to_all | solution.py:370
  74.7 52.3 %copy-start.1 = (bf16[16,128,128]{2,1,0:T(8,128)(2,1)S(1)}, bf16[16,128,128]{2,1,0:T(8,128)(2,1)}, u32[]{:S(2)}) copy-start(bf16[16,128,128]{2,1,0:T(8,128)(2,1)} %get-tuple-element.9.w2) | copy-start | bytes 1572868
  91.7 35.4 %copy-start = (bf16[16,128,128]{2,1,0:T(8,128)(2,1)S(1)}, bf16[16,128,128]{2,1,0:T(8,128)(2,1)}, u32[]{:S(2)}) copy-start(bf16[16,128,128]{2,1,0:T(8,128)(2,1)} %get-tuple-element.8.w1) | copy-start | bytes 1572868
  91.7 22.7 %all-to-all-start.2 = ((f32[128,2,128]{2,1,0:T(2,128)}), f32[128,2,128]{2,1,0:T(2,128)S(1)}, u32[]{:S(2)}, u32[]{:S(2)}) async-start(f32[128,2,128]{2,1,0:T(2,128)} %bitcast.67), calls=%async_computation.2 | async-start | bytes 262144 | tf_op jit(solution)/shard_map/all_to_all | solution.py:381

commit v3 on v2

--- a/solution.py
+++ b/solution.py
@@ -1,7 +1,9 @@
+import functools
 import math
 
 import jax
 import jax.numpy as jnp
+import ml_dtypes
 import numpy as np
 from jax import lax
 from jax.experimental import pallas as pl
@@ -36,7 +38,15 @@
     a_odd = np.where(zero, 1.0 + beta, 1.0 - beta * np.cos(theta))
     b_even = np.where(zero, 0.0, -beta * np.sin(theta))
     factors = np.stack([a_even, a_odd, b_even, zero.astype(np.float64)], axis=1)
-    return forward.astype(np.float32), inverse.astype(np.float32), factors.astype(np.float32)
+    return pieces_of(forward), inverse.astype(np.float32), factors.astype(np.float32)
+
+
+def pieces_of(table):
+    rest, pieces = table.astype(np.float32), []
+    for _ in range(3):
+        pieces.append(rest.astype(ml_dtypes.bfloat16))
+        rest = rest - pieces[-1].astype(np.float32)
+    return pieces
 
 
 def split3(value):
@@ -54,20 +64,79 @@
                 out[tile] = piece
 
 
-def gather_kernel(state, force, mult, out, sems):
-    copies = []
+def gather_kernel(state, force, mult, out, sbuf, fbuf, mbuf, sin, sout):
+    ns, nm = sbuf.shape[0], mbuf.shape[0]
+    pairs = [(state, sbuf), (force, fbuf), (mult, mbuf)]
+    loads = [pltpu.make_async_copy(a, b, sin.at[i]) for i, (a, b) in enumerate(pairs)]
+    for load in loads:
+        load.start()
+    targets = [(sbuf, 0, ns), (fbuf, ns, ns), (mbuf, 2 * ns, nm), (sbuf, 2 * ns + nm, ns)]
+    end = 3 * ns + nm
+    while end < out.shape[0]:
+        count = min(ns, out.shape[0] - end)
+        targets.append((fbuf, end, count))
+        end += count
+    stores = []
+    for load, (_, buf) in zip(loads, pairs):
+        load.wait()
+        for src, start, count in targets:
+            if src is buf:
+                stores.append(
+                    pltpu.make_async_copy(
+                        buf.at[pl.ds(0, count)], out.at[pl.ds(start, count)], sout.at[len(stores)]
+                    )
+                )
+                stores[-1].start()
+    for store in stores:
+        store.wait()
+
+
+def extra_kernel(at_ref, initial, mass, stiff, stab, offs, ktiles, cols, gtiles, out, buf):
+    nb, ncb = mass.shape[0], stab.shape[0]
+    buf[...] = jnp.zeros(buf.shape, F32)
     start = 0
-    while start < out.shape[0]:
-        for src in (state, force, mult) if start == 0 else (state, force):
-            count = min(src.shape[0], out.shape[0] - start)
-            if count > 0:
-                copies.append((src.at[pl.ds(0, count)], out.at[pl.ds(start, count)]))
-                start += count
-    copies = [pltpu.make_async_copy(a, b, sems.at[i]) for i, (a, b) in enumerate(copies)]
-    for copy in copies:
-        copy.start()
-    for copy in copies:
-        copy.wait()
+    for first, second in (
+        (initial[...], mass[...]),
+        (stiff[: nb // 2], stiff[nb // 2 :]),
+        (stab[: ncb // 2], stab[ncb // 2 :]),
+        (offs[...].astype(F32), ktiles[...].astype(F32)),
+        (cols[...].astype(F32), gtiles[...].astype(F32)),
+    ):
+        count, width = first.shape
+        buf[pl.ds(start, count, stride=2), :width] = first
+        buf[pl.ds(start + 1, count, stride=2), :width] = second
+        start += 2 * count
+    out[...] = buf[pl.ds(at_ref[0], 2), :]
+
+
+def spread_kernel(at_ref, x_ref, extra, t1, t2, t3, out, *, wraps):
+    rows = x_ref.shape[0]
+    co = out.shape[0] // rows
+    at = at_ref[0]
+
+    @pl.when(at < 0)
+    def _():
+        high, mid, low = split3(x_ref[...])
+        two = jnp.concatenate([high, mid], axis=1)
+        res = jnp.dot(t2[...], two, preferred_element_type=F32)
+        low_part = jnp.dot(t3[...], high, preferred_element_type=F32)
+        low_part += jnp.dot(t1[...], low, preferred_element_type=F32)
+        res += jnp.dot(t1[...], two, preferred_element_type=F32)
+        res = res[:, :BLK] + (res[:, BLK:] + low_part)
+        for p in range(rows // 2):
+            for o in range(co):
+                row = (p * co + o) * 2
+                out[row : row + 2] = res[2 * p : 2 * p + 2]
+
+    @pl.when(at >= 0)
+    def _():
+        first, second = extra[0:1], extra[1:2]
+        wrap = second * (first - ALPHA * x_ref[rows - 1 : rows])
+        first = jnp.where(at < wraps, wrap, first)
+        even = lax.broadcasted_iota(jnp.int32, (8, BLK), 0) % 2 == 0
+        value = jnp.where(even, first, second)
+        for row in range(0, out.shape[0], 8):
+            out[row : row + 8] = value
 
 
 def finish_kernel(cols_ref, tiles_ref, state, mult, stab, update, w1, w2, new_state, new_mult):
@@ -86,7 +155,10 @@
             res = jnp.dot(two, jnp.concatenate([b1, b1]), preferred_element_type=F32)
             res += jnp.dot(two, jnp.concatenate([b2, b2]), preferred_element_type=F32)
             total += jnp.where(owner == c, res, 0.0)
-    new_mult[...] = mult[...] + (total - stab[...] * mult[...]) / stab[...]
+    weight = jnp.zeros(mult.shape, F32)
+    for c in range(ncb):
+        weight = jnp.where(owner == c, stab[c : c + 1], weight)
+    new_mult[...] = mult[...] + (total - weight * mult[...]) / weight
 
 
 def swapped(value):
@@ -107,6 +179,7 @@
     nrow = 2 * nb * co
     crow = 2 * ncb * co
     prow = tiles * nrow
+    nidx = 2 * co * (knb + ncb)
 
     def kernel(
         fac_ref, own_ref, r_ref, w1, w2, v1, v2, out_ref,
@@ -118,22 +191,20 @@
             start += lay[name] * 2 * co
             return r_ref[start : start + rows]
 
-        raw = part("idx", 2 * co).astype(jnp.int32)
+        raw = part("idx", nidx).astype(jnp.int32)
         lane = lax.broadcasted_iota(jnp.int32, raw.shape, 1)
         line = lax.broadcasted_iota(jnp.int32, raw.shape, 0)
-        coord = line // 2
-        column = jnp.where(line % 2 == 0, raw, pltpu.roll(raw, 1, 0))
-        tile = jnp.where(line % 2 == 0, pltpu.roll(raw, 2 * co - 1, 0), raw)
-        block = coord * nb + lane // knb + column - REACH
+        coord = line // 2 % co
+        column, tile = raw, pltpu.roll(raw, nidx - 1, 0)
+        block = coord * nb + lane + column - REACH
         inside = (block >= 0) & (block < nb * co)
         k_row = ((block % nb) * co + block // nb) * 2
         k_row = jnp.where(inside, tile * nrow + k_row, prow)
         g_row = (column * co + coord) * 2
-        is_k = lane < nb * knb
-        q_row = tile * crow + (((lane - nb * knb) // gnb) * co + coord) * 2
-        idxv[: 2 * co] = jnp.where(is_k, k_row, tile * nrow + g_row)
-        idxv[2 * co : 4 * co] = q_row
-        idxv[4 * co :] = g_row
+        q_row = tile * crow + line - 2 * knb * co
+        idxv[:nidx] = jnp.where(line < 2 * knb * co, k_row, tile * nrow + g_row)
+        idxv[nidx : 2 * nidx] = q_row
+        idxv[2 * nidx :] = g_row
         copy = pltpu.make_async_copy(idxv, idxs, sem)
         copy.start()
         p_ref[prow : prow + 8] = jnp.zeros((8, BLK), F32)
@@ -160,27 +231,27 @@
             for b in range(i * count, (i + 1) * count):
                 for o in range(co):
                     row = (b * co + o) * 2
-                    total = p_ref[pl.ds(idxs[2 * o, b * knb], 2), :]
+                    total = p_ref[pl.ds(idxs[2 * o, b], 2), :]
                     for k in range(1, knb):
-                        total = total + p_ref[pl.ds(idxs[2 * o, b * knb + k], 2), :]
+                        total = total + p_ref[pl.ds(idxs[2 * (k * co + o), b], 2), :]
                     acc[row : row + 2] = total
 
         def constrain():
             for c in range(ncb):
                 for o in range(co):
                     row = (c * co + o) * 2
-                    at = nb * knb + c * gnb
-                    total = p_ref[pl.ds(idxs[2 * o, at], 2), :]
+                    at = 2 * ((knb + c) * co + o)
+                    total = p_ref[pl.ds(idxs[at, 0], 2), :]
                     for j in range(1, gnb):
-                        total = total + p_ref[pl.ds(idxs[2 * o, at + j], 2), :]
+                        total = total + p_ref[pl.ds(idxs[at, j], 2), :]
                     gy[row : row + 2] = total
 
         def scatter():
             for c in range(ncb):
                 for o in range(co):
+                    at = 2 * ((knb + c) * co + o)
                     for j in range(gnb):
-                        src = idxs[2 * (co + o), nb * knb + c * gnb + j]
-                        dst = idxs[2 * (2 * co + o), nb * knb + c * gnb + j]
+                        src, dst = idxs[nidx + at, j], idxs[2 * nidx + at, j]
                         gts[c, pl.ds(dst, 2), :] = q_ref[pl.ds(src, 2), :]
 
         def coupled():
@@ -254,8 +325,8 @@
         pltpu.VMEM((crow, BLK), F32),
         pltpu.VMEM((crow, BLK), F32),
         pltpu.VMEM((crow, BLK), F32),
-        pltpu.VMEM((6 * co, BLK), jnp.int32),
-        pltpu.SMEM((6 * co, BLK), jnp.int32),
+        pltpu.VMEM((3 * nidx, BLK), jnp.int32),
+        pltpu.SMEM((3 * nidx, BLK), jnp.int32),
         pltpu.SemaphoreType.DMA(()),
     ]
 
@@ -293,14 +364,37 @@
 
 
 def gather_call(state, force, mult, count):
+    hbm = pl.BlockSpec(memory_space=pl.ANY)
     return pl.pallas_call(
         gather_kernel,
         out_shape=jax.ShapeDtypeStruct((count, 2, BLK), F32),
-        in_specs=[pl.BlockSpec(memory_space=pl.ANY)] * 3,
-        out_specs=pl.BlockSpec(memory_space=pl.ANY),
-        scratch_shapes=[pltpu.SemaphoreType.DMA((8,))],
+        in_specs=[hbm] * 3,
+        out_specs=hbm,
+        scratch_shapes=[pltpu.VMEM(v.shape, F32) for v in (state, force, mult)]
+        + [pltpu.SemaphoreType.DMA((3,)), pltpu.SemaphoreType.DMA((8,))],
         name="gather",
     )(state, force, mult)
+
+
+def extra_call(at, initial, mass, stiff, stab, offs, ktiles, cols, gtiles, rows):
+    return pl.pallas_call(
+        extra_kernel,
+        out_shape=jax.ShapeDtypeStruct((2, BLK), F32),
+        in_specs=[SM] + [VM] * 8,
+        out_specs=VM,
+        scratch_shapes=[pltpu.VMEM((rows, BLK), F32)],
+        name="extra",
+    )(at, initial, mass, stiff, stab, offs, ktiles, cols, gtiles)
+
+
+def spread_call(at, columns, extra, pieces, co, wraps):
+    return pl.pallas_call(
+        functools.partial(spread_kernel, wraps=wraps),
+        out_shape=jax.ShapeDtypeStruct((columns.shape[0] * co, BLK), F32),
+        in_specs=[SM] + [VM] * 5,
+        out_specs=VM,
+        name="spread",
+    )(at, columns, extra, *pieces)
 
 
 def finish_call(cols, tiles, state, mult, stab, update, w1, w2):
@@ -316,15 +410,8 @@
     )(cols, tiles, state, mult, stab, update, w1, w2)
 
 
-def index_rows(k_offsets, k_tiles, g_cols, g_tiles):
-    first = jnp.concatenate([k_offsets.reshape(-1), g_cols.reshape(-1)])
-    second = jnp.concatenate([k_tiles.reshape(-1), g_tiles.reshape(-1)])
-    both = jnp.pad(jnp.stack([first, second]), ((0, 0), (0, BLK - first.shape[0])))
-    return both.astype(F32)[None]
-
-
 def make_local(forward, inverse, factors, low):
-    steps = forward.shape[0]
+    steps = forward[0].shape[0]
     group = ("high", "low")
 
     def blocks(value):
@@ -345,28 +432,24 @@
         lay = layout(nb, ncb)
         sent = gather_call(blocks(state), blocks(force), blocks(multiplier), tm)
         columns = lax.all_to_all(sent, group, split_axis=0, concat_axis=0, tiled=True)
-        columns = columns.reshape(steps, BLK)
-
-        mb = mass.reshape(nb, BLK)
-        extra = jnp.concatenate(
-            [
-                jnp.stack([initial.reshape(nb, BLK), mb], axis=1),
-                stiff_diag.reshape(2, nb // 2, BLK).transpose(1, 0, 2),
-                stab.reshape(2, ncb // 2, BLK).transpose(1, 0, 2),
-                index_rows(k_offsets, k_tiles, g_cols, g_tiles),
-            ],
-            axis=0,
+        columns = pltpu.with_memory_space_constraint(columns.reshape(steps, BLK), pltpu.VMEM)
+        at = t - lay["wrap"]
+        count = 2 * (tm - lay["wrap"])
+        extra = extra_call(
+            jnp.clip(2 * at, 0, count - 2).reshape(1),
+            initial.reshape(nb, BLK),
+            mass.reshape(nb, BLK),
+            stiff_diag.reshape(nb, BLK),
+            stab.reshape(ncb, BLK),
+            k_offsets.T,
+            k_tiles.T,
+            g_cols,
+            g_tiles,
+            -(-count // 8) * 8,
         )
-        at = t - lay["wrap"]
-        extra = lax.dynamic_index_in_dim(
-            extra, jnp.clip(at, 0, extra.shape[0] - 1), 0, keepdims=False
-        )
-        is_wrap = (at >= 0) & (at < nb)
-        wrap = jnp.where(is_wrap, extra[1] * (extra[0] - ALPHA * columns[-1]), extra[0])
-        extra = jnp.stack([wrap, extra[1]])
-        spectrum = jnp.dot(forward, columns, precision=HIGHEST).reshape(tm, 2, BLK)
-        spectrum = jnp.where(at < 0, spectrum, extra[None])
-        spread = jnp.broadcast_to(spectrum[:, None], (tm, co, 2, BLK)).reshape(tm * co, 2, BLK)
+        pieces = [pltpu.with_memory_space_constraint(jnp.asarray(p), pltpu.VMEM) for p in forward]
+        spread = spread_call(at.reshape(1), columns, extra, pieces, co, nb)
+        spread = spread.reshape(tm * co, 2, BLK)
         recv = lax.all_to_all(
             spread, group + ("coord",), split_axis=0, concat_axis=0, tiled=True
         ).reshape(tm * co * 2, BLK)
@@ -394,7 +477,7 @@
             g_tiles,
             blocks(state).reshape(2 * nb, BLK),
             blocks(multiplier).reshape(2 * ncb, BLK),
-            jnp.repeat(stab.reshape(ncb, BLK), 2, axis=0),
+            stab.reshape(ncb, BLK),
             pltpu.with_memory_space_constraint(rows, pltpu.VMEM),
             *[pltpu.with_memory_space_constraint(m, pltpu.VMEM) for m in mats[:2]],
         )

time: 130 us -> 127 us (0.977)
  local copies, waits for them, and re-layouts: 7.21 us -> 2.08 us
  waiting for transfers between devices: 43.9 us -> 46.3 us
    pallas_call x1, Pallas kernels: 5.15 us -> 1.54 us  [gather_call(): pl.pallas_call(gather_kernel, out_shape=jax.ShapeDtypeStruct((count, 2, B...]
    unnamed x25 -> x10, local copies, waits for them, and re-layouts: 3.25 us -> 0.03 us
    pallas_call x0 -> x2, Pallas kernels: none -> 3.18 us  [the longest x1 1.81 us: spread_call(): pl.pallas_call(functools.partial(spread_kernel, wraps=wraps), out_shape=j...]
    all_to_all x1, waiting for transfers between devices: 11.5 us -> 14 us  [local(): lax.all_to_all(sent, group, split_axis=0, concat_axis=0, tiled=True)]
    broadcast_in_dim x2 -> x0, local copies, waits for them, and re-layouts: 1.52 us -> none  [the longest x1 0.93 us: local(): jnp.broadcast_to(spectrum[:, None], (tm, co, 2, BLK))]
  transfers between devices with their start and end apart: 3 -> 3, of which waited for: 3 -> 3; matrix products, arithmetic and copies ran while one was open for 2% -> 2% of each run, Pallas kernels for 2% -> 3%
where the time goes in v3:
time: 127 us; the launch traced here: 126 us
  waiting for transfers between devices  46.3 us (36%)
  starting transfers between devices  37.6 us (30%)
  Pallas kernels  27.5 us (22%)
  blocking collectives  11.9 us (9%)
  local copies, waits for them, and re-layouts  2.08 us (2%)
    all_to_all x1, starting transfers between devices, local(): lax.all_to_all(sent, group, split_axis=0, concat_axis=0, tiled=True)  21 us
    pallas_call x1, Pallas kernels, solve_call(): pl.pallas_call(kernel, out_shape=jax.ShapeDtypeStruct((2 * nb * parts, BL...  18.2 us
    all_to_all x1, waiting for transfers between devices, local(): lax.all_to_all(spread, group + ('coord',), split_axis=0, concat_axis=0, t...  17.9 us
    all_to_all x1, waiting for transfers between devices, local(): lax.all_to_all(solved.reshape(tm, 2, BLK), group, split_axis=0, concat_ax...  14.5 us
    all_to_all x1, waiting for transfers between devices, local(): lax.all_to_all(sent, group, split_axis=0, concat_axis=0, tiled=True)  14 us
    all_to_all x1, blocking collectives, local(): lax.all_to_all(rows.reshape(high, 2, BLK), 'high', split_axis=0, concat_a...  11.9 us
    all_to_all x1, starting transfers between devices, local(): lax.all_to_all(spread, group + ('coord',), split_axis=0, concat_axis=0, t...  9.39 us
    all_to_all x1, starting transfers between devices, local(): lax.all_to_all(solved.reshape(tm, 2, BLK), group, split_axis=0, concat_ax...  7.25 us
  transfers between devices with their start and end apart: 3, of which 3 were waited for; matrix products, arithmetic and copies ran while one was open for 2% of the time, Pallas kernels for 3%

profile of v3, /device:TPU:1, one launch (start us, length us, event | category | flops | bytes accessed | tf_op | source)
XLA Modules:
  0.0 126.5 jit_solution(18178262622947077620)
XLA Ops:
  0.6 0.0 copy-start.4
  0.6 1.5 %gather.1 = f32[128,2,128]{2,1,0:T(2,128)} custom-call(f32[32,2,128]{2,1,0:T(2,128)} %bitcast.49, f32[32,2,128]{2,1,0:T(2,128)} %bitcast.52, f32[4,2,128]{2,1,0:T(2,128)} %bitcast.53), custom_call_target="tpu_custom_call" | custom-call | tf_op jit(solution)/shard_map/gather/pallas_call | solution.py:368
  2.2 0.0 copy-start.2
  2.2 0.0 copy-start.3
  2.2 21.0 %all-to-all-start = ((f32[128,2,128]{2,1,0:T(2,128)}), f32[128,2,128]{2,1,0:T(2,128)S(1)}, u32[]{:S(2)}, u32[]{:S(2)}) async-start(f32[128,2,128]{2,1,0:T(2,128)} %gather.1), calls=%async_computation | async-start | bytes 262144 | tf_op jit(solution)/shard_map/all_to_all | solution.py:434
  23.2 1.4 %extra.1 = f32[2,128]{1,0:T(2,128)} custom-call(s32[1]{0:T(128)} %bitcast.15.at_ref, f32[32,128]{1,0:T(8,128)} %bitcast.55, f32[32,128]{1,0:T(8,128)} %bitcast.56, f32[32,128]{1,0:T(8,128)} %bitcast.57, f32[4,128]{1,0:T(4,128)} %bitcast.58, s32[3,32]{1,0:T(4,128)} %bitcast.60, s32[3,32]{1,0:T(4,128)} %bitcast.61, s32[4,4]{1,0:T(4,128)} %cols_ref.1, ...), custom_call_target="tpu_custom_call" | custom-call | tf_op jit(solution)/shard_map/extra/pallas_call | solution.py:380
  24.6 14.0 %all-to-all-done = f32[128,2,128]{2,1,0:T(2,128)S(1)} async-done(((f32[128,2,128]{2,1,0:T(2,128)}), f32[128,2,128]{2,1,0:T(2,128)S(1)}, u32[]{:S(2)}, u32[]{:S(2)}) %all-to-all-start) | async-done | bytes 131104 | tf_op jit(solution)/shard_map/all_to_all | solution.py:434
  38.6 0.0 copy-done.4
  38.6 0.0 copy-done.2
  38.6 0.0 copy-done.3
  38.6 1.8 %spread.1 = f32[1024,128]{1,0:T(8,128)} custom-call(s32[1]{0:T(128)} %bitcast.9.at_ref, f32[256,128]{1,0:T(8,128)S(1)} %bitcast.44, f32[2,128]{1,0:T(2,128)} %extra.1, bf16[256,256]{1,0:T(8,128)(2,1)S(1)} %copy-done.2, bf16[256,256]{1,0:T(8,128)(2,1)S(1)} %copy-done.3, bf16[256,256]{1,0:T(8,128)(2,1)S(1)} %copy-done.4), custom_call_target="tpu_custom_call" | custom-call | tf_op jit(solution)/shard_map/spread/pallas_call | solution.py:391
  40.4 9.4 %all-to-all-start.1 = ((f32[512,2,128]{2,1,0:T(2,128)}), f32[512,2,128]{2,1,0:T(2,128)S(1)}, u32[]{:S(2)}, u32[]{:S(2)}) async-start(f32[512,2,128]{2,1,0:T(2,128)} %bitcast.46), calls=%async_computation.1 | async-start | bytes 1048576 | tf_op jit(solution)/shard_map/all_to_all | solution.py:453
  49.8 2.8 %bank.1 = (bf16[16,128,128]{2,1,0:T(8,128)(2,1)}, bf16[16,128,128]{2,1,0:T(8,128)(2,1)}, bf16[16,128,128]{2,1,0:T(8,128)(2,1)}, bf16[16,128,128]{2,1,0:T(8,128)(2,1)}) custom-call(f32[16,128,128]{2,1,0:T(8,128)} %bank_ref.1), custom_call_target="tpu_custom_call" | custom-call | tf_op jit(solution)/shard_map/bank/pallas_call | solution.py:361
  52.6 1.2 dynamic-slice_bitcast_fusion.fac_ref
  53.8 17.9 %all-to-all-done.1 = f32[512,2,128]{2,1,0:T(2,128)S(1)} async-done(((f32[512,2,128]{2,1,0:T(2,128)}), f32[512,2,128]{2,1,0:T(2,128)S(1)}, u32[]{:S(2)}, u32[]{:S(2)}) %all-to-all-start.1) | async-done | bytes 524320 | tf_op jit(solution)/shard_map/all_to_all | solution.py:453
  71.6 18.2 %solve.1 = f32[256,128]{1,0:T(8,128)} custom-call(f32[4]{0:T(128)} %dynamic-slice_bitcast_fusion.fac_ref, s32[1]{0:T(128)} %bitcast.8.own_ref, f32[1024,128]{1,0:T(8,128)S(1)} %bitcast.43, bf16[16,128,128]{2,1,0:T(8,128)(2,1)} %get-tuple-element.8.w1, bf16[16,128,128]{2,1,0:T(8,128)(2,1)} %get-tuple-element.9.w2, ...), custom_call_target="tpu_custom_call" | custom-call | tf_op jit(solution)/shard_map/solve/pallas_call | solution.py:349
  89.8 0.0 copy-start
  89.8 7.3 %all-to-all-start.2 = ((f32[128,2,128]{2,1,0:T(2,128)}), f32[128,2,128]{2,1,0:T(2,128)S(1)}, u32[]{:S(2)}, u32[]{:S(2)}) async-start(f32[128,2,128]{2,1,0:T(2,128)} %bitcast.47), calls=%async_computation.2 | async-start | bytes 262144 | tf_op jit(solution)/shard_map/all_to_all | solution.py:464
  97.1 0.9 constant_dynamic-slice_fusion
  97.9 14.5 %all-to-all-done.2 = f32[128,2,128]{2,1,0:T(2,128)S(1)} async-done(((f32[128,2,128]{2,1,0:T(2,128)}), f32[128,2,128]{2,1,0:T(2,128)S(1)}, u32[]{:S(2)}, u32[]{:S(2)}) %all-to-all-start.2) | async-done | bytes 131104 | tf_op jit(solution)/shard_map/all_to_all | solution.py:464
  112.4 0.2 fusion
  112.7 11.9 %all_to_all.20 = f32[32,2,128]{2,1,0:T(2,128)S(1)} all-to-all(f32[32,2,128]{2,1,0:T(2,128)S(1)} %bitcast.51), channel_id=1, replica_groups=mesh['high'=32,'low'=4,'coord'=4] {'high'}, dimensions={0} | all-to-all | bytes 65536 | tf_op jit(solution)/shard_map/all_to_all | solution.py:472
  124.6 0.0 copy-done.1
  124.6 1.9 %finish.1 = (f32[64,128]{1,0:T(8,128)}, f32[8,128]{1,0:T(8,128)}) custom-call(s32[4,4]{1,0:T(4,128)} %cols_ref.1, s32[4,4]{1,0:T(4,128)} %tiles_ref.1, f32[64,128]{1,0:T(8,128)} %bitcast.50, f32[8,128]{1,0:T(8,128)} %bitcast.54, f32[4,128]{1,0:T(4,128)} %bitcast.59, f32[64,128]{1,0:T(8,128)S(1)} %bitcast.45, bf16[16,128,128]{2,1,0:T(8,128)(2,1)S(1)} %copy-done, ...), custom_call_target="tpu_custom_call" | custom-call | tf_op jit(solution)/shard_map/finish/pallas_call | solution.py:401
  (2 shorter events, 0.0 us)
Async XLA Ops:
  0.6 38.0 %copy-start.4 = (bf16[256,256]{1,0:T(8,128)(2,1)S(1)}, bf16[256,256]{1,0:T(8,128)(2,1)}, u32[]{:S(2)}) copy-start(bf16[256,256]{1,0:T(8,128)(2,1)} %constant.45.clone.t3) | copy-start | bytes 393220
  2.2 36.4 %copy-start.2 = (bf16[256,256]{1,0:T(8,128)(2,1)S(1)}, bf16[256,256]{1,0:T(8,128)(2,1)}, u32[]{:S(2)}) copy-start(bf16[256,256]{1,0:T(8,128)(2,1)} %constant.43.clone.t1) | copy-start | bytes 393220
  2.2 36.4 %copy-start.3 = (bf16[256,256]{1,0:T(8,128)(2,1)S(1)}, bf16[256,256]{1,0:T(8,128)(2,1)}, u32[]{:S(2)}) copy-start(bf16[256,256]{1,0:T(8,128)(2,1)} %constant.44.clone.t2) | copy-start | bytes 393220
  2.2 36.4 %all-to-all-start = ((f32[128,2,128]{2,1,0:T(2,128)}), f32[128,2,128]{2,1,0:T(2,128)S(1)}, u32[]{:S(2)}, u32[]{:S(2)}) async-start(f32[128,2,128]{2,1,0:T(2,128)} %gather.1), calls=%async_computation | async-start | bytes 262144 | tf_op jit(solution)/shard_map/all_to_all | solution.py:434
  40.4 31.2 %all-to-all-start.1 = ((f32[512,2,128]{2,1,0:T(2,128)}), f32[512,2,128]{2,1,0:T(2,128)S(1)}, u32[]{:S(2)}, u32[]{:S(2)}) async-start(f32[512,2,128]{2,1,0:T(2,128)} %bitcast.46), calls=%async_computation.1 | async-start | bytes 1048576 | tf_op jit(solution)/shard_map/all_to_all | solution.py:453
  71.6 53.0 %copy-start.1 = (bf16[16,128,128]{2,1,0:T(8,128)(2,1)S(1)}, bf16[16,128,128]{2,1,0:T(8,128)(2,1)}, u32[]{:S(2)}) copy-start(bf16[16,128,128]{2,1,0:T(8,128)(2,1)} %get-tuple-element.9.w2) | copy-start | bytes 1572868
  89.8 34.8 %copy-start = (bf16[16,128,128]{2,1,0:T(8,128)(2,1)S(1)}, bf16[16,128,128]{2,1,0:T(8,128)(2,1)}, u32[]{:S(2)}) copy-start(bf16[16,128,128]{2,1,0:T(8,128)(2,1)} %get-tuple-element.8.w1) | copy-start | bytes 1572868
  89.8 22.6 %all-to-all-start.2 = ((f32[128,2,128]{2,1,0:T(2,128)}), f32[128,2,128]{2,1,0:T(2,128)S(1)}, u32[]{:S(2)}, u32[]{:S(2)}) async-start(f32[128,2,128]{2,1,0:T(2,128)} %bitcast.47), calls=%async_computation.2 | async-start | bytes 262144 | tf_op jit(solution)/shard_map/all_to_all | solution.py:464

commit v4 on v3

--- a/solution.py
+++ b/solution.py
@@ -109,9 +109,8 @@
     out[...] = buf[pl.ds(at_ref[0], 2), :]
 
 
-def spread_kernel(at_ref, x_ref, extra, t1, t2, t3, out, *, wraps):
+def spread_kernel(at_ref, x_ref, extra, t1, t2, t3, out, buf, sems, *, wraps):
     rows = x_ref.shape[0]
-    co = out.shape[0] // rows
     at = at_ref[0]
 
     @pl.when(at < 0)
@@ -123,20 +122,23 @@
         low_part += jnp.dot(t1[...], low, preferred_element_type=F32)
         res += jnp.dot(t1[...], two, preferred_element_type=F32)
         res = res[:, :BLK] + (res[:, BLK:] + low_part)
-        for p in range(rows // 2):
-            for o in range(co):
-                row = (p * co + o) * 2
-                out[row : row + 2] = res[2 * p : 2 * p + 2]
+        buf[...] = res.reshape(buf.shape)
 
     @pl.when(at >= 0)
     def _():
         first, second = extra[0:1], extra[1:2]
         wrap = second * (first - ALPHA * x_ref[rows - 1 : rows])
         first = jnp.where(at < wraps, wrap, first)
-        even = lax.broadcasted_iota(jnp.int32, (8, BLK), 0) % 2 == 0
-        value = jnp.where(even, first, second)
-        for row in range(0, out.shape[0], 8):
-            out[row : row + 8] = value
+        even = lax.broadcasted_iota(jnp.int32, (2, BLK), 0) == 0
+        buf[...] = jnp.broadcast_to(jnp.where(even, first, second)[None], buf.shape)
+
+    copies = [
+        pltpu.make_async_copy(buf, out.at[:, o], sems.at[o]) for o in range(out.shape[1])
+    ]
+    for copy in copies:
+        copy.start()
+    for copy in copies:
+        copy.wait()
 
 
 def finish_kernel(cols_ref, tiles_ref, state, mult, stab, update, w1, w2, new_state, new_mult):
@@ -183,7 +185,7 @@
 
     def kernel(
         fac_ref, own_ref, r_ref, w1, w2, v1, v2, out_ref,
-        p_ref, q_ref, acc, gts, xs, rhs, e_ref, c_ref, gy, sc, istab, idxv, idxs, sem,
+        p_ref, q_ref, acc, gts, xs, rhs, e_ref, c_ref, xt, xl, gy, sc, istab, wide, idxv, idxs, sem,
     ):
         a_even, a_odd, b_even, is_zero = fac_ref[0], fac_ref[1], fac_ref[2], fac_ref[3]
 
@@ -194,33 +196,35 @@
         raw = part("idx", nidx).astype(jnp.int32)
         lane = lax.broadcasted_iota(jnp.int32, raw.shape, 1)
         line = lax.broadcasted_iota(jnp.int32, raw.shape, 0)
-        coord = line // 2 % co
+        coord = (line >> 1) & (co - 1)
         column, tile = raw, pltpu.roll(raw, nidx - 1, 0)
         block = coord * nb + lane + column - REACH
         inside = (block >= 0) & (block < nb * co)
-        k_row = ((block % nb) * co + block // nb) * 2
+        k_row = ((block & (nb - 1)) * co + (block >> (nb.bit_length() - 1))) * 2
         k_row = jnp.where(inside, tile * nrow + k_row, prow)
         g_row = (column * co + coord) * 2
         q_row = tile * crow + line - 2 * knb * co
-        idxv[:nidx] = jnp.where(line < 2 * knb * co, k_row, tile * nrow + g_row)
-        idxv[nidx : 2 * nidx] = q_row
-        idxv[2 * nidx :] = g_row
+        q_row = pltpu.roll(q_row, gnb, 1)
+        g_rows = jnp.where(lane < gnb, tile * nrow + g_row, pltpu.roll(g_row, 2 * gnb, 1))
+        g_rows = jnp.where((lane >= gnb) & (lane < 2 * gnb), q_row, g_rows)
+        wide[...] = jnp.where(line < 2 * knb * co, k_row, g_rows)
+        idxv[...] = jnp.zeros(idxv.shape, jnp.int32)
+        idxv[: nidx // 2] = wide[pl.ds(0, nidx // 2, stride=2), :]
         copy = pltpu.make_async_copy(idxv, idxs, sem)
         copy.start()
         p_ref[prow : prow + 8] = jnp.zeros((8, BLK), F32)
         gts[...] = jnp.zeros(gts.shape, F32)
 
-        def products(value, mats, dst, beside):
-            rows = value.shape[0]
-            high, mid, low = split3(value)
-            two = jnp.concatenate([high, mid], axis=1)
+        def products(x1, x2, x3, mats, dst, beside):
+            rows = x1.shape[0]
+            pairs = ((x1, x1), (x2, x2), (x3, jnp.zeros_like(x3)))
+            stack = jnp.concatenate([jnp.concatenate(p, axis=1) for p in pairs], axis=0)
             m1, m2 = mats
             for pair in range(tiles // 2):
                 b1 = jnp.concatenate([m1[2 * pair], m1[2 * pair + 1]], axis=1)
                 b2 = jnp.concatenate([m2[2 * pair], m2[2 * pair + 1]], axis=1)
-                res = jnp.dot(two, jnp.concatenate([b1, b1]), preferred_element_type=F32)
-                res += jnp.dot(two, jnp.concatenate([b2, b2]), preferred_element_type=F32)
-                res += jnp.dot(low, b1, preferred_element_type=F32)
+                res = jnp.dot(stack, jnp.concatenate([b1, b2]), preferred_element_type=F32)
+                res = res[:rows] + (res[rows : 2 * rows] + res[2 * rows :])
                 for side in range(2):
                     start = (2 * pair + side) * rows
                     dst[start : start + rows] = res[:, side * BLK : side * BLK + BLK]
@@ -231,16 +235,16 @@
             for b in range(i * count, (i + 1) * count):
                 for o in range(co):
                     row = (b * co + o) * 2
-                    total = p_ref[pl.ds(idxs[2 * o, b], 2), :]
+                    total = p_ref[pl.ds(idxs[o, b], 2), :]
                     for k in range(1, knb):
-                        total = total + p_ref[pl.ds(idxs[2 * (k * co + o), b], 2), :]
+                        total = total + p_ref[pl.ds(idxs[k * co + o, b], 2), :]
                     acc[row : row + 2] = total
 
         def constrain():
             for c in range(ncb):
                 for o in range(co):
                     row = (c * co + o) * 2
-                    at = 2 * ((knb + c) * co + o)
+                    at = (knb + c) * co + o
                     total = p_ref[pl.ds(idxs[at, 0], 2), :]
                     for j in range(1, gnb):
                         total = total + p_ref[pl.ds(idxs[at, j], 2), :]
@@ -249,15 +253,15 @@
         def scatter():
             for c in range(ncb):
                 for o in range(co):
-                    at = 2 * ((knb + c) * co + o)
+                    at = (knb + c) * co + o
                     for j in range(gnb):
-                        src, dst = idxs[nidx + at, j], idxs[2 * nidx + at, j]
+                        src, dst = idxs[at, gnb + j], idxs[at, 2 * gnb + j]
                         gts[c, pl.ds(dst, 2), :] = q_ref[pl.ds(src, 2), :]
 
-        def coupled():
-            total = acc[...]
+        def coupled(rows):
+            total = acc[rows]
             for c in range(ncb):
-                total = total + gts[c]
+                total = total + gts[c, rows]
             return total
 
         chunk = nrow // (tiles // 2)
@@ -279,29 +283,39 @@
             c_ref[rows] = cross * inv
             rhs[rows] = part("force", chunk, start) + wrap - (d_self * state + cross * swapped(state))
 
-        def precondition(res):
-            xs[...] = e_ref[...] * res - c_ref[...] * swapped(res)
+        def advance(first):
+            for i in range(nrow // chunk):
+                rows = slice(i * chunk, i * chunk + chunk)
+                res = rhs[rows] - coupled(rows)
+                if first:
+                    rhs[rows] = res
+                value = e_ref[rows] * res - c_ref[rows] * swapped(res)
+                xs[rows] = value
+                xt[rows, :BLK], xt[rows, BLK:], xl[rows] = split3(value)
 
         mult = part("mult", crow)
         shalf = part("stab", crow // 2)
         stab = jnp.concatenate([doubled(shalf, False), doubled(shalf, True)], axis=0)
         istab[...] = 1.0 / stab
-        products(part("state", nrow), (w1, w2), p_ref, prepare)
+        products(*split3(part("state", nrow)), (w1, w2), p_ref, lambda i: None)
         copy.wait()
-        products(mult, (v1, v2), q_ref, couple)
+
+        def both(i):
+            prepare(i)
+            couple(i)
+
+        products(*split3(mult), (v1, v2), q_ref, both)
         constrain()
         scatter()
-        spec = rhs[...] - coupled()
-        rhs[...] = spec
         sc[...] = stab * mult - gy[...]
-        precondition(spec)
+        advance(True)
 
         def sweep(_, carry):
-            products(xs[...], (w1, w2), p_ref, lambda i: None)
+            products(xt[:, :BLK], xt[:, BLK:], xl[...], (w1, w2), p_ref, lambda i: None)
             constrain()
-            products((gy[...] - sc[...]) * istab[...], (v1, v2), q_ref, couple)
+            products(*split3((gy[...] - sc[...]) * istab[...]), (v1, v2), q_ref, couple)
             scatter()
-            precondition(rhs[...] - coupled())
+            advance(False)
             return carry
 
         lax.fori_loop(0, SWEEPS - 1, sweep, 0)
@@ -322,11 +336,14 @@
         pltpu.VMEM((nrow, BLK), F32),
         pltpu.VMEM((nrow, BLK), F32),
         pltpu.VMEM((nrow, BLK), F32),
+        pltpu.VMEM((nrow, 2 * BLK), BF16),
+        pltpu.VMEM((nrow, BLK), BF16),
         pltpu.VMEM((crow, BLK), F32),
         pltpu.VMEM((crow, BLK), F32),
         pltpu.VMEM((crow, BLK), F32),
-        pltpu.VMEM((3 * nidx, BLK), jnp.int32),
-        pltpu.SMEM((3 * nidx, BLK), jnp.int32),
+        pltpu.VMEM((nidx, BLK), jnp.int32),
+        pltpu.VMEM((-(-nidx // 16) * 8, BLK), jnp.int32),
+        pltpu.SMEM((-(-nidx // 16) * 8, BLK), jnp.int32),
         pltpu.SemaphoreType.DMA(()),
     ]
 
@@ -390,9 +407,13 @@
 def spread_call(at, columns, extra, pieces, co, wraps):
     return pl.pallas_call(
         functools.partial(spread_kernel, wraps=wraps),
-        out_shape=jax.ShapeDtypeStruct((columns.shape[0] * co, BLK), F32),
+        out_shape=jax.ShapeDtypeStruct((columns.shape[0] // 2, co, 2, BLK), F32),
         in_specs=[SM] + [VM] * 5,
-        out_specs=VM,
+        out_specs=pl.BlockSpec(memory_space=pl.ANY),
+        scratch_shapes=[
+            pltpu.VMEM((columns.shape[0] // 2, 2, BLK), F32),
+            pltpu.SemaphoreType.DMA((co,)),
+        ],
         name="spread",
     )(at, columns, extra, *pieces)
 
@@ -475,9 +496,9 @@
         new_state, new_mult = finish_call(
             g_cols,
             g_tiles,
-            blocks(state).reshape(2 * nb, BLK),
-            blocks(multiplier).reshape(2 * ncb, BLK),
-            stab.reshape(ncb, BLK),
+            pltpu.with_memory_space_constraint(blocks(state).reshape(2 * nb, BLK), pltpu.VMEM),
+            pltpu.with_memory_space_constraint(blocks(multiplier).reshape(2 * ncb, BLK), pltpu.VMEM),
+            pltpu.with_memory_space_constraint(stab.reshape(ncb, BLK), pltpu.VMEM),
             pltpu.with_memory_space_constraint(rows, pltpu.VMEM),
             *[pltpu.with_memory_space_constraint(m, pltpu.VMEM) for m in mats[:2]],
         )

time: 127 us -> 125 us (0.984)
  Pallas kernels: 27.5 us -> 24.5 us
    pallas_call x1, Pallas kernels: 18.2 us -> 15.2 us  [solve_call(): pl.pallas_call(kernel, out_shape=jax.ShapeDtypeStruct((2 * nb * parts, BL...]
where the time goes in v4:
time: 125 us; the launch traced here: 124 us
  waiting for transfers between devices  46.3 us (37%)
  starting transfers between devices  37.6 us (30%)
  Pallas kernels  24.5 us (20%)
  blocking collectives  12 us (10%)
  local copies, waits for them, and re-layouts  2.76 us (2%)
    all_to_all x1, starting transfers between devices, local(): lax.all_to_all(sent, group, split_axis=0, concat_axis=0, tiled=True)  21 us
    all_to_all x1, waiting for transfers between devices, local(): lax.all_to_all(spread, group + ('coord',), split_axis=0, concat_axis=0, t...  17.8 us
    pallas_call x1, Pallas kernels, solve_call(): pl.pallas_call(kernel, out_shape=jax.ShapeDtypeStruct((2 * nb * parts, BL...  15.2 us
    all_to_all x1, waiting for transfers between devices, local(): lax.all_to_all(solved.reshape(tm, 2, BLK), group, split_axis=0, concat_ax...  14.5 us
    all_to_all x1, waiting for transfers between devices, local(): lax.all_to_all(sent, group, split_axis=0, concat_axis=0, tiled=True)  14 us
    all_to_all x1, blocking collectives, local(): lax.all_to_all(rows.reshape(high, 2, BLK), 'high', split_axis=0, concat_a...  12 us
    all_to_all x1, starting transfers between devices, local(): lax.all_to_all(spread, group + ('coord',), split_axis=0, concat_axis=0, t...  9.33 us
    all_to_all x1, starting transfers between devices, local(): lax.all_to_all(solved.reshape(tm, 2, BLK), group, split_axis=0, concat_ax...  7.27 us
  transfers between devices with their start and end apart: 3, of which 3 were waited for; matrix products, arithmetic and copies ran while one was open for 2% of the time, Pallas kernels for 3%

profile of v4, /device:TPU:1, one launch (start us, length us, event | category | flops | bytes accessed | tf_op | source)
XLA Modules:
  0.0 124.1 jit_solution(14287356896570745023)
XLA Ops:
  0.6 0.0 copy-start.4
  0.6 1.6 %gather.1 = f32[128,2,128]{2,1,0:T(2,128)} custom-call(f32[32,2,128]{2,1,0:T(2,128)} %bitcast.45, f32[32,2,128]{2,1,0:T(2,128)} %bitcast.56, f32[4,2,128]{2,1,0:T(2,128)} %bitcast.48), custom_call_target="tpu_custom_call" | custom-call | tf_op jit(solution)/shard_map/gather/pallas_call | solution.py:385
  2.2 0.0 copy-start.2
  2.2 0.0 copy-start.3
  2.2 21.0 %all-to-all-start = ((f32[128,2,128]{2,1,0:T(2,128)}), f32[128,2,128]{2,1,0:T(2,128)S(1)}, u32[]{:S(2)}, u32[]{:S(2)}) async-start(f32[128,2,128]{2,1,0:T(2,128)} %gather.1), calls=%async_computation | async-start | bytes 262144 | tf_op jit(solution)/shard_map/all_to_all | solution.py:455
  23.2 1.4 %extra.1 = f32[2,128]{1,0:T(2,128)} custom-call(s32[1]{0:T(128)} %bitcast.15.at_ref, f32[32,128]{1,0:T(8,128)} %bitcast.57, f32[32,128]{1,0:T(8,128)} %bitcast.58, f32[32,128]{1,0:T(8,128)} %bitcast.59, f32[4,128]{1,0:T(4,128)} %bitcast.50, s32[3,32]{1,0:T(4,128)} %bitcast.60, s32[3,32]{1,0:T(4,128)} %bitcast.61, s32[4,4]{1,0:T(4,128)} %cols_ref.1, ...), custom_call_target="tpu_custom_call" | custom-call | tf_op jit(solution)/shard_map/extra/pallas_call | solution.py:397
  24.6 14.0 %all-to-all-done = f32[128,2,128]{2,1,0:T(2,128)S(1)} async-done(((f32[128,2,128]{2,1,0:T(2,128)}), f32[128,2,128]{2,1,0:T(2,128)S(1)}, u32[]{:S(2)}, u32[]{:S(2)}) %all-to-all-start) | async-done | bytes 131104 | tf_op jit(solution)/shard_map/all_to_all | solution.py:455
  38.6 0.0 copy-done.4
  38.6 1.8 %spread.1 = f32[128,4,2,128]{3,2,1,0:T(2,128)} custom-call(s32[1]{0:T(128)} %bitcast.9.at_ref, f32[256,128]{1,0:T(8,128)S(1)} %bitcast.44, f32[2,128]{1,0:T(2,128)} %extra.1, bf16[256,256]{1,0:T(8,128)(2,1)S(1)} %copy-done.2, bf16[256,256]{1,0:T(8,128)(2,1)S(1)} %copy-done.3, bf16[256,256]{1,0:T(8,128)(2,1)S(1)} %copy-done.4), custom_call_target="tpu_custom_call" | custom-call | tf_op jit(solution)/shard_map/spread/pallas_call | solution.py:408
  40.4 9.3 %all-to-all-start.1 = ((f32[512,2,128]{2,1,0:T(2,128)}), f32[512,2,128]{2,1,0:T(2,128)S(1)}, u32[]{:S(2)}, u32[]{:S(2)}) async-start(f32[512,2,128]{2,1,0:T(2,128)} %bitcast.52), calls=%async_computation.1 | async-start | bytes 1048576 | tf_op jit(solution)/shard_map/all_to_all | solution.py:474
  49.8 2.8 %bank.1 = (bf16[16,128,128]{2,1,0:T(8,128)(2,1)}, bf16[16,128,128]{2,1,0:T(8,128)(2,1)}, bf16[16,128,128]{2,1,0:T(8,128)(2,1)}, bf16[16,128,128]{2,1,0:T(8,128)(2,1)}) custom-call(f32[16,128,128]{2,1,0:T(8,128)} %bank_ref.1), custom_call_target="tpu_custom_call" | custom-call | tf_op jit(solution)/shard_map/bank/pallas_call | solution.py:378
  52.5 1.2 dynamic-slice_bitcast_fusion.fac_ref
  53.8 17.8 %all-to-all-done.1 = f32[512,2,128]{2,1,0:T(2,128)S(1)} async-done(((f32[512,2,128]{2,1,0:T(2,128)}), f32[512,2,128]{2,1,0:T(2,128)S(1)}, u32[]{:S(2)}, u32[]{:S(2)}) %all-to-all-start.1) | async-done | bytes 524320 | tf_op jit(solution)/shard_map/all_to_all | solution.py:474
  71.6 15.2 %solve.1 = f32[256,128]{1,0:T(8,128)} custom-call(f32[4]{0:T(128)} %dynamic-slice_bitcast_fusion.fac_ref, s32[1]{0:T(128)} %bitcast.8.own_ref, f32[1024,128]{1,0:T(8,128)S(1)} %bitcast.43, bf16[16,128,128]{2,1,0:T(8,128)(2,1)} %get-tuple-element.8.w1, bf16[16,128,128]{2,1,0:T(8,128)(2,1)} %get-tuple-element.9.w2, ...), custom_call_target="tpu_custom_call" | custom-call | tf_op jit(solution)/shard_map/solve/pallas_call | solution.py:366
  86.8 7.3 %all-to-all-start.2 = ((f32[128,2,128]{2,1,0:T(2,128)}), f32[128,2,128]{2,1,0:T(2,128)S(1)}, u32[]{:S(2)}, u32[]{:S(2)}) async-start(f32[128,2,128]{2,1,0:T(2,128)} %bitcast.53), calls=%async_computation.2 | async-start | bytes 262144 | tf_op jit(solution)/shard_map/all_to_all | solution.py:485
  94.1 0.9 constant_dynamic-slice_fusion
  95.0 14.5 %all-to-all-done.2 = f32[128,2,128]{2,1,0:T(2,128)S(1)} async-done(((f32[128,2,128]{2,1,0:T(2,128)}), f32[128,2,128]{2,1,0:T(2,128)S(1)}, u32[]{:S(2)}, u32[]{:S(2)}) %all-to-all-start.2) | async-done | bytes 131104 | tf_op jit(solution)/shard_map/all_to_all | solution.py:485
  109.5 0.2 fusion
  109.7 0.0 copy-start.5
  109.7 12.0 %all_to_all.20 = f32[32,2,128]{2,1,0:T(2,128)S(1)} all-to-all(f32[32,2,128]{2,1,0:T(2,128)S(1)} %bitcast.55), channel_id=1, replica_groups=mesh['high'=32,'low'=4,'coord'=4] {'high'}, dimensions={0} | all-to-all | bytes 65536 | tf_op jit(solution)/shard_map/all_to_all | solution.py:493
  121.7 0.0 copy-done
  121.7 0.0 copy-done.5
  121.7 0.7 copy-done.6
  122.4 1.7 %finish.1 = (f32[64,128]{1,0:T(8,128)}, f32[8,128]{1,0:T(8,128)}) custom-call(s32[4,4]{1,0:T(4,128)} %cols_ref.1, s32[4,4]{1,0:T(4,128)} %tiles_ref.1, f32[64,128]{1,0:T(8,128)S(1)} %bitcast.46, f32[8,128]{1,0:T(8,128)S(1)} %bitcast.49, f32[4,128]{1,0:T(4,128)S(1)} %bitcast.51, f32[64,128]{1,0:T(8,128)S(1)} %bitcast.47, bf16[16,128,128]{2,1,0:T(8,128)(2,1)S(1)} %copy-done, ...), custom_call_target="tpu_custom_call" | custom-call | tf_op jit(solution)/shard_map/finish/pallas_call | solution.py:422
  (8 shorter events, 0.0 us)
Async XLA Ops:
  0.6 38.0 %copy-start.4 = (bf16[256,256]{1,0:T(8,128)(2,1)S(1)}, bf16[256,256]{1,0:T(8,128)(2,1)}, u32[]{:S(2)}) copy-start(bf16[256,256]{1,0:T(8,128)(2,1)} %constant.45.clone.t3) | copy-start | bytes 393220
  2.2 36.4 %copy-start.2 = (bf16[256,256]{1,0:T(8,128)(2,1)S(1)}, bf16[256,256]{1,0:T(8,128)(2,1)}, u32[]{:S(2)}) copy-start(bf16[256,256]{1,0:T(8,128)(2,1)} %constant.43.clone.t1) | copy-start | bytes 393220
  2.2 36.4 %copy-start.3 = (bf16[256,256]{1,0:T(8,128)(2,1)S(1)}, bf16[256,256]{1,0:T(8,128)(2,1)}, u32[]{:S(2)}) copy-start(bf16[256,256]{1,0:T(8,128)(2,1)} %constant.44.clone.t2) | copy-start | bytes 393220
  2.2 36.4 %all-to-all-start = ((f32[128,2,128]{2,1,0:T(2,128)}), f32[128,2,128]{2,1,0:T(2,128)S(1)}, u32[]{:S(2)}, u32[]{:S(2)}) async-start(f32[128,2,128]{2,1,0:T(2,128)} %gather.1), calls=%async_computation | async-start | bytes 262144 | tf_op jit(solution)/shard_map/all_to_all | solution.py:455
  40.4 31.2 %all-to-all-start.1 = ((f32[512,2,128]{2,1,0:T(2,128)}), f32[512,2,128]{2,1,0:T(2,128)S(1)}, u32[]{:S(2)}, u32[]{:S(2)}) async-start(f32[512,2,128]{2,1,0:T(2,128)} %bitcast.52), calls=%async_computation.1 | async-start | bytes 1048576 | tf_op jit(solution)/shard_map/all_to_all | solution.py:474
  71.6 50.1 %copy-start.1 = (bf16[16,128,128]{2,1,0:T(8,128)(2,1)S(1)}, bf16[16,128,128]{2,1,0:T(8,128)(2,1)}, u32[]{:S(2)}) copy-start(bf16[16,128,128]{2,1,0:T(8,128)(2,1)} %get-tuple-element.9.w2) | copy-start | bytes 1572868
  86.8 34.9 %copy-start = (bf16[16,128,128]{2,1,0:T(8,128)(2,1)S(1)}, bf16[16,128,128]{2,1,0:T(8,128)(2,1)}, u32[]{:S(2)}) copy-start(bf16[16,128,128]{2,1,0:T(8,128)(2,1)} %get-tuple-element.8.w1) | copy-start | bytes 1572868
  86.8 22.6 %all-to-all-start.2 = ((f32[128,2,128]{2,1,0:T(2,128)}), f32[128,2,128]{2,1,0:T(2,128)S(1)}, u32[]{:S(2)}, u32[]{:S(2)}) async-start(f32[128,2,128]{2,1,0:T(2,128)} %bitcast.53), calls=%async_computation.2 | async-start | bytes 262144 | tf_op jit(solution)/shard_map/all_to_all | solution.py:485
  109.5 12.2 %copy-start.7 = (f32[512]{0:T(512)S(1)}, f32[512]{0:T(512)}, u32[]{:S(2)}) copy-start(f32[512]{0:T(512)} %param.23) | copy-start | bytes 6148
  109.7 12.0 %copy-start.5 = (f32[2,4096]{1,0:T(2,128)S(1)}, f32[2,4096]{1,0:T(2,128)}, u32[]{:S(2)}) copy-start(f32[2,4096]{1,0:T(2,128)} %param.17) | copy-start | bytes 98308
  121.7 0.7 copy-start.6

commit v5 on v4

--- a/solution.py
+++ b/solution.py
@@ -109,7 +109,7 @@
     out[...] = buf[pl.ds(at_ref[0], 2), :]
 
 
-def spread_kernel(at_ref, x_ref, extra, t1, t2, t3, out, buf, sems, *, wraps):
+def spread_kernel(at_ref, x_ref, extra, t1, t2, t3, out, buf, wide, sems, *, wraps):
     rows = x_ref.shape[0]
     at = at_ref[0]
 
@@ -121,29 +121,40 @@
         low_part = jnp.dot(t3[...], high, preferred_element_type=F32)
         low_part += jnp.dot(t1[...], low, preferred_element_type=F32)
         res += jnp.dot(t1[...], two, preferred_element_type=F32)
-        res = res[:, :BLK] + (res[:, BLK:] + low_part)
-        buf[...] = res.reshape(buf.shape)
+        buf[...] = res[:, :BLK] + (res[:, BLK:] + low_part)
 
     @pl.when(at >= 0)
     def _():
         first, second = extra[0:1], extra[1:2]
         wrap = second * (first - ALPHA * x_ref[rows - 1 : rows])
         first = jnp.where(at < wraps, wrap, first)
-        even = lax.broadcasted_iota(jnp.int32, (2, BLK), 0) == 0
-        buf[...] = jnp.broadcast_to(jnp.where(even, first, second)[None], buf.shape)
-
-    copies = [
-        pltpu.make_async_copy(buf, out.at[:, o], sems.at[o]) for o in range(out.shape[1])
-    ]
-    for copy in copies:
-        copy.start()
+        even = lax.broadcasted_iota(jnp.int32, buf.shape, 0) % 2 == 0
+        buf[...] = jnp.where(even, first, second)
+
+    each = out.shape[0] // (rows // 2)
+    even = lax.broadcasted_iota(jnp.int32, (each, BLK), 0) % 2 == 0
+    parts = sems.shape[0]
+    size = out.shape[0] // parts
+    copies = []
+    for part in range(parts):
+        for p in range(part * rows // (2 * parts), (part + 1) * rows // (2 * parts)):
+            wide[p * each : (p + 1) * each] = jnp.where(
+                even, buf[2 * p : 2 * p + 1], buf[2 * p + 1 : 2 * p + 2]
+            )
+        span = pl.ds(part * size, size)
+        copies.append(pltpu.make_async_copy(wide.at[span], out.at[span], sems.at[part]))
+        copies[-1].start()
     for copy in copies:
         copy.wait()
 
 
-def finish_kernel(cols_ref, tiles_ref, state, mult, stab, update, w1, w2, new_state, new_mult):
+def finish_kernel(
+    cols_ref, tiles_ref, state, mult, stab, update, w1, w2, out_state, new_mult, new_state, sem
+):
     ncb, gnb = cols_ref.shape
     new_state[...] = state[...] + update[...]
+    copy = pltpu.make_async_copy(new_state, out_state, sem)
+    copy.start()
     owner = lax.broadcasted_iota(jnp.int32, mult.shape, 0) // 2
     total = jnp.zeros(mult.shape, F32)
     for j in range(gnb):
@@ -161,6 +172,7 @@
     for c in range(ncb):
         weight = jnp.where(owner == c, stab[c : c + 1], weight)
     new_mult[...] = mult[...] + (total - weight * mult[...]) / weight
+    copy.wait()
 
 
 def swapped(value):
@@ -407,12 +419,13 @@
 def spread_call(at, columns, extra, pieces, co, wraps):
     return pl.pallas_call(
         functools.partial(spread_kernel, wraps=wraps),
-        out_shape=jax.ShapeDtypeStruct((columns.shape[0] // 2, co, 2, BLK), F32),
+        out_shape=jax.ShapeDtypeStruct((columns.shape[0] * co, BLK), F32),
         in_specs=[SM] + [VM] * 5,
         out_specs=pl.BlockSpec(memory_space=pl.ANY),
         scratch_shapes=[
-            pltpu.VMEM((columns.shape[0] // 2, 2, BLK), F32),
-            pltpu.SemaphoreType.DMA((co,)),
+            pltpu.VMEM(columns.shape, F32),
+            pltpu.VMEM((columns.shape[0] * co, BLK), F32),
+            pltpu.SemaphoreType.DMA((4,)),
         ],
         name="spread",
     )(at, columns, extra, *pieces)
@@ -426,7 +439,8 @@
             jax.ShapeDtypeStruct(mult.shape, F32),
         ],
         in_specs=[SM, SM] + [VM] * 6,
-        out_specs=[VM, VM],
+        out_specs=[pl.BlockSpec(memory_space=pl.ANY), VM],
+        scratch_shapes=[pltpu.VMEM(state.shape, F32), pltpu.SemaphoreType.DMA(())],
         name="finish",
     )(cols, tiles, state, mult, stab, update, w1, w2)
 
@@ -475,7 +489,8 @@
             spread, group + ("coord",), split_axis=0, concat_axis=0, tiled=True
         ).reshape(tm * co * 2, BLK)
 
-        mats = bank_call(bank)
+        mats = list(bank_call(bank))
+        mats = [pltpu.with_memory_space_constraint(m, pltpu.VMEM) for m in mats[:2]] + mats[2:]
         recv = pltpu.with_memory_space_constraint(recv, pltpu.VMEM)
         fac = lax.dynamic_index_in_dim(jnp.asarray(factors), t, 0, keepdims=False)
         solved = solve_call(
@@ -489,18 +504,24 @@
             jnp.asarray(inverse), lax.axis_index("low") * (2 * high), 2 * high, axis=0
         )
         table = lax.optimization_barrier(table)
-        rows = lax.optimization_barrier(jnp.dot(table, slots, precision=HIGHEST))
+        kept = (
+            blocks(state).reshape(2 * nb, BLK),
+            blocks(multiplier).reshape(2 * ncb, BLK),
+            stab.reshape(ncb, BLK),
+        )
+        kept = [pltpu.with_memory_space_constraint(v, pltpu.VMEM) for v in kept]
+        rows, *kept = lax.optimization_barrier(
+            (jnp.dot(table, slots, precision=HIGHEST), *kept)
+        )
         rows = lax.all_to_all(
             rows.reshape(high, 2, BLK), "high", split_axis=0, concat_axis=0, tiled=True
         ).reshape(2 * nb, BLK)
         new_state, new_mult = finish_call(
             g_cols,
             g_tiles,
-            pltpu.with_memory_space_constraint(blocks(state).reshape(2 * nb, BLK), pltpu.VMEM),
-            pltpu.with_memory_space_constraint(blocks(multiplier).reshape(2 * ncb, BLK), pltpu.VMEM),
-            pltpu.with_memory_space_constraint(stab.reshape(ncb, BLK), pltpu.VMEM),
+            *kept,
             pltpu.with_memory_space_constraint(rows, pltpu.VMEM),
-            *[pltpu.with_memory_space_constraint(m, pltpu.VMEM) for m in mats[:2]],
+            *mats[:2],
         )
 
         def lines(value):

time: 125 us -> 126 us (level)
  local copies, waits for them, and re-layouts: 2.76 us -> 4.18 us
    unnamed x16 -> x20, local copies, waits for them, and re-layouts: 0.7 us -> 2.12 us
where the time goes in v5:
time: 126 us
  waiting for transfers between devices  46.4 us (37%)
  starting transfers between devices  37.7 us (30%)
  Pallas kernels  24.6 us (20%)
  blocking collectives  11.9 us (9%)
  local copies, waits for them, and re-layouts  4.18 us (3%)
    all_to_all x1, starting transfers between devices, local(): lax.all_to_all(sent, group, split_axis=0, concat_axis=0, tiled=True)  21 us
    all_to_all x1, waiting for transfers between devices, local(): lax.all_to_all(spread, group + ('coord',), split_axis=0, concat_axis=0, t...  17.8 us
    pallas_call x1, Pallas kernels, solve_call(): pl.pallas_call(kernel, out_shape=jax.ShapeDtypeStruct((2 * nb * parts, BL...  14.9 us
    all_to_all x1, waiting for transfers between devices, local(): lax.all_to_all(solved.reshape(tm, 2, BLK), group, split_axis=0, concat_ax...  14.5 us
    all_to_all x1, waiting for transfers between devices, local(): lax.all_to_all(sent, group, split_axis=0, concat_axis=0, tiled=True)  14 us
    all_to_all x1, blocking collectives, local(): lax.all_to_all(rows.reshape(high, 2, BLK), 'high', split_axis=0, concat_a...  11.9 us
    all_to_all x1, starting transfers between devices, local(): lax.all_to_all(spread, group + ('coord',), split_axis=0, concat_axis=0, t...  9.4 us
    all_to_all x1, starting transfers between devices, local(): lax.all_to_all(solved.reshape(tm, 2, BLK), group, split_axis=0, concat_ax...  7.26 us
  transfers between devices with their start and end apart: 3, of which 3 were waited for; matrix products, arithmetic and copies ran while one was open for 2% of the time, Pallas kernels for 3%

profile of v5, /device:TPU:1, one launch (start us, length us, event | category | flops | bytes accessed | tf_op | source)
XLA Modules:
  0.0 125.7 jit_solution(7663068748433367792)
XLA Ops:
  0.6 0.0 copy-start.6
  0.6 1.5 %gather.1 = f32[128,2,128]{2,1,0:T(2,128)} custom-call(f32[32,2,128]{2,1,0:T(2,128)} %bitcast.45, f32[32,2,128]{2,1,0:T(2,128)} %bitcast.56, f32[4,2,128]{2,1,0:T(2,128)} %bitcast.48), custom_call_target="tpu_custom_call" | custom-call | tf_op jit(solution)/shard_map/gather/pallas_call | solution.py:397
  2.2 0.0 copy-start.4
  2.2 0.0 copy-start.5
  2.2 21.0 %all-to-all-start = ((f32[128,2,128]{2,1,0:T(2,128)}), f32[128,2,128]{2,1,0:T(2,128)S(1)}, u32[]{:S(2)}, u32[]{:S(2)}) async-start(f32[128,2,128]{2,1,0:T(2,128)} %gather.1), calls=%async_computation | async-start | bytes 262144 | tf_op jit(solution)/shard_map/all_to_all | solution.py:469
  23.2 1.4 %extra.1 = f32[2,128]{1,0:T(2,128)} custom-call(s32[1]{0:T(128)} %bitcast.10.at_ref, f32[32,128]{1,0:T(8,128)} %bitcast.57, f32[32,128]{1,0:T(8,128)} %bitcast.58, f32[32,128]{1,0:T(8,128)} %bitcast.59, f32[4,128]{1,0:T(4,128)} %bitcast.50, s32[3,32]{1,0:T(4,128)} %bitcast.60, s32[3,32]{1,0:T(4,128)} %bitcast.61, s32[4,4]{1,0:T(4,128)} %cols_ref.1, ...), custom_call_target="tpu_custom_call" | custom-call | tf_op jit(solution)/shard_map/extra/pallas_call | solution.py:409
  24.6 14.0 %all-to-all-done = f32[128,2,128]{2,1,0:T(2,128)S(1)} async-done(((f32[128,2,128]{2,1,0:T(2,128)}), f32[128,2,128]{2,1,0:T(2,128)S(1)}, u32[]{:S(2)}, u32[]{:S(2)}) %all-to-all-start) | async-done | bytes 131104 | tf_op jit(solution)/shard_map/all_to_all | solution.py:469
  38.6 0.0 copy-done.6
  38.6 0.0 copy-done.4
  38.6 1.8 %spread.1 = f32[1024,128]{1,0:T(8,128)} custom-call(s32[1]{0:T(128)} %bitcast.2.at_ref, f32[256,128]{1,0:T(8,128)S(1)} %bitcast.44, f32[2,128]{1,0:T(2,128)} %extra.1, bf16[256,256]{1,0:T(8,128)(2,1)S(1)} %copy-done.4, bf16[256,256]{1,0:T(8,128)(2,1)S(1)} %copy-done.5, bf16[256,256]{1,0:T(8,128)(2,1)S(1)} %copy-done.6), custom_call_target="tpu_custom_call" | custom-call | tf_op jit(solution)/shard_map/spread/pallas_call | solution.py:420
  40.5 9.4 %all-to-all-start.1 = ((f32[512,2,128]{2,1,0:T(2,128)}), f32[512,2,128]{2,1,0:T(2,128)S(1)}, u32[]{:S(2)}, u32[]{:S(2)}) async-start(f32[512,2,128]{2,1,0:T(2,128)} %bitcast.52), calls=%async_computation.1 | async-start | bytes 1048576 | tf_op jit(solution)/shard_map/all_to_all | solution.py:488
  49.9 2.8 %bank.1 = (bf16[16,128,128]{2,1,0:T(8,128)(2,1)}, bf16[16,128,128]{2,1,0:T(8,128)(2,1)}, bf16[16,128,128]{2,1,0:T(8,128)(2,1)}, bf16[16,128,128]{2,1,0:T(8,128)(2,1)}) custom-call(f32[16,128,128]{2,1,0:T(8,128)} %bank_ref.1), custom_call_target="tpu_custom_call" | custom-call | tf_op jit(solution)/shard_map/bank/pallas_call | solution.py:390
  52.6 1.2 dynamic-slice_bitcast_fusion.fac_ref
  53.8 17.8 %all-to-all-done.1 = f32[512,2,128]{2,1,0:T(2,128)S(1)} async-done(((f32[512,2,128]{2,1,0:T(2,128)}), f32[512,2,128]{2,1,0:T(2,128)S(1)}, u32[]{:S(2)}, u32[]{:S(2)}) %all-to-all-start.1) | async-done | bytes 524320 | tf_op jit(solution)/shard_map/all_to_all | solution.py:488
  71.7 1.0 copy-done
  72.7 1.0 copy-done.2
  73.8 14.9 %solve.1 = f32[256,128]{1,0:T(8,128)} custom-call(f32[4]{0:T(128)} %dynamic-slice_bitcast_fusion.fac_ref, s32[1]{0:T(128)} %bitcast.1.own_ref, f32[1024,128]{1,0:T(8,128)S(1)} %bitcast.43, bf16[16,128,128]{2,1,0:T(8,128)(2,1)S(1)} %copy-done, bf16[16,128,128]{2,1,0:T(8,128)(2,1)S(1)} %copy-done.2, bf16[16,128,128]{2,1,0:T(8,128)(2,1)} %get-tuple-element.14.v1, ...), custom_call_target="tpu_custom_call" | custom-call | tf_op jit(solution)/shard_map/solve/pallas_call | solution.py:378
  88.7 7.3 %all-to-all-start.2 = ((f32[128,2,128]{2,1,0:T(2,128)}), f32[128,2,128]{2,1,0:T(2,128)S(1)}, u32[]{:S(2)}, u32[]{:S(2)}) async-start(f32[128,2,128]{2,1,0:T(2,128)} %bitcast.53), calls=%async_computation.2 | async-start | bytes 262144 | tf_op jit(solution)/shard_map/all_to_all | solution.py:500
  96.0 0.9 constant_dynamic-slice_fusion
  96.8 14.5 %all-to-all-done.2 = f32[128,2,128]{2,1,0:T(2,128)S(1)} async-done(((f32[128,2,128]{2,1,0:T(2,128)}), f32[128,2,128]{2,1,0:T(2,128)S(1)}, u32[]{:S(2)}, u32[]{:S(2)}) %all-to-all-start.2) | async-done | bytes 131104 | tf_op jit(solution)/shard_map/all_to_all | solution.py:500
  111.4 0.2 fusion
  111.6 0.0 copy-start.7
  111.6 11.9 %all_to_all.20 = f32[32,2,128]{2,1,0:T(2,128)S(1)} all-to-all(f32[32,2,128]{2,1,0:T(2,128)S(1)} %bitcast.55), channel_id=1, replica_groups=mesh['high'=32,'low'=4,'coord'=4] {'high'}, dimensions={0} | all-to-all | bytes 65536 | tf_op jit(solution)/shard_map/all_to_all | solution.py:516
  123.6 2.1 %finish.1 = (f32[64,128]{1,0:T(8,128)}, f32[8,128]{1,0:T(8,128)}) custom-call(s32[4,4]{1,0:T(4,128)} %cols_ref.1, s32[4,4]{1,0:T(4,128)} %tiles_ref.1, f32[64,128]{1,0:T(8,128)S(1)} %bitcast.46, f32[8,128]{1,0:T(8,128)S(1)} %bitcast.49, f32[4,128]{1,0:T(4,128)S(1)} %bitcast.51, f32[64,128]{1,0:T(8,128)S(1)} %bitcast.47, bf16[16,128,128]{2,1,0:T(8,128)(2,1)S(1)} %copy-done.1, ...), custom_call_target="tpu_custom_call" | custom-call | tf_op jit(solution)/shard_map/finish/pallas_call | solution.py:435
  (12 shorter events, 0.0 us)
Async XLA Ops:
  0.6 38.0 %copy-start.6 = (bf16[256,256]{1,0:T(8,128)(2,1)S(1)}, bf16[256,256]{1,0:T(8,128)(2,1)}, u32[]{:S(2)}) copy-start(bf16[256,256]{1,0:T(8,128)(2,1)} %constant.45.clone.t3) | copy-start | bytes 393220
  2.2 36.4 %copy-start.4 = (bf16[256,256]{1,0:T(8,128)(2,1)S(1)}, bf16[256,256]{1,0:T(8,128)(2,1)}, u32[]{:S(2)}) copy-start(bf16[256,256]{1,0:T(8,128)(2,1)} %constant.43.clone.t1) | copy-start | bytes 393220
  2.2 36.4 %copy-start.5 = (bf16[256,256]{1,0:T(8,128)(2,1)S(1)}, bf16[256,256]{1,0:T(8,128)(2,1)}, u32[]{:S(2)}) copy-start(bf16[256,256]{1,0:T(8,128)(2,1)} %constant.44.clone.t2) | copy-start | bytes 393220
  2.2 36.4 %all-to-all-start = ((f32[128,2,128]{2,1,0:T(2,128)}), f32[128,2,128]{2,1,0:T(2,128)S(1)}, u32[]{:S(2)}, u32[]{:S(2)}) async-start(f32[128,2,128]{2,1,0:T(2,128)} %gather.1), calls=%async_computation | async-start | bytes 262144 | tf_op jit(solution)/shard_map/all_to_all | solution.py:469
  40.5 31.2 %all-to-all-start.1 = ((f32[512,2,128]{2,1,0:T(2,128)}), f32[512,2,128]{2,1,0:T(2,128)S(1)}, u32[]{:S(2)}, u32[]{:S(2)}) async-start(f32[512,2,128]{2,1,0:T(2,128)} %bitcast.52), calls=%async_computation.1 | async-start | bytes 1048576 | tf_op jit(solution)/shard_map/all_to_all | solution.py:488
  71.7 1.0 copy-start
  72.7 1.0 copy-start.2
  73.8 49.8 %copy-start.3 = (bf16[16,128,128]{2,1,0:T(8,128)(2,1)S(1)}, bf16[16,128,128]{2,1,0:T(8,128)(2,1)}, u32[]{:S(2)}) copy-start(bf16[16,128,128]{2,1,0:T(8,128)(2,1)} %get-tuple-element.13.w2) | copy-start | bytes 1572868
  88.7 34.9 %copy-start.1 = (bf16[16,128,128]{2,1,0:T(8,128)(2,1)S(1)}, bf16[16,128,128]{2,1,0:T(8,128)(2,1)}, u32[]{:S(2)}) copy-start(bf16[16,128,128]{2,1,0:T(8,128)(2,1)} %get-tuple-element.12.w1) | copy-start | bytes 1572868
  88.7 22.7 %all-to-all-start.2 = ((f32[128,2,128]{2,1,0:T(2,128)}), f32[128,2,128]{2,1,0:T(2,128)S(1)}, u32[]{:S(2)}, u32[]{:S(2)}) async-start(f32[128,2,128]{2,1,0:T(2,128)} %bitcast.53), calls=%async_computation.2 | async-start | bytes 262144 | tf_op jit(solution)/shard_map/all_to_all | solution.py:500
  111.4 12.2 %copy-start.8 = (f32[2,512]{1,0:T(2,128)S(1)}, f32[2,512]{1,0:T(2,128)}, u32[]{:S(2)}) copy-start(f32[2,512]{1,0:T(2,128)} %param.18) | copy-start | bytes 12292
  111.4 12.2 %copy-start.9 = (f32[512]{0:T(512)S(1)}, f32[512]{0:T(512)}, u32[]{:S(2)}) copy-start(f32[512]{0:T(512)} %param.23) | copy-start | bytes 6148
  111.6 12.0 %copy-start.7 = (f32[2,4096]{1,0:T(2,128)S(1)}, f32[2,4096]{1,0:T(2,128)}, u32[]{:S(2)}) copy-start(f32[2,4096]{1,0:T(2,128)} %param.17) | copy-start | bytes 98308

commit v6 on v4

--- a/solution.py
+++ b/solution.py
@@ -1,9 +1,7 @@
-import functools
 import math
 
 import jax
 import jax.numpy as jnp
-import ml_dtypes
 import numpy as np
 from jax import lax
 from jax.experimental import pallas as pl
@@ -38,15 +36,7 @@
     a_odd = np.where(zero, 1.0 + beta, 1.0 - beta * np.cos(theta))
     b_even = np.where(zero, 0.0, -beta * np.sin(theta))
     factors = np.stack([a_even, a_odd, b_even, zero.astype(np.float64)], axis=1)
-    return pieces_of(forward), inverse.astype(np.float32), factors.astype(np.float32)
-
-
-def pieces_of(table):
-    rest, pieces = table.astype(np.float32), []
-    for _ in range(3):
-        pieces.append(rest.astype(ml_dtypes.bfloat16))
-        rest = rest - pieces[-1].astype(np.float32)
-    return pieces
+    return forward.astype(np.float32), inverse.astype(np.float32), factors.astype(np.float32)
 
 
 def split3(value):
@@ -109,38 +99,6 @@
     out[...] = buf[pl.ds(at_ref[0], 2), :]
 
 
-def spread_kernel(at_ref, x_ref, extra, t1, t2, t3, out, buf, sems, *, wraps):
-    rows = x_ref.shape[0]
-    at = at_ref[0]
-
-    @pl.when(at < 0)
-    def _():
-        high, mid, low = split3(x_ref[...])
-        two = jnp.concatenate([high, mid], axis=1)
-        res = jnp.dot(t2[...], two, preferred_element_type=F32)
-        low_part = jnp.dot(t3[...], high, preferred_element_type=F32)
-        low_part += jnp.dot(t1[...], low, preferred_element_type=F32)
-        res += jnp.dot(t1[...], two, preferred_element_type=F32)
-        res = res[:, :BLK] + (res[:, BLK:] + low_part)
-        buf[...] = res.reshape(buf.shape)
-
-    @pl.when(at >= 0)
-    def _():
-        first, second = extra[0:1], extra[1:2]
-        wrap = second * (first - ALPHA * x_ref[rows - 1 : rows])
-        first = jnp.where(at < wraps, wrap, first)
-        even = lax.broadcasted_iota(jnp.int32, (2, BLK), 0) == 0
-        buf[...] = jnp.broadcast_to(jnp.where(even, first, second)[None], buf.shape)
-
-    copies = [
-        pltpu.make_async_copy(buf, out.at[:, o], sems.at[o]) for o in range(out.shape[1])
-    ]
-    for copy in copies:
-        copy.start()
-    for copy in copies:
-        copy.wait()
-
-
 def finish_kernel(cols_ref, tiles_ref, state, mult, stab, update, w1, w2, new_state, new_mult):
     ncb, gnb = cols_ref.shape
     new_state[...] = state[...] + update[...]
@@ -404,20 +362,6 @@
     )(at, initial, mass, stiff, stab, offs, ktiles, cols, gtiles)
 
 
-def spread_call(at, columns, extra, pieces, co, wraps):
-    return pl.pallas_call(
-        functools.partial(spread_kernel, wraps=wraps),
-        out_shape=jax.ShapeDtypeStruct((columns.shape[0] // 2, co, 2, BLK), F32),
-        in_specs=[SM] + [VM] * 5,
-        out_specs=pl.BlockSpec(memory_space=pl.ANY),
-        scratch_shapes=[
-            pltpu.VMEM((columns.shape[0] // 2, 2, BLK), F32),
-            pltpu.SemaphoreType.DMA((co,)),
-        ],
-        name="spread",
-    )(at, columns, extra, *pieces)
-
-
 def finish_call(cols, tiles, state, mult, stab, update, w1, w2):
     return pl.pallas_call(
         finish_kernel,
@@ -432,7 +376,7 @@
 
 
 def make_local(forward, inverse, factors, low):
-    steps = forward[0].shape[0]
+    steps = forward.shape[0]
     group = ("high", "low")
 
     def blocks(value):
@@ -453,7 +397,7 @@
         lay = layout(nb, ncb)
         sent = gather_call(blocks(state), blocks(force), blocks(multiplier), tm)
         columns = lax.all_to_all(sent, group, split_axis=0, concat_axis=0, tiled=True)
-        columns = pltpu.with_memory_space_constraint(columns.reshape(steps, BLK), pltpu.VMEM)
+        columns = columns.reshape(steps, BLK)
         at = t - lay["wrap"]
         count = 2 * (tm - lay["wrap"])
         extra = extra_call(
@@ -468,9 +412,12 @@
             g_tiles,
             -(-count // 8) * 8,
         )
-        pieces = [pltpu.with_memory_space_constraint(jnp.asarray(p), pltpu.VMEM) for p in forward]
-        spread = spread_call(at.reshape(1), columns, extra, pieces, co, nb)
-        spread = spread.reshape(tm * co, 2, BLK)
+        is_wrap = (at >= 0) & (at < nb)
+        wrap = jnp.where(is_wrap, extra[1] * (extra[0] - ALPHA * columns[-1]), extra[0])
+        extra = jnp.stack([wrap, extra[1]])
+        spectrum = jnp.dot(forward, columns, precision=HIGHEST).reshape(tm, 2, BLK)
+        spectrum = jnp.where(at < 0, spectrum, extra[None])
+        spread = jnp.broadcast_to(spectrum[:, None], (tm, co, 2, BLK)).reshape(tm * co, 2, BLK)
         recv = lax.all_to_all(
             spread, group + ("coord",), split_axis=0, concat_axis=0, tiled=True
         ).reshape(tm * co * 2, BLK)
@@ -489,16 +436,22 @@
             jnp.asarray(inverse), lax.axis_index("low") * (2 * high), 2 * high, axis=0
         )
         table = lax.optimization_barrier(table)
-        rows = lax.optimization_barrier(jnp.dot(table, slots, precision=HIGHEST))
+        kept = (
+            blocks(state).reshape(2 * nb, BLK),
+            blocks(multiplier).reshape(2 * ncb, BLK),
+            stab.reshape(ncb, BLK),
+        )
+        kept = [pltpu.with_memory_space_constraint(v, pltpu.VMEM) for v in kept]
+        rows, *kept = lax.optimization_barrier(
+            (jnp.dot(table, slots, precision=HIGHEST), *kept)
+        )
         rows = lax.all_to_all(
             rows.reshape(high, 2, BLK), "high", split_axis=0, concat_axis=0, tiled=True
         ).reshape(2 * nb, BLK)
         new_state, new_mult = finish_call(
             g_cols,
             g_tiles,
-            pltpu.with_memory_space_constraint(blocks(state).reshape(2 * nb, BLK), pltpu.VMEM),
-            pltpu.with_memory_space_constraint(blocks(multiplier).reshape(2 * ncb, BLK), pltpu.VMEM),
-            pltpu.with_memory_space_constraint(stab.reshape(ncb, BLK), pltpu.VMEM),
+            *kept,
             pltpu.with_memory_space_constraint(rows, pltpu.VMEM),
             *[pltpu.with_memory_space_constraint(m, pltpu.VMEM) for m in mats[:2]],
         )

time: 125 us -> 124 us (level)
  Pallas kernels: 24.5 us -> 22.6 us
    pallas_call x1 -> x0, Pallas kernels: 1.82 us -> none  [spread_call(): pl.pallas_call(functools.partial(spread_kernel, wraps=wraps), out_shape=j...]
where the time goes in v6:
time: 124 us; the launch traced here: 123 us
  waiting for transfers between devices  46.3 us (37%)
  starting transfers between devices  37.4 us (30%)
  Pallas kernels  22.6 us (18%)
  blocking collectives  12 us (10%)
  local copies, waits for them, and re-layouts  3.33 us (3%)
    all_to_all x1, starting transfers between devices, local(): lax.all_to_all(sent, group, split_axis=0, concat_axis=0, tiled=True)  20.9 us
    all_to_all x1, waiting for transfers between devices, local(): lax.all_to_all(spread, group + ('coord',), split_axis=0, concat_axis=0, t...  17.8 us
    pallas_call x1, Pallas kernels, solve_call(): pl.pallas_call(kernel, out_shape=jax.ShapeDtypeStruct((2 * nb * parts, BL...  15.2 us
    all_to_all x1, waiting for transfers between devices, local(): lax.all_to_all(solved.reshape(tm, 2, BLK), group, split_axis=0, concat_ax...  14.5 us
    all_to_all x1, waiting for transfers between devices, local(): lax.all_to_all(sent, group, split_axis=0, concat_axis=0, tiled=True)  14 us
    all_to_all x1, blocking collectives, local(): lax.all_to_all(rows.reshape(high, 2, BLK), 'high', split_axis=0, concat_a...  12 us
    all_to_all x1, starting transfers between devices, local(): lax.all_to_all(spread, group + ('coord',), split_axis=0, concat_axis=0, t...  9.31 us
    all_to_all x1, starting transfers between devices, local(): lax.all_to_all(solved.reshape(tm, 2, BLK), group, split_axis=0, concat_ax...  7.27 us
  transfers between devices with their start and end apart: 3, of which 3 were waited for; matrix products, arithmetic and copies ran while one was open for 2% of the time, Pallas kernels for 3%

profile of v6, /device:TPU:1, one launch (start us, length us, event | category | flops | bytes accessed | tf_op | source)
XLA Modules:
  0.0 123.1 jit_solution(10251293092275548173)
XLA Ops:
  0.6 0.0 copy-start.5
  0.6 1.6 %gather.1 = f32[128,2,128]{2,1,0:T(2,128)} custom-call(f32[32,2,128]{2,1,0:T(2,128)} %bitcast.49, f32[32,2,128]{2,1,0:T(2,128)} %bitcast.63, f32[4,2,128]{2,1,0:T(2,128)} %bitcast.52), custom_call_target="tpu_custom_call" | custom-call | tf_op jit(solution)/shard_map/gather/pallas_call | solution.py:343
  2.2 20.9 %all-to-all-start = ((f32[128,2,128]{2,1,0:T(2,128)}), f32[128,2,128]{2,1,0:T(2,128)S(1)}, u32[]{:S(2)}, u32[]{:S(2)}) async-start(f32[128,2,128]{2,1,0:T(2,128)} %gather.1), calls=%async_computation | async-start | bytes 262144 | tf_op jit(solution)/shard_map/all_to_all | solution.py:399
  23.1 1.4 %extra.1 = f32[2,128]{1,0:T(2,128)} custom-call(s32[1]{0:T(128)} %bitcast.10.at_ref, f32[32,128]{1,0:T(8,128)} %bitcast.65, f32[32,128]{1,0:T(8,128)} %bitcast.66, f32[32,128]{1,0:T(8,128)} %bitcast.67, f32[4,128]{1,0:T(4,128)} %bitcast.54, s32[3,32]{1,0:T(4,128)} %bitcast.68, s32[3,32]{1,0:T(4,128)} %bitcast.69, s32[4,4]{1,0:T(4,128)} %cols_ref.1, ...), custom_call_target="tpu_custom_call" | custom-call | tf_op jit(solution)/shard_map/extra/pallas_call | solution.py:355
  24.5 14.0 %all-to-all-done = f32[128,2,128]{2,1,0:T(2,128)S(1)} async-done(((f32[128,2,128]{2,1,0:T(2,128)}), f32[128,2,128]{2,1,0:T(2,128)S(1)}, u32[]{:S(2)}, u32[]{:S(2)}) %all-to-all-start) | async-done | bytes 131104 | tf_op jit(solution)/shard_map/all_to_all | solution.py:399
  38.4 0.0 copy-done.5
  38.5 0.4 fusion.2
  38.8 0.3 copy-done.6
  39.2 0.9 broadcast_in_dim.16
  40.1 9.3 %all-to-all-start.1 = ((f32[512,2,128]{2,1,0:T(2,128)}), f32[512,2,128]{2,1,0:T(2,128)S(1)}, u32[]{:S(2)}, u32[]{:S(2)}) async-start(f32[512,2,128]{2,1,0:T(2,128)} %bitcast.17), calls=%async_computation.1 | async-start | bytes 1048576 | tf_op jit(solution)/shard_map/all_to_all | solution.py:421
  49.4 2.8 %bank.1 = (bf16[16,128,128]{2,1,0:T(8,128)(2,1)}, bf16[16,128,128]{2,1,0:T(8,128)(2,1)}, bf16[16,128,128]{2,1,0:T(8,128)(2,1)}, bf16[16,128,128]{2,1,0:T(8,128)(2,1)}) custom-call(f32[16,128,128]{2,1,0:T(8,128)} %bank_ref.1), custom_call_target="tpu_custom_call" | custom-call | tf_op jit(solution)/shard_map/bank/pallas_call | solution.py:336
  52.2 1.2 dynamic-slice_bitcast_fusion.fac_ref
  53.4 17.8 %all-to-all-done.1 = f32[512,2,128]{2,1,0:T(2,128)S(1)} async-done(((f32[512,2,128]{2,1,0:T(2,128)}), f32[512,2,128]{2,1,0:T(2,128)S(1)}, u32[]{:S(2)}, u32[]{:S(2)}) %all-to-all-start.1) | async-done | bytes 524320 | tf_op jit(solution)/shard_map/all_to_all | solution.py:421
  71.3 15.2 %solve.1 = f32[256,128]{1,0:T(8,128)} custom-call(f32[4]{0:T(128)} %dynamic-slice_bitcast_fusion.fac_ref, s32[1]{0:T(128)} %bitcast.1.own_ref, f32[1024,128]{1,0:T(8,128)S(1)} %bitcast.48, bf16[16,128,128]{2,1,0:T(8,128)(2,1)} %get-tuple-element.12.w1, bf16[16,128,128]{2,1,0:T(8,128)(2,1)} %get-tuple-element.13.w2, ...), custom_call_target="tpu_custom_call" | custom-call | tf_op jit(solution)/shard_map/solve/pallas_call | solution.py:324
  86.5 0.0 copy-start
  86.5 7.3 %all-to-all-start.2 = ((f32[128,2,128]{2,1,0:T(2,128)}), f32[128,2,128]{2,1,0:T(2,128)S(1)}, u32[]{:S(2)}, u32[]{:S(2)}) async-start(f32[128,2,128]{2,1,0:T(2,128)} %bitcast.58), calls=%async_computation.2 | async-start | bytes 262144 | tf_op jit(solution)/shard_map/all_to_all | solution.py:432
  93.8 0.9 constant_dynamic-slice_fusion
  94.6 14.5 %all-to-all-done.2 = f32[128,2,128]{2,1,0:T(2,128)S(1)} async-done(((f32[128,2,128]{2,1,0:T(2,128)}), f32[128,2,128]{2,1,0:T(2,128)S(1)}, u32[]{:S(2)}, u32[]{:S(2)}) %all-to-all-start.2) | async-done | bytes 131104 | tf_op jit(solution)/shard_map/all_to_all | solution.py:432
  109.1 0.2 fusion.3
  109.4 0.0 copy-start.2
  109.4 12.0 %all_to_all.20 = f32[32,2,128]{2,1,0:T(2,128)S(1)} all-to-all(f32[32,2,128]{2,1,0:T(2,128)S(1)} %bitcast.62), channel_id=1, replica_groups=mesh['high'=32,'low'=4,'coord'=4] {'high'}, dimensions={0} | all-to-all | bytes 65536 | tf_op jit(solution)/shard_map/all_to_all | solution.py:448
  121.3 0.0 copy-done.1
  121.3 0.0 copy-done
  121.4 1.7 %finish.1 = (f32[64,128]{1,0:T(8,128)}, f32[8,128]{1,0:T(8,128)}) custom-call(s32[4,4]{1,0:T(4,128)} %cols_ref.1, s32[4,4]{1,0:T(4,128)} %tiles_ref.1, f32[64,128]{1,0:T(8,128)S(1)} %bitcast.50, f32[8,128]{1,0:T(8,128)S(1)} %bitcast.53, f32[4,128]{1,0:T(4,128)S(1)} %bitcast.55, f32[64,128]{1,0:T(8,128)S(1)} %bitcast.51, bf16[16,128,128]{2,1,0:T(8,128)(2,1)S(1)} %copy-done, ...), custom_call_target="tpu_custom_call" | custom-call | tf_op jit(solution)/shard_map/finish/pallas_call | solution.py:366
  (11 shorter events, 0.0 us)
Async XLA Ops:
  0.6 37.8 %copy-start.5 = (f32[256,256]{1,0:T(8,128)S(1)}, f32[256,256]{1,0:T(8,128)}, u32[]{:S(2)}) copy-start(f32[256,256]{1,0:T(8,128)} %constant.43.clone) | copy-start | bytes 786436
  2.2 36.2 %all-to-all-start = ((f32[128,2,128]{2,1,0:T(2,128)}), f32[128,2,128]{2,1,0:T(2,128)S(1)}, u32[]{:S(2)}, u32[]{:S(2)}) async-start(f32[128,2,128]{2,1,0:T(2,128)} %gather.1), calls=%async_computation | async-start | bytes 262144 | tf_op jit(solution)/shard_map/all_to_all | solution.py:399
  38.5 0.7 copy-start.6
  40.1 31.1 %all-to-all-start.1 = ((f32[512,2,128]{2,1,0:T(2,128)}), f32[512,2,128]{2,1,0:T(2,128)S(1)}, u32[]{:S(2)}, u32[]{:S(2)}) async-start(f32[512,2,128]{2,1,0:T(2,128)} %bitcast.17), calls=%async_computation.1 | async-start | bytes 1048576 | tf_op jit(solution)/shard_map/all_to_all | solution.py:421
  71.3 50.1 %copy-start.1 = (bf16[16,128,128]{2,1,0:T(8,128)(2,1)S(1)}, bf16[16,128,128]{2,1,0:T(8,128)(2,1)}, u32[]{:S(2)}) copy-start(bf16[16,128,128]{2,1,0:T(8,128)(2,1)} %get-tuple-element.13.w2) | copy-start | bytes 1572868
  86.5 34.9 %copy-start = (bf16[16,128,128]{2,1,0:T(8,128)(2,1)S(1)}, bf16[16,128,128]{2,1,0:T(8,128)(2,1)}, u32[]{:S(2)}) copy-start(bf16[16,128,128]{2,1,0:T(8,128)(2,1)} %get-tuple-element.12.w1) | copy-start | bytes 1572868
  86.5 22.6 %all-to-all-start.2 = ((f32[128,2,128]{2,1,0:T(2,128)}), f32[128,2,128]{2,1,0:T(2,128)S(1)}, u32[]{:S(2)}, u32[]{:S(2)}) async-start(f32[128,2,128]{2,1,0:T(2,128)} %bitcast.58), calls=%async_computation.2 | async-start | bytes 262144 | tf_op jit(solution)/shard_map/all_to_all | solution.py:432
  109.1 12.2 %copy-start.3 = (f32[2,512]{1,0:T(2,128)S(1)}, f32[2,512]{1,0:T(2,128)}, u32[]{:S(2)}) copy-start(f32[2,512]{1,0:T(2,128)} %param.16) | copy-start | bytes 12292
  109.1 12.2 %copy-start.4 = (f32[512]{0:T(512)S(1)}, f32[512]{0:T(512)}, u32[]{:S(2)}) copy-start(f32[512]{0:T(512)} %param.21) | copy-start | bytes 6148
  109.4 12.0 %copy-start.2 = (f32[2,4096]{1,0:T(2,128)S(1)}, f32[2,4096]{1,0:T(2,128)}, u32[]{:S(2)}) copy-start(f32[2,4096]{1,0:T(2,128)} %param.15) | copy-start | bytes 98308

commit v7 on v6

--- a/solution.py
+++ b/solution.py
@@ -11,6 +11,7 @@
 BLK = 128
 REACH = 2
 SWEEPS = 8
+FULL = 3
 ALPHA = 0.001
 HIGHEST = lax.Precision.HIGHEST
 F32 = jnp.float32
@@ -142,8 +143,9 @@
     nidx = 2 * co * (knb + ncb)
 
     def kernel(
-        fac_ref, own_ref, r_ref, w1, w2, v1, v2, out_ref,
+        fac_ref, own_ref, r_ref, w1_hbm, w2_hbm, v1_hbm, v2_hbm, out_ref,
         p_ref, q_ref, acc, gts, xs, rhs, e_ref, c_ref, xt, xl, gy, sc, istab, wide, idxv, idxs, sem,
+        w1, w2, v1, v2, sems,
     ):
         a_even, a_odd, b_even, is_zero = fac_ref[0], fac_ref[1], fac_ref[2], fac_ref[3]
 
@@ -151,6 +153,14 @@
             start += lay[name] * 2 * co
             return r_ref[start : start + rows]
 
+        loads = [
+            pltpu.make_async_copy(src, dst, sems.at[i])
+            for i, (src, dst) in enumerate(
+                ((w1_hbm, w1), (w2_hbm, w2), (v1_hbm, v1), (v2_hbm, v2))
+            )
+        ]
+        for load in loads:
+            load.start()
         raw = part("idx", nidx).astype(jnp.int32)
         lane = lax.broadcasted_iota(jnp.int32, raw.shape, 1)
         line = lax.broadcasted_iota(jnp.int32, raw.shape, 0)
@@ -175,14 +185,19 @@
 
         def products(x1, x2, x3, mats, dst, beside):
             rows = x1.shape[0]
-            pairs = ((x1, x1), (x2, x2), (x3, jnp.zeros_like(x3)))
+            pairs = [(x1, x1), (x2, x2)]
+            if x3 is not None:
+                pairs.append((x3, jnp.zeros_like(x3)))
             stack = jnp.concatenate([jnp.concatenate(p, axis=1) for p in pairs], axis=0)
             m1, m2 = mats
             for pair in range(tiles // 2):
                 b1 = jnp.concatenate([m1[2 * pair], m1[2 * pair + 1]], axis=1)
                 b2 = jnp.concatenate([m2[2 * pair], m2[2 * pair + 1]], axis=1)
                 res = jnp.dot(stack, jnp.concatenate([b1, b2]), preferred_element_type=F32)
-                res = res[:rows] + (res[rows : 2 * rows] + res[2 * rows :])
+                low = res[rows : 2 * rows]
+                if x3 is not None:
+                    low = low + res[2 * rows :]
+                res = res[:rows] + low
                 for side in range(2):
                     start = (2 * pair + side) * rows
                     dst[start : start + rows] = res[:, side * BLK : side * BLK + BLK]
@@ -255,28 +270,33 @@
         shalf = part("stab", crow // 2)
         stab = jnp.concatenate([doubled(shalf, False), doubled(shalf, True)], axis=0)
         istab[...] = 1.0 / stab
+        for i in range(nrow // chunk):
+            prepare(i)
+        for load in loads[:2]:
+            load.wait()
         products(*split3(part("state", nrow)), (w1, w2), p_ref, lambda i: None)
         copy.wait()
-
-        def both(i):
-            prepare(i)
-            couple(i)
-
-        products(*split3(mult), (v1, v2), q_ref, both)
+        for load in loads[2:]:
+            load.wait()
+        products(*split3(mult), (v1, v2), q_ref, couple)
         constrain()
         scatter()
         sc[...] = stab * mult - gy[...]
         advance(True)
 
-        def sweep(_, carry):
-            products(xt[:, :BLK], xt[:, BLK:], xl[...], (w1, w2), p_ref, lambda i: None)
+        def sweep(low):
+            x3 = xl[...] if low else None
+            products(xt[:, :BLK], xt[:, BLK:], x3, (w1, w2), p_ref, lambda i: None)
             constrain()
             products(*split3((gy[...] - sc[...]) * istab[...]), (v1, v2), q_ref, couple)
             scatter()
             advance(False)
-            return carry
-
-        lax.fori_loop(0, SWEEPS - 1, sweep, 0)
+
+        def loop(count, low):
+            lax.fori_loop(0, count, lambda i, carry: (sweep(low), carry)[1], 0)
+
+        loop(SWEEPS - 1 - FULL, False)
+        loop(FULL, True)
         own = own_ref[0]
         parts = out_ref.shape[0] // (2 * nb)
         for b in range(nb):
@@ -303,6 +323,11 @@
         pltpu.VMEM((-(-nidx // 16) * 8, BLK), jnp.int32),
         pltpu.SMEM((-(-nidx // 16) * 8, BLK), jnp.int32),
         pltpu.SemaphoreType.DMA(()),
+        pltpu.VMEM((tiles, BLK, BLK), BF16),
+        pltpu.VMEM((tiles, BLK, BLK), BF16),
+        pltpu.VMEM((tiles, BLK, BLK), BF16),
+        pltpu.VMEM((tiles, BLK, BLK), BF16),
+        pltpu.SemaphoreType.DMA((4,)),
     ]
 
 
@@ -324,7 +349,7 @@
     return pl.pallas_call(
         kernel,
         out_shape=jax.ShapeDtypeStruct((2 * nb * parts, BLK), F32),
-        in_specs=[SM, SM] + [VM] * 5,
+        in_specs=[SM, SM, VM] + [pl.BlockSpec(memory_space=pl.ANY)] * 4,
         out_specs=VM,
         scratch_shapes=scratch,
         name="solve",

time: 124 us -> 122 us (0.984)
  Pallas kernels: 22.6 us -> 21.3 us
    pallas_call x1, Pallas kernels: 15.2 us -> 13.9 us  [solve_call(): pl.pallas_call(kernel, out_shape=jax.ShapeDtypeStruct((2 * nb * parts, BL...]
where the time goes in v7:
time: 122 us
  waiting for transfers between devices  46.3 us (38%)
  starting transfers between devices  37.4 us (31%)
  Pallas kernels  21.3 us (17%)
  blocking collectives  12 us (10%)
  local copies, waits for them, and re-layouts  3.33 us (3%)
    all_to_all x1, starting transfers between devices, local(): lax.all_to_all(sent, group, split_axis=0, concat_axis=0, tiled=True)  20.9 us
    all_to_all x1, waiting for transfers between devices, local(): lax.all_to_all(spread, group + ('coord',), split_axis=0, concat_axis=0, t...  17.8 us
    all_to_all x1, waiting for transfers between devices, local(): lax.all_to_all(solved.reshape(tm, 2, BLK), group, split_axis=0, concat_ax...  14.5 us
    all_to_all x1, waiting for transfers between devices, local(): lax.all_to_all(sent, group, split_axis=0, concat_axis=0, tiled=True)  14 us
    pallas_call x1, Pallas kernels, solve_call(): pl.pallas_call(kernel, out_shape=jax.ShapeDtypeStruct((2 * nb * parts, BL...  13.9 us
    all_to_all x1, blocking collectives, local(): lax.all_to_all(rows.reshape(high, 2, BLK), 'high', split_axis=0, concat_a...  12 us
    all_to_all x1, starting transfers between devices, local(): lax.all_to_all(spread, group + ('coord',), split_axis=0, concat_axis=0, t...  9.31 us
    all_to_all x1, starting transfers between devices, local(): lax.all_to_all(solved.reshape(tm, 2, BLK), group, split_axis=0, concat_ax...  7.27 us
  transfers between devices with their start and end apart: 3, of which 3 were waited for; matrix products, arithmetic and copies ran while one was open for 2% of the time, Pallas kernels for 3%

profile of v7, /device:TPU:1, one launch (start us, length us, event | category | flops | bytes accessed | tf_op | source)
XLA Modules:
  0.0 121.7 jit_solution(14031280959500147111)
XLA Ops:
  0.6 0.0 copy-start.5
  0.6 1.6 %gather.1 = f32[128,2,128]{2,1,0:T(2,128)} custom-call(f32[32,2,128]{2,1,0:T(2,128)} %bitcast.49, f32[32,2,128]{2,1,0:T(2,128)} %bitcast.63, f32[4,2,128]{2,1,0:T(2,128)} %bitcast.52), custom_call_target="tpu_custom_call" | custom-call | tf_op jit(solution)/shard_map/gather/pallas_call | solution.py:368
  2.2 20.9 %all-to-all-start = ((f32[128,2,128]{2,1,0:T(2,128)}), f32[128,2,128]{2,1,0:T(2,128)S(1)}, u32[]{:S(2)}, u32[]{:S(2)}) async-start(f32[128,2,128]{2,1,0:T(2,128)} %gather.1), calls=%async_computation | async-start | bytes 262144 | tf_op jit(solution)/shard_map/all_to_all | solution.py:424
  23.1 1.4 %extra.1 = f32[2,128]{1,0:T(2,128)} custom-call(s32[1]{0:T(128)} %bitcast.10.at_ref, f32[32,128]{1,0:T(8,128)} %bitcast.65, f32[32,128]{1,0:T(8,128)} %bitcast.66, f32[32,128]{1,0:T(8,128)} %bitcast.67, f32[4,128]{1,0:T(4,128)} %bitcast.54, s32[3,32]{1,0:T(4,128)} %bitcast.68, s32[3,32]{1,0:T(4,128)} %bitcast.69, s32[4,4]{1,0:T(4,128)} %cols_ref.1, ...), custom_call_target="tpu_custom_call" | custom-call | tf_op jit(solution)/shard_map/extra/pallas_call | solution.py:380
  24.5 14.0 %all-to-all-done = f32[128,2,128]{2,1,0:T(2,128)S(1)} async-done(((f32[128,2,128]{2,1,0:T(2,128)}), f32[128,2,128]{2,1,0:T(2,128)S(1)}, u32[]{:S(2)}, u32[]{:S(2)}) %all-to-all-start) | async-done | bytes 131104 | tf_op jit(solution)/shard_map/all_to_all | solution.py:424
  38.4 0.0 copy-done.5
  38.5 0.4 fusion.2
  38.8 0.3 copy-done.6
  39.2 0.9 broadcast_in_dim.16
  40.1 9.3 %all-to-all-start.1 = ((f32[512,2,128]{2,1,0:T(2,128)}), f32[512,2,128]{2,1,0:T(2,128)S(1)}, u32[]{:S(2)}, u32[]{:S(2)}) async-start(f32[512,2,128]{2,1,0:T(2,128)} %bitcast.17), calls=%async_computation.1 | async-start | bytes 1048576 | tf_op jit(solution)/shard_map/all_to_all | solution.py:446
  49.4 2.8 %bank.1 = (bf16[16,128,128]{2,1,0:T(8,128)(2,1)}, bf16[16,128,128]{2,1,0:T(8,128)(2,1)}, bf16[16,128,128]{2,1,0:T(8,128)(2,1)}, bf16[16,128,128]{2,1,0:T(8,128)(2,1)}) custom-call(f32[16,128,128]{2,1,0:T(8,128)} %bank_ref.1), custom_call_target="tpu_custom_call" | custom-call | tf_op jit(solution)/shard_map/bank/pallas_call | solution.py:361
  52.2 1.2 dynamic-slice_bitcast_fusion.fac_ref
  53.4 17.8 %all-to-all-done.1 = f32[512,2,128]{2,1,0:T(2,128)S(1)} async-done(((f32[512,2,128]{2,1,0:T(2,128)}), f32[512,2,128]{2,1,0:T(2,128)S(1)}, u32[]{:S(2)}, u32[]{:S(2)}) %all-to-all-start.1) | async-done | bytes 524320 | tf_op jit(solution)/shard_map/all_to_all | solution.py:446
  71.3 13.9 %solve.1 = f32[256,128]{1,0:T(8,128)} custom-call(f32[4]{0:T(128)} %dynamic-slice_bitcast_fusion.fac_ref, s32[1]{0:T(128)} %bitcast.1.own_ref, f32[1024,128]{1,0:T(8,128)S(1)} %bitcast.48, bf16[16,128,128]{2,1,0:T(8,128)(2,1)} %get-tuple-element.12.w1_hbm.w1, bf16[16,128,128]{2,1,0:T(8,128)(2,1)} %get-tuple-element.13.w2_hbm.w2, ...), custom_call_target="tpu_custom_call" | custom-call | tf_op jit(solution)/shard_map/solve/pallas_call | solution.py:349
  85.1 0.0 copy-start
  85.1 7.3 %all-to-all-start.2 = ((f32[128,2,128]{2,1,0:T(2,128)}), f32[128,2,128]{2,1,0:T(2,128)S(1)}, u32[]{:S(2)}, u32[]{:S(2)}) async-start(f32[128,2,128]{2,1,0:T(2,128)} %bitcast.58), calls=%async_computation.2 | async-start | bytes 262144 | tf_op jit(solution)/shard_map/all_to_all | solution.py:457
  92.4 0.9 constant_dynamic-slice_fusion
  93.3 14.5 %all-to-all-done.2 = f32[128,2,128]{2,1,0:T(2,128)S(1)} async-done(((f32[128,2,128]{2,1,0:T(2,128)}), f32[128,2,128]{2,1,0:T(2,128)S(1)}, u32[]{:S(2)}, u32[]{:S(2)}) %all-to-all-start.2) | async-done | bytes 131104 | tf_op jit(solution)/shard_map/all_to_all | solution.py:457
  107.8 0.2 fusion.3
  108.0 0.0 copy-start.2
  108.0 12.0 %all_to_all.20 = f32[32,2,128]{2,1,0:T(2,128)S(1)} all-to-all(f32[32,2,128]{2,1,0:T(2,128)S(1)} %bitcast.62), channel_id=1, replica_groups=mesh['high'=32,'low'=4,'coord'=4] {'high'}, dimensions={0} | all-to-all | bytes 65536 | tf_op jit(solution)/shard_map/all_to_all | solution.py:473
  120.0 0.0 copy-done.1
  120.0 0.0 copy-done
  120.0 1.7 %finish.1 = (f32[64,128]{1,0:T(8,128)}, f32[8,128]{1,0:T(8,128)}) custom-call(s32[4,4]{1,0:T(4,128)} %cols_ref.1, s32[4,4]{1,0:T(4,128)} %tiles_ref.1, f32[64,128]{1,0:T(8,128)S(1)} %bitcast.50, f32[8,128]{1,0:T(8,128)S(1)} %bitcast.53, f32[4,128]{1,0:T(4,128)S(1)} %bitcast.55, f32[64,128]{1,0:T(8,128)S(1)} %bitcast.51, bf16[16,128,128]{2,1,0:T(8,128)(2,1)S(1)} %copy-done, ...), custom_call_target="tpu_custom_call" | custom-call | tf_op jit(solution)/shard_map/finish/pallas_call | solution.py:391
  (11 shorter events, 0.0 us)
Async XLA Ops:
  0.6 37.8 %copy-start.5 = (f32[256,256]{1,0:T(8,128)S(1)}, f32[256,256]{1,0:T(8,128)}, u32[]{:S(2)}) copy-start(f32[256,256]{1,0:T(8,128)} %constant.43.clone) | copy-start | bytes 786436
  2.2 36.2 %all-to-all-start = ((f32[128,2,128]{2,1,0:T(2,128)}), f32[128,2,128]{2,1,0:T(2,128)S(1)}, u32[]{:S(2)}, u32[]{:S(2)}) async-start(f32[128,2,128]{2,1,0:T(2,128)} %gather.1), calls=%async_computation | async-start | bytes 262144 | tf_op jit(solution)/shard_map/all_to_all | solution.py:424
  38.5 0.7 copy-start.6
  40.1 31.1 %all-to-all-start.1 = ((f32[512,2,128]{2,1,0:T(2,128)}), f32[512,2,128]{2,1,0:T(2,128)S(1)}, u32[]{:S(2)}, u32[]{:S(2)}) async-start(f32[512,2,128]{2,1,0:T(2,128)} %bitcast.17), calls=%async_computation.1 | async-start | bytes 1048576 | tf_op jit(solution)/shard_map/all_to_all | solution.py:446
  71.3 48.7 %copy-start.1 = (bf16[16,128,128]{2,1,0:T(8,128)(2,1)S(1)}, bf16[16,128,128]{2,1,0:T(8,128)(2,1)}, u32[]{:S(2)}) copy-start(bf16[16,128,128]{2,1,0:T(8,128)(2,1)} %get-tuple-element.13.w2_hbm.w2) | copy-start | bytes 1572868
  85.1 34.9 %copy-start = (bf16[16,128,128]{2,1,0:T(8,128)(2,1)S(1)}, bf16[16,128,128]{2,1,0:T(8,128)(2,1)}, u32[]{:S(2)}) copy-start(bf16[16,128,128]{2,1,0:T(8,128)(2,1)} %get-tuple-element.12.w1_hbm.w1) | copy-start | bytes 1572868
  85.1 22.6 %all-to-all-start.2 = ((f32[128,2,128]{2,1,0:T(2,128)}), f32[128,2,128]{2,1,0:T(2,128)S(1)}, u32[]{:S(2)}, u32[]{:S(2)}) async-start(f32[128,2,128]{2,1,0:T(2,128)} %bitcast.58), calls=%async_computation.2 | async-start | bytes 262144 | tf_op jit(solution)/shard_map/all_to_all | solution.py:457
  107.8 12.2 %copy-start.3 = (f32[2,512]{1,0:T(2,128)S(1)}, f32[2,512]{1,0:T(2,128)}, u32[]{:S(2)}) copy-start(f32[2,512]{1,0:T(2,128)} %param.16) | copy-start | bytes 12292
  107.8 12.2 %copy-start.4 = (f32[512]{0:T(512)S(1)}, f32[512]{0:T(512)}, u32[]{:S(2)}) copy-start(f32[512]{0:T(512)} %param.21) | copy-start | bytes 6148
  108.0 12.0 %copy-start.2 = (f32[2,4096]{1,0:T(2,128)S(1)}, f32[2,4096]{1,0:T(2,128)}, u32[]{:S(2)}) copy-start(f32[2,4096]{1,0:T(2,128)} %param.15) | copy-start | bytes 98308

commit v8 on v7

--- a/solution.py
+++ b/solution.py
@@ -110,12 +110,12 @@
             [new_state[pl.ds(cols_ref[c, j] * 2, 2), :] for c in range(ncb)], axis=0
         )
         high, mid, _ = split3(value)
-        two = jnp.concatenate([high, mid], axis=1)
+        stack = jnp.concatenate([high, mid], axis=0)
+        stack = jnp.concatenate([stack, stack], axis=1)
         for c in range(ncb):
-            b1, b2 = w1[tiles_ref[c, j]], w2[tiles_ref[c, j]]
-            res = jnp.dot(two, jnp.concatenate([b1, b1]), preferred_element_type=F32)
-            res += jnp.dot(two, jnp.concatenate([b2, b2]), preferred_element_type=F32)
-            total += jnp.where(owner == c, res, 0.0)
+            both = jnp.concatenate([w1[tiles_ref[c, j]], w2[tiles_ref[c, j]]])
+            res = jnp.dot(stack, both, preferred_element_type=F32)
+            total += jnp.where(owner == c, res[: 2 * ncb] + res[2 * ncb :], 0.0)
     weight = jnp.zeros(mult.shape, F32)
     for c in range(ncb):
         weight = jnp.where(owner == c, stab[c : c + 1], weight)
@@ -256,15 +256,17 @@
             c_ref[rows] = cross * inv
             rhs[rows] = part("force", chunk, start) + wrap - (d_self * state + cross * swapped(state))
 
-        def advance(first):
+        def advance(first, full):
             for i in range(nrow // chunk):
                 rows = slice(i * chunk, i * chunk + chunk)
                 res = rhs[rows] - coupled(rows)
                 if first:
                     rhs[rows] = res
                 value = e_ref[rows] * res - c_ref[rows] * swapped(res)
-                xs[rows] = value
-                xt[rows, :BLK], xt[rows, BLK:], xl[rows] = split3(value)
+                xt[rows, :BLK], xt[rows, BLK:], low = split3(value)
+                if full:
+                    xs[rows] = value
+                    xl[rows] = low
 
         mult = part("mult", crow)
         shalf = part("stab", crow // 2)
@@ -282,21 +284,22 @@
         constrain()
         scatter()
         sc[...] = stab * mult - gy[...]
-        advance(True)
-
-        def sweep(low):
+        advance(True, False)
+
+        def sweep(low, full):
             x3 = xl[...] if low else None
             products(xt[:, :BLK], xt[:, BLK:], x3, (w1, w2), p_ref, lambda i: None)
             constrain()
             products(*split3((gy[...] - sc[...]) * istab[...]), (v1, v2), q_ref, couple)
             scatter()
-            advance(False)
-
-        def loop(count, low):
-            lax.fori_loop(0, count, lambda i, carry: (sweep(low), carry)[1], 0)
-
-        loop(SWEEPS - 1 - FULL, False)
-        loop(FULL, True)
+            advance(False, full)
+
+        def loop(count, low, full):
+            lax.fori_loop(0, count, lambda i, carry: (sweep(low, full), carry)[1], 0)
+
+        loop(SWEEPS - 2 - FULL, False, False)
+        sweep(False, True)
+        loop(FULL, True, True)
         own = own_ref[0]
         parts = out_ref.shape[0] // (2 * nb)
         for b in range(nb):

time: 122 us -> 122 us (level)
  no operation moved by 1% of the time
where the time goes in v8:
time: 122 us
  waiting for transfers between devices  46.3 us (38%)
  starting transfers between devices  37.4 us (31%)
  Pallas kernels  21.1 us (17%)
  blocking collectives  12 us (10%)
  local copies, waits for them, and re-layouts  3.33 us (3%)
    all_to_all x1, starting transfers between devices, local(): lax.all_to_all(sent, group, split_axis=0, concat_axis=0, tiled=True)  20.9 us
    all_to_all x1, waiting for transfers between devices, local(): lax.all_to_all(spread, group + ('coord',), split_axis=0, concat_axis=0, t...  17.8 us
    all_to_all x1, waiting for transfers between devices, local(): lax.all_to_all(solved.reshape(tm, 2, BLK), group, split_axis=0, concat_ax...  14.5 us
    all_to_all x1, waiting for transfers between devices, local(): lax.all_to_all(sent, group, split_axis=0, concat_axis=0, tiled=True)  14 us
    pallas_call x1, Pallas kernels, solve_call(): pl.pallas_call(kernel, out_shape=jax.ShapeDtypeStruct((2 * nb * parts, BL...  13.9 us
    all_to_all x1, blocking collectives, local(): lax.all_to_all(rows.reshape(high, 2, BLK), 'high', split_axis=0, concat_a...  12 us
    all_to_all x1, starting transfers between devices, local(): lax.all_to_all(spread, group + ('coord',), split_axis=0, concat_axis=0, t...  9.31 us
    all_to_all x1, starting transfers between devices, local(): lax.all_to_all(solved.reshape(tm, 2, BLK), group, split_axis=0, concat_ax...  7.27 us
  transfers between devices with their start and end apart: 3, of which 3 were waited for; matrix products, arithmetic and copies ran while one was open for 2% of the time, Pallas kernels for 3%

profile of v8, /device:TPU:1, one launch (start us, length us, event | category | flops | bytes accessed | tf_op | source)
XLA Modules:
  0.0 121.6 jit_solution(1644302904186843587)
XLA Ops:
  0.6 0.0 copy-start.5
  0.6 1.6 %gather.1 = f32[128,2,128]{2,1,0:T(2,128)} custom-call(f32[32,2,128]{2,1,0:T(2,128)} %bitcast.49, f32[32,2,128]{2,1,0:T(2,128)} %bitcast.63, f32[4,2,128]{2,1,0:T(2,128)} %bitcast.52), custom_call_target="tpu_custom_call" | custom-call | tf_op jit(solution)/shard_map/gather/pallas_call | solution.py:371
  2.2 20.9 %all-to-all-start = ((f32[128,2,128]{2,1,0:T(2,128)}), f32[128,2,128]{2,1,0:T(2,128)S(1)}, u32[]{:S(2)}, u32[]{:S(2)}) async-start(f32[128,2,128]{2,1,0:T(2,128)} %gather.1), calls=%async_computation | async-start | bytes 262144 | tf_op jit(solution)/shard_map/all_to_all | solution.py:427
  23.1 1.4 %extra.1 = f32[2,128]{1,0:T(2,128)} custom-call(s32[1]{0:T(128)} %bitcast.10.at_ref, f32[32,128]{1,0:T(8,128)} %bitcast.65, f32[32,128]{1,0:T(8,128)} %bitcast.66, f32[32,128]{1,0:T(8,128)} %bitcast.67, f32[4,128]{1,0:T(4,128)} %bitcast.54, s32[3,32]{1,0:T(4,128)} %bitcast.68, s32[3,32]{1,0:T(4,128)} %bitcast.69, s32[4,4]{1,0:T(4,128)} %cols_ref.1, ...), custom_call_target="tpu_custom_call" | custom-call | tf_op jit(solution)/shard_map/extra/pallas_call | solution.py:383
  24.5 14.0 %all-to-all-done = f32[128,2,128]{2,1,0:T(2,128)S(1)} async-done(((f32[128,2,128]{2,1,0:T(2,128)}), f32[128,2,128]{2,1,0:T(2,128)S(1)}, u32[]{:S(2)}, u32[]{:S(2)}) %all-to-all-start) | async-done | bytes 131104 | tf_op jit(solution)/shard_map/all_to_all | solution.py:427
  38.4 0.0 copy-done.5
  38.5 0.4 fusion.2
  38.8 0.3 copy-done.6
  39.2 0.9 broadcast_in_dim.16
  40.1 9.3 %all-to-all-start.1 = ((f32[512,2,128]{2,1,0:T(2,128)}), f32[512,2,128]{2,1,0:T(2,128)S(1)}, u32[]{:S(2)}, u32[]{:S(2)}) async-start(f32[512,2,128]{2,1,0:T(2,128)} %bitcast.17), calls=%async_computation.1 | async-start | bytes 1048576 | tf_op jit(solution)/shard_map/all_to_all | solution.py:449
  49.4 2.8 %bank.1 = (bf16[16,128,128]{2,1,0:T(8,128)(2,1)}, bf16[16,128,128]{2,1,0:T(8,128)(2,1)}, bf16[16,128,128]{2,1,0:T(8,128)(2,1)}, bf16[16,128,128]{2,1,0:T(8,128)(2,1)}) custom-call(f32[16,128,128]{2,1,0:T(8,128)} %bank_ref.1), custom_call_target="tpu_custom_call" | custom-call | tf_op jit(solution)/shard_map/bank/pallas_call | solution.py:364
  52.2 1.2 dynamic-slice_bitcast_fusion.fac_ref
  53.4 17.8 %all-to-all-done.1 = f32[512,2,128]{2,1,0:T(2,128)S(1)} async-done(((f32[512,2,128]{2,1,0:T(2,128)}), f32[512,2,128]{2,1,0:T(2,128)S(1)}, u32[]{:S(2)}, u32[]{:S(2)}) %all-to-all-start.1) | async-done | bytes 524320 | tf_op jit(solution)/shard_map/all_to_all | solution.py:449
  71.3 13.9 %solve.1 = f32[256,128]{1,0:T(8,128)} custom-call(f32[4]{0:T(128)} %dynamic-slice_bitcast_fusion.fac_ref, s32[1]{0:T(128)} %bitcast.1.own_ref, f32[1024,128]{1,0:T(8,128)S(1)} %bitcast.48, bf16[16,128,128]{2,1,0:T(8,128)(2,1)} %get-tuple-element.12.w1_hbm.w1, bf16[16,128,128]{2,1,0:T(8,128)(2,1)} %get-tuple-element.13.w2_hbm.w2, ...), custom_call_target="tpu_custom_call" | custom-call | tf_op jit(solution)/shard_map/solve/pallas_call | solution.py:352
  85.1 0.0 copy-start
  85.1 7.3 %all-to-all-start.2 = ((f32[128,2,128]{2,1,0:T(2,128)}), f32[128,2,128]{2,1,0:T(2,128)S(1)}, u32[]{:S(2)}, u32[]{:S(2)}) async-start(f32[128,2,128]{2,1,0:T(2,128)} %bitcast.58), calls=%async_computation.2 | async-start | bytes 262144 | tf_op jit(solution)/shard_map/all_to_all | solution.py:460
  92.4 0.9 constant_dynamic-slice_fusion
  93.3 14.5 %all-to-all-done.2 = f32[128,2,128]{2,1,0:T(2,128)S(1)} async-done(((f32[128,2,128]{2,1,0:T(2,128)}), f32[128,2,128]{2,1,0:T(2,128)S(1)}, u32[]{:S(2)}, u32[]{:S(2)}) %all-to-all-start.2) | async-done | bytes 131104 | tf_op jit(solution)/shard_map/all_to_all | solution.py:460
  107.8 0.2 fusion.3
  108.0 0.0 copy-start.2
  108.0 12.0 %all_to_all.20 = f32[32,2,128]{2,1,0:T(2,128)S(1)} all-to-all(f32[32,2,128]{2,1,0:T(2,128)S(1)} %bitcast.62), channel_id=1, replica_groups=mesh['high'=32,'low'=4,'coord'=4] {'high'}, dimensions={0} | all-to-all | bytes 65536 | tf_op jit(solution)/shard_map/all_to_all | solution.py:476
  120.0 0.0 copy-done.1
  120.0 0.0 copy-done.3
  120.0 1.6 %finish.1 = (f32[64,128]{1,0:T(8,128)}, f32[8,128]{1,0:T(8,128)}) custom-call(s32[4,4]{1,0:T(4,128)} %cols_ref.1, s32[4,4]{1,0:T(4,128)} %tiles_ref.1, f32[64,128]{1,0:T(8,128)S(1)} %bitcast.50, f32[8,128]{1,0:T(8,128)S(1)} %bitcast.53, f32[4,128]{1,0:T(4,128)S(1)} %bitcast.55, f32[64,128]{1,0:T(8,128)S(1)} %bitcast.51, bf16[16,128,128]{2,1,0:T(8,128)(2,1)S(1)} %copy-done, ...), custom_call_target="tpu_custom_call" | custom-call | tf_op jit(solution)/shard_map/finish/pallas_call | solution.py:394
  (11 shorter events, 0.0 us)
Async XLA Ops:
  0.6 37.8 %copy-start.5 = (f32[256,256]{1,0:T(8,128)S(1)}, f32[256,256]{1,0:T(8,128)}, u32[]{:S(2)}) copy-start(f32[256,256]{1,0:T(8,128)} %constant.43.clone) | copy-start | bytes 786436
  2.2 36.2 %all-to-all-start = ((f32[128,2,128]{2,1,0:T(2,128)}), f32[128,2,128]{2,1,0:T(2,128)S(1)}, u32[]{:S(2)}, u32[]{:S(2)}) async-start(f32[128,2,128]{2,1,0:T(2,128)} %gather.1), calls=%async_computation | async-start | bytes 262144 | tf_op jit(solution)/shard_map/all_to_all | solution.py:427
  38.5 0.7 copy-start.6
  40.1 31.1 %all-to-all-start.1 = ((f32[512,2,128]{2,1,0:T(2,128)}), f32[512,2,128]{2,1,0:T(2,128)S(1)}, u32[]{:S(2)}, u32[]{:S(2)}) async-start(f32[512,2,128]{2,1,0:T(2,128)} %bitcast.17), calls=%async_computation.1 | async-start | bytes 1048576 | tf_op jit(solution)/shard_map/all_to_all | solution.py:449
  71.3 48.7 %copy-start.1 = (bf16[16,128,128]{2,1,0:T(8,128)(2,1)S(1)}, bf16[16,128,128]{2,1,0:T(8,128)(2,1)}, u32[]{:S(2)}) copy-start(bf16[16,128,128]{2,1,0:T(8,128)(2,1)} %get-tuple-element.13.w2_hbm.w2) | copy-start | bytes 1572868
  85.1 34.9 %copy-start = (bf16[16,128,128]{2,1,0:T(8,128)(2,1)S(1)}, bf16[16,128,128]{2,1,0:T(8,128)(2,1)}, u32[]{:S(2)}) copy-start(bf16[16,128,128]{2,1,0:T(8,128)(2,1)} %get-tuple-element.12.w1_hbm.w1) | copy-start | bytes 1572868
  85.1 22.6 %all-to-all-start.2 = ((f32[128,2,128]{2,1,0:T(2,128)}), f32[128,2,128]{2,1,0:T(2,128)S(1)}, u32[]{:S(2)}, u32[]{:S(2)}) async-start(f32[128,2,128]{2,1,0:T(2,128)} %bitcast.58), calls=%async_computation.2 | async-start | bytes 262144 | tf_op jit(solution)/shard_map/all_to_all | solution.py:460
  107.8 12.2 %copy-start.3 = (f32[2,512]{1,0:T(2,128)S(1)}, f32[2,512]{1,0:T(2,128)}, u32[]{:S(2)}) copy-start(f32[2,512]{1,0:T(2,128)} %param.16) | copy-start | bytes 12292
  107.8 12.2 %copy-start.4 = (f32[512]{0:T(512)S(1)}, f32[512]{0:T(512)}, u32[]{:S(2)}) copy-start(f32[512]{0:T(512)} %param.21) | copy-start | bytes 6148
  108.0 12.0 %copy-start.2 = (f32[2,4096]{1,0:T(2,128)S(1)}, f32[2,4096]{1,0:T(2,128)}, u32[]{:S(2)}) copy-start(f32[2,4096]{1,0:T(2,128)} %param.15) | copy-start | bytes 98308

commit v9 on v8

--- a/solution.py
+++ b/solution.py
@@ -11,7 +11,7 @@
 BLK = 128
 REACH = 2
 SWEEPS = 8
-FULL = 3
+FULL = 2
 ALPHA = 0.001
 HIGHEST = lax.Precision.HIGHEST
 F32 = jnp.float32

time: 122 us -> 122 us (level)
  no operation moved by 1% of the time
where the time goes in v9:
time: 122 us; the launch traced here: 121 us
  waiting for transfers between devices  46.3 us (38%)
  starting transfers between devices  37.4 us (31%)
  Pallas kernels  20.8 us (17%)
  blocking collectives  12 us (10%)
  local copies, waits for them, and re-layouts  3.33 us (3%)
    all_to_all x1, starting transfers between devices, local(): lax.all_to_all(sent, group, split_axis=0, concat_axis=0, tiled=True)  20.9 us
    all_to_all x1, waiting for transfers between devices, local(): lax.all_to_all(spread, group + ('coord',), split_axis=0, concat_axis=0, t...  17.8 us
    all_to_all x1, waiting for transfers between devices, local(): lax.all_to_all(solved.reshape(tm, 2, BLK), group, split_axis=0, concat_ax...  14.5 us
    all_to_all x1, waiting for transfers between devices, local(): lax.all_to_all(sent, group, split_axis=0, concat_axis=0, tiled=True)  14 us
    pallas_call x1, Pallas kernels, solve_call(): pl.pallas_call(kernel, out_shape=jax.ShapeDtypeStruct((2 * nb * parts, BL...  13.6 us
    all_to_all x1, blocking collectives, local(): lax.all_to_all(rows.reshape(high, 2, BLK), 'high', split_axis=0, concat_a...  12 us
    all_to_all x1, starting transfers between devices, local(): lax.all_to_all(spread, group + ('coord',), split_axis=0, concat_axis=0, t...  9.31 us
    all_to_all x1, starting transfers between devices, local(): lax.all_to_all(solved.reshape(tm, 2, BLK), group, split_axis=0, concat_ax...  7.27 us
  transfers between devices with their start and end apart: 3, of which 3 were waited for; matrix products, arithmetic and copies ran while one was open for 2% of the time, Pallas kernels for 3%

profile of v9, /device:TPU:1, one launch (start us, length us, event | category | flops | bytes accessed | tf_op | source)
XLA Modules:
  0.0 121.3 jit_solution(11909241220619183242)
XLA Ops:
  0.6 0.0 copy-start.5
  0.6 1.6 %gather.1 = f32[128,2,128]{2,1,0:T(2,128)} custom-call(f32[32,2,128]{2,1,0:T(2,128)} %bitcast.49, f32[32,2,128]{2,1,0:T(2,128)} %bitcast.63, f32[4,2,128]{2,1,0:T(2,128)} %bitcast.52), custom_call_target="tpu_custom_call" | custom-call | tf_op jit(solution)/shard_map/gather/pallas_call | solution.py:371
  2.2 20.9 %all-to-all-start = ((f32[128,2,128]{2,1,0:T(2,128)}), f32[128,2,128]{2,1,0:T(2,128)S(1)}, u32[]{:S(2)}, u32[]{:S(2)}) async-start(f32[128,2,128]{2,1,0:T(2,128)} %gather.1), calls=%async_computation | async-start | bytes 262144 | tf_op jit(solution)/shard_map/all_to_all | solution.py:427
  23.1 1.4 %extra.1 = f32[2,128]{1,0:T(2,128)} custom-call(s32[1]{0:T(128)} %bitcast.10.at_ref, f32[32,128]{1,0:T(8,128)} %bitcast.65, f32[32,128]{1,0:T(8,128)} %bitcast.66, f32[32,128]{1,0:T(8,128)} %bitcast.67, f32[4,128]{1,0:T(4,128)} %bitcast.54, s32[3,32]{1,0:T(4,128)} %bitcast.68, s32[3,32]{1,0:T(4,128)} %bitcast.69, s32[4,4]{1,0:T(4,128)} %cols_ref.1, ...), custom_call_target="tpu_custom_call" | custom-call | tf_op jit(solution)/shard_map/extra/pallas_call | solution.py:383
  24.5 14.0 %all-to-all-done = f32[128,2,128]{2,1,0:T(2,128)S(1)} async-done(((f32[128,2,128]{2,1,0:T(2,128)}), f32[128,2,128]{2,1,0:T(2,128)S(1)}, u32[]{:S(2)}, u32[]{:S(2)}) %all-to-all-start) | async-done | bytes 131104 | tf_op jit(solution)/shard_map/all_to_all | solution.py:427
  38.4 0.0 copy-done.5
  38.5 0.4 fusion.2
  38.8 0.3 copy-done.6
  39.2 0.9 broadcast_in_dim.16
  40.1 9.3 %all-to-all-start.1 = ((f32[512,2,128]{2,1,0:T(2,128)}), f32[512,2,128]{2,1,0:T(2,128)S(1)}, u32[]{:S(2)}, u32[]{:S(2)}) async-start(f32[512,2,128]{2,1,0:T(2,128)} %bitcast.17), calls=%async_computation.1 | async-start | bytes 1048576 | tf_op jit(solution)/shard_map/all_to_all | solution.py:449
  49.4 2.8 %bank.1 = (bf16[16,128,128]{2,1,0:T(8,128)(2,1)}, bf16[16,128,128]{2,1,0:T(8,128)(2,1)}, bf16[16,128,128]{2,1,0:T(8,128)(2,1)}, bf16[16,128,128]{2,1,0:T(8,128)(2,1)}) custom-call(f32[16,128,128]{2,1,0:T(8,128)} %bank_ref.1), custom_call_target="tpu_custom_call" | custom-call | tf_op jit(solution)/shard_map/bank/pallas_call | solution.py:364
  52.2 1.2 dynamic-slice_bitcast_fusion.fac_ref
  53.4 17.8 %all-to-all-done.1 = f32[512,2,128]{2,1,0:T(2,128)S(1)} async-done(((f32[512,2,128]{2,1,0:T(2,128)}), f32[512,2,128]{2,1,0:T(2,128)S(1)}, u32[]{:S(2)}, u32[]{:S(2)}) %all-to-all-start.1) | async-done | bytes 524320 | tf_op jit(solution)/shard_map/all_to_all | solution.py:449
  71.3 13.6 %solve.1 = f32[256,128]{1,0:T(8,128)} custom-call(f32[4]{0:T(128)} %dynamic-slice_bitcast_fusion.fac_ref, s32[1]{0:T(128)} %bitcast.1.own_ref, f32[1024,128]{1,0:T(8,128)S(1)} %bitcast.48, bf16[16,128,128]{2,1,0:T(8,128)(2,1)} %get-tuple-element.12.w1_hbm.w1, bf16[16,128,128]{2,1,0:T(8,128)(2,1)} %get-tuple-element.13.w2_hbm.w2, ...), custom_call_target="tpu_custom_call" | custom-call | tf_op jit(solution)/shard_map/solve/pallas_call | solution.py:352
  84.8 0.0 copy-start
  84.8 7.3 %all-to-all-start.2 = ((f32[128,2,128]{2,1,0:T(2,128)}), f32[128,2,128]{2,1,0:T(2,128)S(1)}, u32[]{:S(2)}, u32[]{:S(2)}) async-start(f32[128,2,128]{2,1,0:T(2,128)} %bitcast.58), calls=%async_computation.2 | async-start | bytes 262144 | tf_op jit(solution)/shard_map/all_to_all | solution.py:460
  92.1 0.9 constant_dynamic-slice_fusion
  93.0 14.5 %all-to-all-done.2 = f32[128,2,128]{2,1,0:T(2,128)S(1)} async-done(((f32[128,2,128]{2,1,0:T(2,128)}), f32[128,2,128]{2,1,0:T(2,128)S(1)}, u32[]{:S(2)}, u32[]{:S(2)}) %all-to-all-start.2) | async-done | bytes 131104 | tf_op jit(solution)/shard_map/all_to_all | solution.py:460
  107.5 0.2 fusion.3
  107.7 0.0 copy-start.2
  107.7 12.0 %all_to_all.20 = f32[32,2,128]{2,1,0:T(2,128)S(1)} all-to-all(f32[32,2,128]{2,1,0:T(2,128)S(1)} %bitcast.62), channel_id=1, replica_groups=mesh['high'=32,'low'=4,'coord'=4] {'high'}, dimensions={0} | all-to-all | bytes 65536 | tf_op jit(solution)/shard_map/all_to_all | solution.py:476
  119.7 0.0 copy-done.1
  119.7 0.0 copy-done
  119.7 1.6 %finish.1 = (f32[64,128]{1,0:T(8,128)}, f32[8,128]{1,0:T(8,128)}) custom-call(s32[4,4]{1,0:T(4,128)} %cols_ref.1, s32[4,4]{1,0:T(4,128)} %tiles_ref.1, f32[64,128]{1,0:T(8,128)S(1)} %bitcast.50, f32[8,128]{1,0:T(8,128)S(1)} %bitcast.53, f32[4,128]{1,0:T(4,128)S(1)} %bitcast.55, f32[64,128]{1,0:T(8,128)S(1)} %bitcast.51, bf16[16,128,128]{2,1,0:T(8,128)(2,1)S(1)} %copy-done, ...), custom_call_target="tpu_custom_call" | custom-call | tf_op jit(solution)/shard_map/finish/pallas_call | solution.py:394
  (11 shorter events, 0.0 us)
Async XLA Ops:
  0.6 37.8 %copy-start.5 = (f32[256,256]{1,0:T(8,128)S(1)}, f32[256,256]{1,0:T(8,128)}, u32[]{:S(2)}) copy-start(f32[256,256]{1,0:T(8,128)} %constant.43.clone) | copy-start | bytes 786436
  2.2 36.2 %all-to-all-start = ((f32[128,2,128]{2,1,0:T(2,128)}), f32[128,2,128]{2,1,0:T(2,128)S(1)}, u32[]{:S(2)}, u32[]{:S(2)}) async-start(f32[128,2,128]{2,1,0:T(2,128)} %gather.1), calls=%async_computation | async-start | bytes 262144 | tf_op jit(solution)/shard_map/all_to_all | solution.py:427
  38.5 0.7 copy-start.6
  40.1 31.1 %all-to-all-start.1 = ((f32[512,2,128]{2,1,0:T(2,128)}), f32[512,2,128]{2,1,0:T(2,128)S(1)}, u32[]{:S(2)}, u32[]{:S(2)}) async-start(f32[512,2,128]{2,1,0:T(2,128)} %bitcast.17), calls=%async_computation.1 | async-start | bytes 1048576 | tf_op jit(solution)/shard_map/all_to_all | solution.py:449
  71.3 48.4 %copy-start.1 = (bf16[16,128,128]{2,1,0:T(8,128)(2,1)S(1)}, bf16[16,128,128]{2,1,0:T(8,128)(2,1)}, u32[]{:S(2)}) copy-start(bf16[16,128,128]{2,1,0:T(8,128)(2,1)} %get-tuple-element.13.w2_hbm.w2) | copy-start | bytes 1572868
  84.8 34.9 %copy-start = (bf16[16,128,128]{2,1,0:T(8,128)(2,1)S(1)}, bf16[16,128,128]{2,1,0:T(8,128)(2,1)}, u32[]{:S(2)}) copy-start(bf16[16,128,128]{2,1,0:T(8,128)(2,1)} %get-tuple-element.12.w1_hbm.w1) | copy-start | bytes 1572868
  84.8 22.6 %all-to-all-start.2 = ((f32[128,2,128]{2,1,0:T(2,128)}), f32[128,2,128]{2,1,0:T(2,128)S(1)}, u32[]{:S(2)}, u32[]{:S(2)}) async-start(f32[128,2,128]{2,1,0:T(2,128)} %bitcast.58), calls=%async_computation.2 | async-start | bytes 262144 | tf_op jit(solution)/shard_map/all_to_all | solution.py:460
  107.5 12.2 %copy-start.3 = (f32[2,512]{1,0:T(2,128)S(1)}, f32[2,512]{1,0:T(2,128)}, u32[]{:S(2)}) copy-start(f32[2,512]{1,0:T(2,128)} %param.16) | copy-start | bytes 12292
  107.5 12.2 %copy-start.4 = (f32[512]{0:T(512)S(1)}, f32[512]{0:T(512)}, u32[]{:S(2)}) copy-start(f32[512]{0:T(512)} %param.21) | copy-start | bytes 6148
  107.7 12.0 %copy-start.2 = (f32[2,4096]{1,0:T(2,128)S(1)}, f32[2,4096]{1,0:T(2,128)}, u32[]{:S(2)}) copy-start(f32[2,4096]{1,0:T(2,128)} %param.15) | copy-start | bytes 98308

commit v10 on v9

--- a/solution.py
+++ b/solution.py
@@ -295,7 +295,8 @@
             advance(False, full)
 
         def loop(count, low, full):
-            lax.fori_loop(0, count, lambda i, carry: (sweep(low, full), carry)[1], 0)
+            for _ in range(count):
+                sweep(low, full)
 
         loop(SWEEPS - 2 - FULL, False, False)
         sweep(False, True)

time: 122 us -> 123 us (level)
  no operation moved by 1% of the time
where the time goes in v10:
time: 123 us; the launch traced here: 122 us
  waiting for transfers between devices  46.3 us (38%)
  starting transfers between devices  37.5 us (30%)
  Pallas kernels  21.6 us (18%)
  blocking collectives  12 us (10%)
  local copies, waits for them, and re-layouts  3.33 us (3%)
    all_to_all x1, starting transfers between devices, local(): lax.all_to_all(sent, group, split_axis=0, concat_axis=0, tiled=True)  20.9 us
    all_to_all x1, waiting for transfers between devices, local(): lax.all_to_all(spread, group + ('coord',), split_axis=0, concat_axis=0, t...  17.8 us
    all_to_all x1, waiting for transfers between devices, local(): lax.all_to_all(solved.reshape(tm, 2, BLK), group, split_axis=0, concat_ax...  14.5 us
    pallas_call x1, Pallas kernels, solve_call(): pl.pallas_call(kernel, out_shape=jax.ShapeDtypeStruct((2 * nb * parts, BL...  14.3 us
    all_to_all x1, waiting for transfers between devices, local(): lax.all_to_all(sent, group, split_axis=0, concat_axis=0, tiled=True)  14 us
    all_to_all x1, blocking collectives, local(): lax.all_to_all(rows.reshape(high, 2, BLK), 'high', split_axis=0, concat_a...  12 us
    all_to_all x1, starting transfers between devices, local(): lax.all_to_all(spread, group + ('coord',), split_axis=0, concat_axis=0, t...  9.32 us
    all_to_all x1, starting transfers between devices, local(): lax.all_to_all(solved.reshape(tm, 2, BLK), group, split_axis=0, concat_ax...  7.27 us
  transfers between devices with their start and end apart: 3, of which 3 were waited for; matrix products, arithmetic and copies ran while one was open for 2% of the time, Pallas kernels for 3%

profile of v10, /device:TPU:1, one launch (start us, length us, event | category | flops | bytes accessed | tf_op | source)
XLA Modules:
  0.0 122.0 jit_solution(6932111559134531095)
XLA Ops:
  0.6 0.0 copy-start.5
  0.6 1.6 %gather.1 = f32[128,2,128]{2,1,0:T(2,128)} custom-call(f32[32,2,128]{2,1,0:T(2,128)} %bitcast.49, f32[32,2,128]{2,1,0:T(2,128)} %bitcast.63, f32[4,2,128]{2,1,0:T(2,128)} %bitcast.52), custom_call_target="tpu_custom_call" | custom-call | tf_op jit(solution)/shard_map/gather/pallas_call | solution.py:372
  2.2 20.9 %all-to-all-start = ((f32[128,2,128]{2,1,0:T(2,128)}), f32[128,2,128]{2,1,0:T(2,128)S(1)}, u32[]{:S(2)}, u32[]{:S(2)}) async-start(f32[128,2,128]{2,1,0:T(2,128)} %gather.1), calls=%async_computation | async-start | bytes 262144 | tf_op jit(solution)/shard_map/all_to_all | solution.py:428
  23.1 1.4 %extra.1 = f32[2,128]{1,0:T(2,128)} custom-call(s32[1]{0:T(128)} %bitcast.10.at_ref, f32[32,128]{1,0:T(8,128)} %bitcast.65, f32[32,128]{1,0:T(8,128)} %bitcast.66, f32[32,128]{1,0:T(8,128)} %bitcast.67, f32[4,128]{1,0:T(4,128)} %bitcast.54, s32[3,32]{1,0:T(4,128)} %bitcast.68, s32[3,32]{1,0:T(4,128)} %bitcast.69, s32[4,4]{1,0:T(4,128)} %cols_ref.1, ...), custom_call_target="tpu_custom_call" | custom-call | tf_op jit(solution)/shard_map/extra/pallas_call | solution.py:384
  24.5 14.0 %all-to-all-done = f32[128,2,128]{2,1,0:T(2,128)S(1)} async-done(((f32[128,2,128]{2,1,0:T(2,128)}), f32[128,2,128]{2,1,0:T(2,128)S(1)}, u32[]{:S(2)}, u32[]{:S(2)}) %all-to-all-start) | async-done | bytes 131104 | tf_op jit(solution)/shard_map/all_to_all | solution.py:428
  38.4 0.0 copy-done.5
  38.5 0.4 fusion.2
  38.8 0.3 copy-done.6
  39.2 0.9 broadcast_in_dim.16
  40.1 9.3 %all-to-all-start.1 = ((f32[512,2,128]{2,1,0:T(2,128)}), f32[512,2,128]{2,1,0:T(2,128)S(1)}, u32[]{:S(2)}, u32[]{:S(2)}) async-start(f32[512,2,128]{2,1,0:T(2,128)} %bitcast.17), calls=%async_computation.1 | async-start | bytes 1048576 | tf_op jit(solution)/shard_map/all_to_all | solution.py:450
  49.5 2.8 %bank.1 = (bf16[16,128,128]{2,1,0:T(8,128)(2,1)}, bf16[16,128,128]{2,1,0:T(8,128)(2,1)}, bf16[16,128,128]{2,1,0:T(8,128)(2,1)}, bf16[16,128,128]{2,1,0:T(8,128)(2,1)}) custom-call(f32[16,128,128]{2,1,0:T(8,128)} %bank_ref.1), custom_call_target="tpu_custom_call" | custom-call | tf_op jit(solution)/shard_map/bank/pallas_call | solution.py:365
  52.2 1.2 dynamic-slice_bitcast_fusion.fac_ref
  53.4 17.8 %all-to-all-done.1 = f32[512,2,128]{2,1,0:T(2,128)S(1)} async-done(((f32[512,2,128]{2,1,0:T(2,128)}), f32[512,2,128]{2,1,0:T(2,128)S(1)}, u32[]{:S(2)}, u32[]{:S(2)}) %all-to-all-start.1) | async-done | bytes 524320 | tf_op jit(solution)/shard_map/all_to_all | solution.py:450
  71.2 14.3 %solve.1 = f32[256,128]{1,0:T(8,128)} custom-call(f32[4]{0:T(128)} %dynamic-slice_bitcast_fusion.fac_ref, s32[1]{0:T(128)} %bitcast.1.own_ref, f32[1024,128]{1,0:T(8,128)S(1)} %bitcast.48, bf16[16,128,128]{2,1,0:T(8,128)(2,1)} %get-tuple-element.12.w1_hbm.w1, bf16[16,128,128]{2,1,0:T(8,128)(2,1)} %get-tuple-element.13.w2_hbm.w2, ...), custom_call_target="tpu_custom_call" | custom-call | tf_op jit(solution)/shard_map/solve/pallas_call | solution.py:353
  85.6 0.0 copy-start
  85.6 7.3 %all-to-all-start.2 = ((f32[128,2,128]{2,1,0:T(2,128)}), f32[128,2,128]{2,1,0:T(2,128)S(1)}, u32[]{:S(2)}, u32[]{:S(2)}) async-start(f32[128,2,128]{2,1,0:T(2,128)} %bitcast.58), calls=%async_computation.2 | async-start | bytes 262144 | tf_op jit(solution)/shard_map/all_to_all | solution.py:461
  92.9 0.9 constant_dynamic-slice_fusion
  93.7 14.5 %all-to-all-done.2 = f32[128,2,128]{2,1,0:T(2,128)S(1)} async-done(((f32[128,2,128]{2,1,0:T(2,128)}), f32[128,2,128]{2,1,0:T(2,128)S(1)}, u32[]{:S(2)}, u32[]{:S(2)}) %all-to-all-start.2) | async-done | bytes 131104 | tf_op jit(solution)/shard_map/all_to_all | solution.py:461
  108.2 0.2 fusion.3
  108.5 0.0 copy-start.2
  108.5 12.0 %all_to_all.20 = f32[32,2,128]{2,1,0:T(2,128)S(1)} all-to-all(f32[32,2,128]{2,1,0:T(2,128)S(1)} %bitcast.62), channel_id=1, replica_groups=mesh['high'=32,'low'=4,'coord'=4] {'high'}, dimensions={0} | all-to-all | bytes 65536 | tf_op jit(solution)/shard_map/all_to_all | solution.py:477
  120.4 0.0 copy-done.1
  120.4 0.0 copy-done
  120.5 1.6 %finish.1 = (f32[64,128]{1,0:T(8,128)}, f32[8,128]{1,0:T(8,128)}) custom-call(s32[4,4]{1,0:T(4,128)} %cols_ref.1, s32[4,4]{1,0:T(4,128)} %tiles_ref.1, f32[64,128]{1,0:T(8,128)S(1)} %bitcast.50, f32[8,128]{1,0:T(8,128)S(1)} %bitcast.53, f32[4,128]{1,0:T(4,128)S(1)} %bitcast.55, f32[64,128]{1,0:T(8,128)S(1)} %bitcast.51, bf16[16,128,128]{2,1,0:T(8,128)(2,1)S(1)} %copy-done, ...), custom_call_target="tpu_custom_call" | custom-call | tf_op jit(solution)/shard_map/finish/pallas_call | solution.py:395
  (11 shorter events, 0.0 us)
Async XLA Ops:
  0.6 37.8 %copy-start.5 = (f32[256,256]{1,0:T(8,128)S(1)}, f32[256,256]{1,0:T(8,128)}, u32[]{:S(2)}) copy-start(f32[256,256]{1,0:T(8,128)} %constant.43.clone) | copy-start | bytes 786436
  2.2 36.2 %all-to-all-start = ((f32[128,2,128]{2,1,0:T(2,128)}), f32[128,2,128]{2,1,0:T(2,128)S(1)}, u32[]{:S(2)}, u32[]{:S(2)}) async-start(f32[128,2,128]{2,1,0:T(2,128)} %gather.1), calls=%async_computation | async-start | bytes 262144 | tf_op jit(solution)/shard_map/all_to_all | solution.py:428
  38.5 0.7 copy-start.6
  40.1 31.1 %all-to-all-start.1 = ((f32[512,2,128]{2,1,0:T(2,128)}), f32[512,2,128]{2,1,0:T(2,128)S(1)}, u32[]{:S(2)}, u32[]{:S(2)}) async-start(f32[512,2,128]{2,1,0:T(2,128)} %bitcast.17), calls=%async_computation.1 | async-start | bytes 1048576 | tf_op jit(solution)/shard_map/all_to_all | solution.py:450
  71.2 49.2 %copy-start.1 = (bf16[16,128,128]{2,1,0:T(8,128)(2,1)S(1)}, bf16[16,128,128]{2,1,0:T(8,128)(2,1)}, u32[]{:S(2)}) copy-start(bf16[16,128,128]{2,1,0:T(8,128)(2,1)} %get-tuple-element.13.w2_hbm.w2) | copy-start | bytes 1572868
  85.6 34.9 %copy-start = (bf16[16,128,128]{2,1,0:T(8,128)(2,1)S(1)}, bf16[16,128,128]{2,1,0:T(8,128)(2,1)}, u32[]{:S(2)}) copy-start(bf16[16,128,128]{2,1,0:T(8,128)(2,1)} %get-tuple-element.12.w1_hbm.w1) | copy-start | bytes 1572868
  85.6 22.6 %all-to-all-start.2 = ((f32[128,2,128]{2,1,0:T(2,128)}), f32[128,2,128]{2,1,0:T(2,128)S(1)}, u32[]{:S(2)}, u32[]{:S(2)}) async-start(f32[128,2,128]{2,1,0:T(2,128)} %bitcast.58), calls=%async_computation.2 | async-start | bytes 262144 | tf_op jit(solution)/shard_map/all_to_all | solution.py:461
  108.2 12.2 %copy-start.3 = (f32[2,512]{1,0:T(2,128)S(1)}, f32[2,512]{1,0:T(2,128)}, u32[]{:S(2)}) copy-start(f32[2,512]{1,0:T(2,128)} %param.16) | copy-start | bytes 12292
  108.2 12.2 %copy-start.4 = (f32[512]{0:T(512)S(1)}, f32[512]{0:T(512)}, u32[]{:S(2)}) copy-start(f32[512]{0:T(512)} %param.21) | copy-start | bytes 6148
  108.5 12.0 %copy-start.2 = (f32[2,4096]{1,0:T(2,128)S(1)}, f32[2,4096]{1,0:T(2,128)}, u32[]{:S(2)}) copy-start(f32[2,4096]{1,0:T(2,128)} %param.15) | copy-start | bytes 98308
